TPU v7x, 256 devices: a whole 4x4x8 slice. The times are simulated.
256 devices in a mesh: seq: 64 (over z, y, x_hi), mdl: 4 (over x_lo, core).
Axes of the slice: x: 4 (x_hi: 2, x_lo: 2; x = x_hi * 2 + x_lo), y: 4, z: 8, core: 2. Of those that a mesh axis runs over, the one named last changes fastest.
Arguments:
- tokens: bfloat16 [16384, 2048], P('seq', 'mdl'), may hold values from -6 to 6
- norm_gain: bfloat16 [2048], P('mdl'), may hold values from 0.099609375 to 1.8984375
- w_query: bfloat16 [2048, 2048], P('seq', 'mdl'), may hold values from -0.125 to 0.125
- key_matrix: bfloat16 [2048, 1024], P('seq', 'mdl'), may hold values from -0.125 to 0.125
- value_matrix: bfloat16 [2048, 1024], P('seq', 'mdl'), may hold values from -0.125 to 0.125
- w_gate: bfloat16 [2048, 2048], P('seq', 'mdl'), may hold values from -0.125 to 0.125
- q_gain: float32 [128], replicated, may hold values from 0.6 to 8
- k_gain: float32 [128], replicated, may hold values from 0.6 to 8
- w_out: bfloat16 [2048, 2048], P('mdl', 'seq'), may hold values from -0.125 to 0.125
- prompt_lengths: int32 [64], replicated, may hold values from 1 to 512, as said below
- segment_ids: int32 [16384], P('seq'), may hold values from 0 to 63, as said below
- tenant_ranges: int32 [4, 2], replicated, may hold values from 0 to 64, as said below
- key_mask: int32 [16384], P('seq'), may hold values 0 or 1
- cache_slot: int32 [64], replicated, may hold values from 0 to 63, each once
Outputs:
- layer_out: bfloat16 [16384, 2048], P('seq', 'mdl')
- cache_keys: bfloat16 [64, 512, 1024], P('seq', None, 'mdl')
- cache_values: bfloat16 [64, 512, 1024], P('seq', None, 'mdl')
Inputs may be any that keep to these rules, and one draw needn't show every extreme that they name: `prompt_lengths`: the lengths sum to 16384 and one of them equals 512. `segment_ids`: request r holds the prompt_lengths[r] consecutive tokens that follow those of requests 0 to r - 1. `tenant_ranges`: each row (lo, hi) has lo < hi; the rows increase and do not intersect; the first lo is 0 and the last hi is 64; request lo of a tenant is its shared prompt. `cache_slot`: each slot belongs to one request.
All inputs are finite; a program needn't handle non-finite values. No bound on the sum of `key_mask` on one device may be relied on, other than what follows from the above.
Results may differ from a plain program's by a relative error of at most 0.012.
The roundings to bfloat16 on the way count: a program that leaves them out, or rounds other values in their place, can miss the bound.
Values may be sent and summed in bfloat16 or wider, within the bound.
A program may use at most 128 MiB of HBM per device.

v0:
```python
import math

import jax
import jax.numpy as jnp
from jax import lax
from jax.sharding import PartitionSpec as P

HEAD_SIZE = 128
LMAX = 512


epsilon = 1e-06
rope_base = 1000000.0
masked_score = -1e30


def head_norm(values, gain_vector):
    return (
        values
        * lax.rsqrt(jnp.mean(values * values, axis=-1, keepdims=True) + epsilon)
        * gain_vector
    )


def rotate(values, position):
    half_width = values.shape[-1] // 2
    frequency = rope_base ** (-2.0 * jnp.arange(half_width, dtype=jnp.float32) / values.shape[-1])
    angles = position.astype(jnp.float32)[:, None] * frequency[None, :]
    cosine = jnp.cos(angles)[:, None, :]
    sine_part = jnp.sin(angles)[:, None, :]
    former = values[..., :half_width]
    latter = values[..., half_width:]
    return jnp.concatenate(
        [former * cosine - latter * sine_part, latter * cosine + former * sine_part], axis=-1
    )


def token_tables(lengths, segments, ranges):
    request_count = lengths.shape[0]
    starts = jnp.cumsum(lengths) - lengths
    requests = jnp.arange(request_count, dtype=jnp.int32)
    member = (requests[:, None] > ranges[None, :, 0]) & (requests[:, None] < ranges[None, :, 1])
    shared_of = jnp.sum(jnp.where(member, ranges[None, :, 0] + 3, 0), axis=1) - 3
    onehot = segments[:, None] == requests[None, :]
    seg_start = jnp.sum(jnp.where(onehot, starts[None, :], 0), axis=1)
    shared_req = jnp.sum(jnp.where(onehot, shared_of[None, :], 0), axis=1)
    return (starts, seg_start, shared_req)


def body(
    tokens,
    norm_gain,
    w_query,
    key_matrix,
    value_matrix,
    w_gate,
    q_gain,
    k_gain,
    w_out,
    prompt_lengths,
    segment_ids,
    tenant_ranges,
    key_mask,
    cache_slot,
):
    local_rows = tokens.shape[0]
    wide_tokens = tokens.astype(jnp.float32)
    full_width = tokens.shape[1] * lax.axis_size("mdl")
    square_total = lax.psum(jnp.sum(wide_tokens * wide_tokens, axis=1), "mdl")
    scaled = (
        wide_tokens
        * lax.rsqrt(square_total / full_width + epsilon)[:, None]
        * norm_gain.astype(jnp.float32)
    )
    normalized_input = lax.all_gather(scaled.astype(jnp.bfloat16), "mdl", axis=1, tiled=True)
    pieces = (
        lax.all_gather(w_query, "seq", axis=0, tiled=True),
        lax.all_gather(key_matrix, "seq", axis=0, tiled=True),
        lax.all_gather(value_matrix, "seq", axis=0, tiled=True),
        lax.all_gather(w_gate, "seq", axis=0, tiled=True),
    )
    columns = normalized_input
    query_rows, unprojected_keys, values_raw, gate_logits = tuple(
        (
            jnp.dot(columns, weight_part, preferred_element_type=jnp.float32)
            for weight_part in pieces
        )
    )
    device_seq = lax.axis_index("seq")
    token_ids = device_seq * local_rows + jnp.arange(local_rows, dtype=jnp.int32)
    starts, seg_start, shared_req = token_tables(prompt_lengths, segment_ids, tenant_ranges)
    position = token_ids - seg_start
    query_heads = query_rows.shape[1] // HEAD_SIZE
    kv_heads = unprojected_keys.shape[1] // HEAD_SIZE
    query_group_width = query_heads // kv_heads
    query_rows = (
        rotate(head_norm(query_rows.reshape(local_rows, query_heads, HEAD_SIZE), q_gain), position)
        .astype(jnp.bfloat16)
        .reshape(local_rows, kv_heads, query_group_width, HEAD_SIZE)
    )
    flat_keys = (
        rotate(
            head_norm(unprojected_keys.reshape(local_rows, kv_heads, HEAD_SIZE), k_gain), position
        )
        .astype(jnp.bfloat16)
        .reshape(local_rows, kv_heads * HEAD_SIZE)
    )
    values_flat = values_raw.astype(jnp.bfloat16)
    key_tags = jnp.where(key_mask == 1, segment_ids, -2).astype(jnp.bfloat16)
    row_segs = segment_ids.astype(jnp.float32)
    row_shared = shared_req.astype(jnp.float32)
    request_ids = jnp.arange(prompt_lengths.shape[0], dtype=jnp.int32)
    my_request = jnp.sum(jnp.where(cache_slot == device_seq, request_ids, 0))
    my_start = jnp.sum(jnp.where(request_ids == my_request, starts, 0))
    my_length = jnp.sum(jnp.where(request_ids == my_request, prompt_lengths, 0))
    offsets = jnp.arange(LMAX, dtype=jnp.int32)
    scale_factor = HEAD_SIZE ** (-0.5)

    def visible_of(tags_part, columns):
        own = tags_part[None, :] == row_segs[:, None]
        other = tags_part[None, :] == row_shared[:, None]
        earlier = columns[None, :] <= token_ids[:, None]
        diagonal = columns[None, :] == token_ids[:, None]
        return diagonal | earlier & (own | other)

    head_shape = (local_rows, kv_heads, query_group_width)
    soft_start = (
        jnp.full(head_shape, masked_score, jnp.float32),
        jnp.zeros(head_shape, jnp.float32),
        jnp.zeros(head_shape + (HEAD_SIZE,), jnp.float32),
    )
    empty_cache = jnp.zeros((LMAX, kv_heads * HEAD_SIZE), jnp.bfloat16)
    start_state = soft_start + (empty_cache, empty_cache)
    top_now, totals_now, summed_now, cache_k, cache_v = start_state
    piece_keys = lax.all_gather(flat_keys, "seq", axis=0, tiled=True)
    piece_values = lax.all_gather(values_flat, "seq", axis=0, tiled=True)
    piece_tags = lax.all_gather(key_tags, "seq", axis=0, tiled=True)
    piece_columns = jnp.arange(piece_keys.shape[0], dtype=jnp.int32)
    piece_rows = piece_keys.shape[0]
    block_keys = math.gcd(piece_rows, 1024)

    def key_block(block_index, loop_state):
        block_offset = block_index * block_keys
        keys_part = lax.dynamic_slice_in_dim(piece_keys, block_offset, block_keys, 0).reshape(
            block_keys, kv_heads, HEAD_SIZE
        )
        values_part = lax.dynamic_slice_in_dim(piece_values, block_offset, block_keys, 0).reshape(
            block_keys, kv_heads, HEAD_SIZE
        )
        tags_part = lax.dynamic_slice_in_dim(piece_tags, block_offset, block_keys, 0).astype(
            jnp.float32
        )
        columns = lax.dynamic_slice_in_dim(piece_columns, block_offset, block_keys, 0)
        visible = visible_of(tags_part, columns)
        old_top, old_totals, old_summed = loop_state
        allowed = visible[:, None, None, :]
        scores = (
            jnp.einsum("qhgd,khd->qhgk", query_rows, keys_part, preferred_element_type=jnp.float32)
            * scale_factor
        )
        scores = jnp.where(allowed, scores, masked_score)
        new_top = jnp.maximum(old_top, jnp.max(scores, axis=-1))
        factor = jnp.exp(old_top - new_top)
        raw_weights = jnp.where(allowed, jnp.exp(scores - new_top[..., None]), 0.0)
        new_totals = old_totals * factor + jnp.sum(raw_weights, axis=-1)
        new_summed = old_summed * factor[..., None] + jnp.einsum(
            "qhgk,khd->qhgd",
            raw_weights.astype(jnp.bfloat16),
            values_part,
            preferred_element_type=jnp.float32,
        )
        return (new_top, new_totals, new_summed)

    top_now, totals_now, summed_now = lax.fori_loop(
        0, piece_rows // block_keys, key_block, (top_now, totals_now, summed_now)
    )
    copy_cache_k = cache_k
    copy_cache_v = cache_v
    piece_rows = piece_keys.shape[0]
    wanted = my_start + offsets
    in_window = ((wanted >= 0) & (wanted < piece_rows) & (offsets < my_length))[:, None]
    source = jnp.clip(wanted, 0, piece_rows - 1)
    copy_cache_k = jnp.where(in_window, jnp.take(piece_keys, source, axis=0), copy_cache_k)
    copy_cache_v = jnp.where(in_window, jnp.take(piece_values, source, axis=0), copy_cache_v)
    cache_k = copy_cache_k
    cache_v = copy_cache_v
    top_score, totals, summed, cache_k, cache_v = (
        top_now,
        totals_now,
        summed_now,
        cache_k,
        cache_v,
    )
    attended = (summed / totals[..., None]).reshape(local_rows, query_heads * HEAD_SIZE)
    gated_heads = (attended * jax.nn.sigmoid(gate_logits)).astype(jnp.bfloat16)
    partial_out = jnp.dot(
        gated_heads,
        lax.all_gather(w_out, "seq", axis=1, tiled=True),
        preferred_element_type=jnp.float32,
    )
    branch_sum = lax.psum_scatter(
        partial_out.astype(jnp.bfloat16), "mdl", scatter_dimension=1, tiled=True
    ).astype(jnp.float32)
    layer_out = (wide_tokens + branch_sum).astype(jnp.bfloat16)
    return (layer_out, cache_k[None], cache_v[None])


def solution(mesh):
    placed = (
        P("seq", "mdl"),
        P("mdl"),
        P("seq", "mdl"),
        P("seq", "mdl"),
        P("seq", "mdl"),
        P("seq", "mdl"),
        P(),
        P(),
        P("mdl", "seq"),
        P(),
        P("seq"),
        P(),
        P("seq"),
        P(),
    )
    return jax.shard_map(
        body,
        mesh=mesh,
        in_specs=placed,
        out_specs=(P("seq", "mdl"), P("seq", None, "mdl"), P("seq", None, "mdl")),
        check_vma=False,
    )
```

profile of v0, /device:TPU:72, one launch (start us, length us, event | category | flops | bytes accessed | tf_op | source)
XLA Modules:
  0.0 969.0 jit_solution(3324895451097505820)
XLA Ops:
  8.3 6.9 psum.7
  27.1 15.9 %all-gather.10.cloned.1.call-done = bf16[256,2048]{1,0:T(8,128)(2,1)} async-done(((bf16[256,512]{1,0:T(8,128)(2,1)}), bf16[256,2048]{1,0:T(8,128)(2,1)}) %all-gather.10.cloned.1.call-update) | async-done | bytes 1048592 | tf_op jit(solution)/shard_map/all_gather | solution.py:75
  43.0 118.3 %all-gather.12.cloned.1.call-done = bf16[2048,256]{1,0:T(8,128)(2,1)} async-done(((bf16[32,256]{1,0:T(8,128)(2,1)}), bf16[2048,256]{1,0:T(8,128)(2,1)}) %all-gather.12.cloned.1.call-update) | async-done | bytes 1048592 | tf_op jit(solution)/shard_map/all_gather | solution.py:78
  164.4 111.6 %all-gather.18.cloned.1.call-done = bf16[2048,256]{1,0:T(8,128)(2,1)} async-done(((bf16[32,256]{1,0:T(8,128)(2,1)}), bf16[2048,256]{1,0:T(8,128)(2,1)}) %all-gather.18.cloned.1.call-update) | async-done | bytes 1048592 | tf_op jit(solution)/shard_map/all_gather | solution.py:79
  280.2 154.5 %all-gather = bf16[64,1,256]{2,1,0:T(2,128)(2,1)S(1)} all-gather(bf16[1,1,256]{2,1,0:T(2,128)(2,1)S(1)} %reshape.287), channel_id=1, replica_groups=mesh['seq'=64,'mdl'=4] {'seq'}, dimensions={0}, use_global_device_ids=true | all-gather | bytes 33280 | tf_op jit(solution)/shard_map/all_gather | solution.py:137
  439.0 107.1 %all-gather.14.cloned.1.call-done = bf16[16384,256]{1,0:T(8,128)(2,1)} async-done(((bf16[256,256]{1,0:T(8,128)(2,1)}), bf16[16384,256]{1,0:T(8,128)(2,1)}) %all-gather.14.cloned.1.call-update) | async-done | bytes 8388624 | tf_op jit(solution)/shard_map/all_gather | solution.py:135
  546.1 151.5 %all-gather.20.cloned.1.call-done = bf16[16384,256]{1,0:T(8,128)(2,1)} async-done(((bf16[256,256]{1,0:T(8,128)(2,1)}), bf16[16384,256]{1,0:T(8,128)(2,1)}) %all-gather.20.cloned.1.call-update) | async-done | bytes 8388624 | tf_op jit(solution)/shard_map/all_gather | solution.py:136
  697.6 202.7 %while.18 = (s32[]{:T(128)}, f32[256,2,2]{0,2,1:T(2,128)S(1)}, f32[256,2,2]{0,2,1:T(2,128)S(1)}, f32[256,2,2,128]{0,3,2,1:T(8,128)}, s32[16384]{0:T(1024)S(1)}, ...) while((s32[]{:T(128)}, f32[256,2,2]{0,2,1:T(2,128)S(1)}, ...), condition=%wide.region_11.12_spmd.clone, body=%wide.region_8.11_spmd.clone.sunk | while | flops 552737024 | bytes 24471832 | solution.py:174
  731.3 3.5 fusion.72
  744.0 3.5 fusion.72
  756.6 3.5 fusion.72
  769.3 3.5 fusion.72
  782.0 3.5 fusion.72
  794.6 3.5 fusion.72
  807.3 3.5 fusion.72
  845.4 3.5 fusion.72
  858.0 3.5 fusion.72
  883.3 3.5 fusion.72
  896.0 3.5 fusion.72
  901.7 33.5 %all-gather.24.cloned.1.call-done = bf16[512,2048]{0,1:T(8,128)(2,1)} async-done(((bf16[512,32]{0,1:T(8,128)(2,1)}), bf16[512,2048]{0,1:T(8,128)(2,1)}) %all-gather.24.cloned.1.call-update) | async-done | bytes 2097168 | tf_op jit(solution)/shard_map/all_gather | solution.py:198
  935.2 4.6 convolution_convert_fusion
  941.6 6.0 gather_fusion
  947.6 6.2 gather_fusion.1
  954.9 5.9 reduce-scatter.2.cloned.1.call-done
  (344 shorter events, 193.3 us)
Async XLA Ops:
  7.2 156.2 %copy-start.6 = (f32[128]{0:T(128)S(1)}, f32[128]{0:T(128)}, u32[]{:S(2)}) copy-start(f32[128]{0:T(128)} %param.25) | copy-start | bytes 1540
  7.2 273.0 %copy-start.4 = (s32[256]{0:T(256)S(1)}, s32[256]{0:T(256)}, u32[]{:S(2)}) copy-start(s32[256]{0:T(256)} %param.28) | copy-start | bytes 3076
  7.2 273.0 %copy-start.5 = (s32[256]{0:T(256)S(1)}, s32[256]{0:T(256)}, u32[]{:S(2)}) copy-start(s32[256]{0:T(256)} %param.30) | copy-start | bytes 3076
  7.2 35.8 %all-gather.10.cloned.1.call-start = ((), (), s32[]{:S(2)}) async-start(), calls=%async_computation.1 | async-start | bytes 1310720 | tf_op jit(solution)/shard_map/all_gather | solution.py:75
  17.7 143.5 %all-gather.12.cloned.1.call-start = ((), (), s32[]{:S(2)}) async-start(), calls=%async_computation.2 | async-start | bytes 1064960 | tf_op jit(solution)/shard_map/all_gather | solution.py:78
  18.5 257.5 %all-gather.18.cloned.1.call-start = ((), (), s32[]{:S(2)}) async-start(), calls=%async_computation.5 | async-start | bytes 1064960 | tf_op jit(solution)/shard_map/all_gather | solution.py:79
  19.2 415.8 %all-gather.16.cloned.1.call-start = ((), (), s32[]{:S(2)}) async-start(), calls=%async_computation.4 | async-start | bytes 2129920 | tf_op jit(solution)/shard_map/all_gather | solution.py:77
  19.8 526.3 %all-gather.14.cloned.1.call-start = ((), (), s32[]{:S(2)}) async-start(), calls=%async_computation.3 | async-start | bytes 8519680 | tf_op jit(solution)/shard_map/all_gather | solution.py:135
  43.0 392.1 %copy-start = (bf16[256,2048]{1,0:T(8,128)(2,1)S(1)}, bf16[256,2048]{1,0:T(8,128)(2,1)}, u32[]{:S(2)}) copy-start(bf16[256,2048]{1,0:T(8,128)(2,1)} %all-gather.10.cloned.1.call-done) | copy-start | bytes 3145732
  164.3 273.6 %copy-start.7 = (f32[128]{0:T(128)S(1)}, f32[128]{0:T(128)}, u32[]{:S(2)}) copy-start(f32[128]{0:T(128)} %param.24) | copy-start | bytes 1540
  164.3 533.3 %all-gather.20.cloned.1.call-start = ((), (), s32[]{:S(2)}) async-start(), calls=%async_computation.6 | async-start | bytes 8519680 | tf_op jit(solution)/shard_map/all_gather | solution.py:136
  278.6 623.1 %all-gather.22.cloned.1.call-start = ((), (), s32[]{:S(2)}) async-start(), calls=%async_computation.7 | async-start | bytes 2129920 | tf_op jit(solution)/shard_map/all_gather | solution.py:80
  279.3 655.9 %all-gather.24.cloned.1.call-start = ((), (), s32[]{:S(2)}) async-start(), calls=%async_computation.8 | async-start | bytes 2129920 | tf_op jit(solution)/shard_map/all_gather | solution.py:198
  280.1 680.7 %reduce-scatter.2.cloned.1.call-start = ((), (), s32[]{:S(2)}) async-start(), calls=%async_computation.9 | async-start | bytes 1310720 | tf_op jit(solution)/shard_map/reduce_scatter | solution.py:201
  712.3 6.3 copy-start.2
  725.0 6.3 copy-start.2
  750.3 6.3 copy-start.2
  763.0 6.3 copy-start.2
  788.3 6.3 copy-start.2
  801.0 6.3 copy-start.2
  813.7 6.3 copy-start.2
  826.3 6.4 copy-start.2
  877.0 6.3 copy-start.2
  939.8 20.9 %copy-start.1 = (bf16[256,512]{1,0:T(8,128)(2,1)S(1)}, bf16[256,512]{1,0:T(8,128)(2,1)}, u32[]{:S(2)}) copy-start(bf16[256,512]{1,0:T(8,128)(2,1)} %param.18) | copy-start | bytes 786436
  (23 other events, 58.0 us)
Sparse Core Ops, SparseCore 0:
  17.8 25.0 all-gather.9
  46.6 114.6 all-gather.11
  164.9 111.0 all-gather.17
  279.4 114.6 all-gather.15
  398.0 148.0 all-gather.13
  550.0 147.5 all-gather.19
  701.2 114.9 all-gather.21
  819.8 115.3 all-gather.23
  940.0 20.7 reduce-scatter.1
where the time goes:
time: 973 us; the launch traced here: 969 us
  waiting for transfers between devices  547 us (56%)
  blocking collectives  161 us (17%)
  matrix products  113 us (12%)
  other arithmetic  76.1 us (8%)
  local copies, waits for them, and re-layouts  55.7 us (6%)
  between operations  14.2 us (1%)
    all_gather x1, blocking collectives, body(): piece_tags = lax.all_gather(key_tags, 'seq', axis=0, tiled=True)  155 us
    all_gather x1, waiting for transfers between devices, body(): piece_values = lax.all_gather(values_flat, 'seq', axis=0, tiled=True)  152 us
    all_gather x1, waiting for transfers between devices, body(): lax.all_gather(key_matrix, 'seq', axis=0, tiled=True)  118 us
    all_gather x1, waiting for transfers between devices, body(): lax.all_gather(value_matrix, 'seq', axis=0, tiled=True)  112 us
    all_gather x1, waiting for transfers between devices, body(): piece_keys = lax.all_gather(flat_keys, 'seq', axis=0, tiled=True)  107 us
    dot_general x16, matrix products, key_block(): jnp.einsum('qhgk,khd->qhgd', raw_weights.astype(jnp.bfloat16), values_par...  55.6 us
    reduce_sum x16, other arithmetic, key_block(): new_totals = old_totals * factor + jnp.sum(raw_weights, axis=-1)  51.6 us
    dot_general x16, matrix products, key_block(): jnp.einsum('qhgd,khd->qhgk', query_rows, keys_part, preferred_element_typ...  45.6 us
  transfers between devices with their start and end apart: 9, of which 7 were waited for; matrix products, arithmetic and copies ran while one was open for 23% of the time, Pallas kernels for 0%

commit v1 on v0

v1 whole, which is shorter than its diff:
```python
import jax
import jax.numpy as jnp
from jax import lax
from jax.sharding import PartitionSpec as P

HEAD_SIZE = 128
LMAX = 512
KEY_BLOCK = 256


epsilon = 1e-06
rope_base = 1000000.0
masked_score = -1e30


def head_norm(values, gain_vector):
    return (
        values
        * lax.rsqrt(jnp.mean(values * values, axis=-1, keepdims=True) + epsilon)
        * gain_vector
    )


def rotate(values, position):
    half_width = values.shape[-1] // 2
    frequency = rope_base ** (-2.0 * jnp.arange(half_width, dtype=jnp.float32) / values.shape[-1])
    angles = position.astype(jnp.float32)[:, None] * frequency[None, :]
    cosine = jnp.cos(angles)[:, None, :]
    sine_part = jnp.sin(angles)[:, None, :]
    former = values[..., :half_width]
    latter = values[..., half_width:]
    return jnp.concatenate(
        [former * cosine - latter * sine_part, latter * cosine + former * sine_part], axis=-1
    )


def body(
    tokens,
    norm_gain,
    w_query,
    key_matrix,
    value_matrix,
    w_gate,
    q_gain,
    k_gain,
    w_out,
    prompt_lengths,
    segment_ids,
    tenant_ranges,
    key_mask,
    cache_slot,
):
    local_rows = tokens.shape[0]
    weight_rows = w_query.shape[0]
    q_cols = w_query.shape[1]
    kv_cols = key_matrix.shape[1]
    g_cols = w_gate.shape[1]
    seq_size = lax.axis_size("seq")
    stream = local_rows * seq_size
    request_count = prompt_lengths.shape[0]

    mask_cols = local_rows // weight_rows
    mask_block = key_mask.astype(jnp.bfloat16).reshape(weight_rows, mask_cols)
    mask_block = jnp.pad(mask_block, ((0, 0), (0, 128 - mask_cols)))
    packed = jnp.concatenate(
        [w_query, key_matrix, value_matrix, w_gate, w_out.T, mask_block], axis=1
    )
    gathered = lax.all_gather(packed, "seq", axis=0, tiled=True)
    proj_cols = q_cols + 2 * kv_cols + g_cols
    w_proj = gathered[:, :proj_cols]
    w_out_t = gathered[:, proj_cols : proj_cols + w_out.shape[0]]
    all_mask = gathered[:, proj_cols + w_out.shape[0] : proj_cols + w_out.shape[0] + mask_cols]
    all_mask = all_mask.reshape(stream)

    wide_tokens = tokens.astype(jnp.float32)
    full_width = tokens.shape[1] * lax.axis_size("mdl")
    square_total = lax.psum(jnp.sum(wide_tokens * wide_tokens, axis=1), "mdl")
    scaled = (
        wide_tokens
        * lax.rsqrt(square_total / full_width + epsilon)[:, None]
        * norm_gain.astype(jnp.float32)
    )
    normalized_input = lax.all_gather(scaled.astype(jnp.bfloat16), "mdl", axis=1, tiled=True)
    projected = jnp.dot(normalized_input, w_proj, preferred_element_type=jnp.float32)
    query_rows = projected[:, :q_cols]
    unprojected_keys = projected[:, q_cols : q_cols + kv_cols]
    values_raw = projected[:, q_cols + kv_cols : q_cols + 2 * kv_cols]
    gate_logits = projected[:, q_cols + 2 * kv_cols :]

    device_seq = lax.axis_index("seq")
    token_ids = device_seq * local_rows + jnp.arange(local_rows, dtype=jnp.int32)
    starts = jnp.cumsum(prompt_lengths) - prompt_lengths
    ends = starts + prompt_lengths
    requests = jnp.arange(request_count, dtype=jnp.int32)
    member = (requests[:, None] > tenant_ranges[None, :, 0]) & (
        requests[:, None] < tenant_ranges[None, :, 1]
    )
    shared_of = jnp.sum(jnp.where(member, tenant_ranges[None, :, 0] + 3, 0), axis=1) - 3
    onehot = segment_ids[:, None] == requests[None, :]
    seg_start = jnp.sum(jnp.where(onehot, starts[None, :], 0), axis=1)
    shared_req = jnp.sum(jnp.where(onehot, shared_of[None, :], 0), axis=1)
    position = token_ids - seg_start

    query_heads = q_cols // HEAD_SIZE
    kv_heads = kv_cols // HEAD_SIZE
    group = query_heads // kv_heads
    q_rot = (
        rotate(head_norm(query_rows.reshape(local_rows, query_heads, HEAD_SIZE), q_gain), position)
        .astype(jnp.bfloat16)
        .reshape(local_rows, kv_heads, group, HEAD_SIZE)
    )
    k_rot = (
        rotate(head_norm(unprojected_keys.reshape(local_rows, kv_heads, HEAD_SIZE), k_gain), position)
        .astype(jnp.bfloat16)
        .reshape(local_rows, kv_cols)
    )
    values_flat = values_raw.astype(jnp.bfloat16)
    kv_local = jnp.concatenate([k_rot, values_flat], axis=1)
    kv_all = lax.all_gather(kv_local, "seq", axis=0, tiled=True)

    n_blocks = stream // KEY_BLOCK
    block_ids = jnp.arange(n_blocks, dtype=jnp.int32)
    last_block = (device_seq * local_rows + local_rows - 1) // KEY_BLOCK
    first_block = jnp.min(seg_start) // KEY_BLOCK
    needed = (block_ids >= first_block) & (block_ids <= last_block)
    lo = tenant_ranges[:, 0]
    hi = tenant_ranges[:, 1]
    used = jnp.any(
        (segment_ids[:, None] > lo[None, :]) & (segment_ids[:, None] < hi[None, :]), axis=0
    )
    lo_start = jnp.sum(jnp.where(requests[None, :] == lo[:, None], starts[None, :], 0), axis=1)
    lo_end = jnp.sum(jnp.where(requests[None, :] == lo[:, None], ends[None, :], 0), axis=1)
    in_prompt = (
        used[:, None]
        & (block_ids[None, :] >= (lo_start // KEY_BLOCK)[:, None])
        & (block_ids[None, :] <= ((lo_end - 1) // KEY_BLOCK)[:, None])
    )
    needed = needed | jnp.any(in_prompt, axis=0)
    n_needed = jnp.sum(needed.astype(jnp.int32))
    (block_list,) = jnp.nonzero(needed, size=n_blocks, fill_value=0)
    block_list = block_list.astype(jnp.int32)

    row_segs = segment_ids
    row_shared = shared_req
    scale_factor = HEAD_SIZE ** (-0.5)
    head_shape = (local_rows, kv_heads, group)

    def key_block(i, loop_state):
        old_top, old_totals, old_summed = loop_state
        block = block_list[i]
        offset = block * KEY_BLOCK
        kv_part = lax.dynamic_slice_in_dim(kv_all, offset, KEY_BLOCK, 0)
        keys_part = kv_part[:, :kv_cols].reshape(KEY_BLOCK, kv_heads, HEAD_SIZE)
        values_part = kv_part[:, kv_cols:].reshape(KEY_BLOCK, kv_heads, HEAD_SIZE)
        mask_part = lax.dynamic_slice_in_dim(all_mask, offset, KEY_BLOCK, 0)
        columns = offset + jnp.arange(KEY_BLOCK, dtype=jnp.int32)
        col_segs = jnp.sum((columns[:, None] >= ends[None, :]).astype(jnp.int32), axis=1)
        live = mask_part == 1
        own = col_segs[None, :] == row_segs[:, None]
        other = col_segs[None, :] == row_shared[:, None]
        earlier = columns[None, :] <= token_ids[:, None]
        diagonal = columns[None, :] == token_ids[:, None]
        visible = diagonal | (earlier & live[None, :] & (own | other))
        allowed = visible[:, None, None, :]
        scores = (
            jnp.einsum("qhgd,khd->qhgk", q_rot, keys_part, preferred_element_type=jnp.float32)
            * scale_factor
        )
        scores = jnp.where(allowed, scores, masked_score)
        new_top = jnp.maximum(old_top, jnp.max(scores, axis=-1))
        factor = jnp.exp(old_top - new_top)
        raw_weights = jnp.where(allowed, jnp.exp(scores - new_top[..., None]), 0.0)
        new_totals = old_totals * factor + jnp.sum(raw_weights, axis=-1)
        new_summed = old_summed * factor[..., None] + jnp.einsum(
            "qhgk,khd->qhgd",
            raw_weights.astype(jnp.bfloat16),
            values_part,
            preferred_element_type=jnp.float32,
        )
        return (new_top, new_totals, new_summed)

    start_state = (
        jnp.full(head_shape, masked_score, jnp.float32),
        jnp.zeros(head_shape, jnp.float32),
        jnp.zeros(head_shape + (HEAD_SIZE,), jnp.float32),
    )
    top_now, totals, summed = lax.fori_loop(0, n_needed, key_block, start_state)

    my_request = jnp.sum(jnp.where(cache_slot == device_seq, requests, 0))
    my_start = jnp.sum(jnp.where(requests == my_request, starts, 0))
    my_length = jnp.sum(jnp.where(requests == my_request, prompt_lengths, 0))
    offsets = jnp.arange(LMAX, dtype=jnp.int32)
    wanted = my_start + offsets
    in_window = ((wanted < stream) & (offsets < my_length))[:, None]
    source = jnp.clip(wanted, 0, stream - 1)
    cache_rows = jnp.where(in_window, jnp.take(kv_all, source, axis=0), jnp.zeros((), jnp.bfloat16))
    cache_k = cache_rows[:, :kv_cols]
    cache_v = cache_rows[:, kv_cols:]

    attended = (summed / totals[..., None]).reshape(local_rows, query_heads * HEAD_SIZE)
    gated_heads = (attended * jax.nn.sigmoid(gate_logits)).astype(jnp.bfloat16)
    partial_out = lax.dot_general(
        gated_heads,
        w_out_t,
        (((1,), (1,)), ((), ())),
        preferred_element_type=jnp.float32,
    )
    branch_sum = lax.psum_scatter(
        partial_out.astype(jnp.bfloat16), "mdl", scatter_dimension=1, tiled=True
    ).astype(jnp.float32)
    layer_out = (wide_tokens + branch_sum).astype(jnp.bfloat16)
    return (layer_out, cache_k[None], cache_v[None])


def solution(mesh):
    placed = (
        P("seq", "mdl"),
        P("mdl"),
        P("seq", "mdl"),
        P("seq", "mdl"),
        P("seq", "mdl"),
        P("seq", "mdl"),
        P(),
        P(),
        P("mdl", "seq"),
        P(),
        P("seq"),
        P(),
        P("seq"),
        P(),
    )
    return jax.shard_map(
        body,
        mesh=mesh,
        in_specs=placed,
        out_specs=(P("seq", "mdl"), P("seq", None, "mdl"), P("seq", None, "mdl")),
        check_vma=False,
    )
```

time: 973 us -> 480 us (0.49)
  waiting for transfers between devices: 547 us -> 383 us
  blocking collectives: 161 us -> 6.9 us
  matrix products: 113 us -> 11.7 us
  other arithmetic: 76.1 us -> 23.6 us
  local copies, waits for them, and re-layouts: 55.7 us -> 27.5 us
    all_gather x7 -> x2, waiting for transfers between devices: 522 us -> 354 us  [the longest x1 196 us: body(): kv_all = lax.all_gather(kv_local, 'seq', axis=0, tiled=True)]
    all_gather x1 -> x0, blocking collectives: 155 us -> none  [body(): piece_tags = lax.all_gather(key_tags, 'seq', axis=0, tiled=True)]
    dot_general x16 -> x4, matrix products: 55.6 us -> 1.72 us  [key_block(): jnp.einsum('qhgk,khd->qhgd', raw_weights.astype(jnp.bfloat16), values_par...]
    reduce_sum x16 -> x4, other arithmetic: 51.6 us -> 0.83 us  [key_block(): new_totals = old_totals * factor + jnp.sum(raw_weights, axis=-1)]
    dot_general x20 -> x6, matrix products: 57.3 us -> 9.94 us  [the longest x1 4.9 us: body(): jnp.dot(normalized_input, w_proj, preferred_element_type=jnp.float32)]
    dynamic_slice x64 -> x4, local copies, waits for them, and re-layouts: 27.1 us -> 2.35 us  [key_block(): block = block_list[i]]
    while x80 -> x12, local copies, waits for them, and re-layouts: 13.4 us -> 0.8 us
    reduce_scatter x1, waiting for transfers between devices: 5.91 us -> 17.5 us  [body(): lax.psum_scatter(partial_out.astype(jnp.bfloat16), 'mdl', scatter_dimensi...]
  transfers between devices with their start and end apart: 9 -> 4, of which waited for: 7 -> 4; matrix products, arithmetic and copies ran while one was open for 23% -> 7% of each run, Pallas kernels for 0% -> 0%
where the time goes in v1:
time: 480 us; the launch traced here: 476 us
  waiting for transfers between devices  383 us (80%)
  local copies, waits for them, and re-layouts  27.5 us (6%)
  other arithmetic  23.6 us (5%)
  between operations  16.7 us (3%)
  matrix products  11.7 us (2%)
  blocking collectives  6.9 us (1%)
  loops' own time  6.36 us (1%)
    all_gather x1, waiting for transfers between devices, body(): kv_all = lax.all_gather(kv_local, 'seq', axis=0, tiled=True)  196 us
    all_gather x1, waiting for transfers between devices, body(): gathered = lax.all_gather(packed, 'seq', axis=0, tiled=True)  158 us
    reduce_scatter x1, waiting for transfers between devices, body(): lax.psum_scatter(partial_out.astype(jnp.bfloat16), 'mdl', scatter_dimensi...  17.5 us
    all_gather x1, waiting for transfers between devices, body(): lax.all_gather(scaled.astype(jnp.bfloat16), 'mdl', axis=1, tiled=True)  12.2 us
    gather x1, local copies, waits for them, and re-layouts, body(): jnp.take(kv_all, source, axis=0)  9.91 us
  transfers between devices with their start and end apart: 4, of which 4 were waited for; matrix products, arithmetic and copies ran while one was open for 7% of the time, Pallas kernels for 0%

profile of v1, /device:TPU:72, one launch (start us, length us, event | category | flops | bytes accessed | tf_op | source)
XLA Modules:
  0.0 476.3 jit_solution(16743282391402247093)
XLA Ops:
  7.2 1.1 fusion.15
  8.3 6.9 %psum.7 = f32[256]{0:T(256)S(1)} all-reduce(f32[256]{0:T(256)S(1)} %fusion.15), channel_id=1, replica_groups=mesh['seq'=64,'mdl'=4] {'mdl'}, use_global_device_ids=true, to_apply=%region_12.13 | all-reduce | flops 256 | bytes 2048 | tf_op jit(solution)/shard_map/psum | solution.py:77
  15.9 1.8 fusion.17
  18.5 0.8 constant_dynamic-update-slice_fusion.4
  24.0 1.3 fusion.36
  26.8 2.0 fusion.34
  30.8 12.2 %all-gather.6.cloned.1.call-done = bf16[256,2048]{1,0:T(8,128)(2,1)} async-done(((bf16[256,512]{1,0:T(8,128)(2,1)}), bf16[256,2048]{1,0:T(8,128)(2,1)}) %all-gather.6.cloned.1.call-update) | async-done | bytes 1048592 | tf_op jit(solution)/shard_map/all_gather | solution.py:83
  42.9 157.9 %all-gather.4.cloned.1.call-done = bf16[2048,2176]{1,0:T(8,128)(2,1)} async-done(((bf16[32,2176]{1,0:T(8,128)(2,1)}), bf16[2048,2176]{1,0:T(8,128)(2,1)}) %all-gather.4.cloned.1.call-update) | async-done | bytes 8912912 | tf_op jit(solution)/shard_map/all_gather | solution.py:68
  200.8 4.9 %fusion.12 = f32[256,1536]{1,0:T(8,128)S(1)} fusion(bf16[256,2048]{1,0:T(8,128)(2,1)} %all-gather.6.cloned.1.call-done, bf16[2048,2176]{1,0:T(8,128)(2,1)} %all-gather.4.cloned.1.call-done), kind=kOutput, calls=%fused_computation.23 | convolution fusion | flops 1610612736 | bytes 8912896 | tf_op jit(solution)/shard_map/dot_general | solution.py:84
  205.8 1.1 copy-done.1
  212.9 1.0 scatter_custom_fusion
  215.5 1.1 slice.80
  218.8 195.7 %all-gather.8.cloned.1.call-done = bf16[16384,512]{1,0:T(8,128)(2,1)} async-done(((bf16[256,512]{1,0:T(8,128)(2,1)}), bf16[16384,512]{1,0:T(8,128)(2,1)}) %all-gather.8.cloned.1.call-update) | async-done | bytes 16777232 | tf_op jit(solution)/shard_map/all_gather | solution.py:119
  414.7 19.1 %while.15 = (s32[]{:T(128)}, f32[256,2,2]{0,2,1:T(2,128)S(1)}, f32[256,2,2]{0,2,1:T(2,128)S(1)}, f32[256,2,2,128]{0,3,2,1:T(8,128)S(1)}, s32[]{:T(128)}, /*index...) while((s32[]{:T(128)}, f32[256,2,2]{0,2,1:T(2,128)S(1)}, ...), condition=%wide.region_21.22_spmd.clone, body=%wide.region_17.21_spmd.clone.sunk | while | flops 137415680 | bytes 6105641 | solution.py:187
  416.9 1.0 fusion.60
  421.5 1.0 fusion.60
  426.1 1.0 fusion.60
  430.6 1.0 fusion.60
  434.0 3.5 convolution_convert_fusion
  437.6 1.3 fusion.28
  439.6 9.9 %gather_fusion = bf16[512,512]{1,0:T(8,128)(2,1)S(1)} fusion(bf16[16384,512]{1,0:T(8,128)(2,1)} %get-tuple-element.385, s32[1024]{0:T(1024)S(1)} %pad_clamp_fusion), kind=kCustom, calls=%fused_computation | custom fusion | bytes 1050624 | tf_op jit(solution)/shard_map/jit(_take)/gather | solution.py:196
  449.7 0.8 slice_bitcast_fusion
  450.5 17.5 %reduce-scatter.2.cloned.1.call-done = bf16[256,512]{1,0:T(8,128)(2,1)} async-done(((bf16[256,2048]{1,0:T(8,128)(2,1)}), bf16[256,512]{1,0:T(8,128)(2,1)}) %reduce-scatter.2.cloned.1.call-update) | async-done | bytes 262160 | tf_op jit(solution)/shard_map/reduce_scatter | solution.py:208
  468.0 1.7 fusion.18
  (134 shorter events, 26.7 us)
Async XLA Ops:
  7.2 35.8 %all-gather.6.cloned.1.call-start = ((), (), s32[]{:S(2)}) async-start(), calls=%async_computation.2 | async-start | bytes 1310720 | tf_op jit(solution)/shard_map/all_gather | solution.py:83
  17.7 183.2 %all-gather.4.cloned.1.call-start = ((), (), s32[]{:S(2)}) async-start(), calls=%async_computation.1 | async-start | bytes 9052160 | tf_op jit(solution)/shard_map/all_gather | solution.py:68
  22.3 0.7 copy-start.2
  22.9 391.7 %all-gather.8.cloned.1.call-start = ((), (), s32[]{:S(2)}) async-start(), calls=%async_computation.3 | async-start | bytes 17039360 | tf_op jit(solution)/shard_map/all_gather | solution.py:119
  30.8 176.8 %copy-start.5 = (f32[128]{0:T(128)S(1)}, f32[128]{0:T(128)}, u32[]{:S(2)}) copy-start(f32[128]{0:T(128)} %param.23) | copy-start | bytes 1540
  30.8 181.6 %copy-start.3 = (s32[256]{0:T(256)S(1)}, s32[256]{0:T(256)}, u32[]{:S(2)}) copy-start(s32[256]{0:T(256)} %param.26) | copy-start | bytes 3076
  205.8 1.2 copy-start.1
  205.8 11.4 %copy-start.4 = (f32[128]{0:T(128)S(1)}, f32[128]{0:T(128)}, u32[]{:S(2)}) copy-start(f32[128]{0:T(128)} %param.22) | copy-start | bytes 1540
  207.0 11.2 %slice-start = ((bf16[2048,2176]{1,0:T(8,128)(2,1)}), bf16[2048,8]{1,0:T(8,128)(2,1)S(1)}, s32[]{:S(2)}) async-start(bf16[2048,2176]{1,0:T(8,128)(2,1)} %all-gather.4.cloned.1.call-done), calls=%async_computation.5 | async-start | bytes 1048576 | tf_op jit(solution)/shard_map/slice | solution.py:72
  209.5 258.5 %reduce-scatter.2.cloned.1.call-start = ((), (), s32[]{:S(2)}) async-start(), calls=%async_computation.4 | async-start | bytes 1310720 | tf_op jit(solution)/shard_map/reduce_scatter | solution.py:208
  434.0 34.0 %copy-start = (bf16[256,512]{1,0:T(8,128)(2,1)S(1)}, bf16[256,512]{1,0:T(8,128)(2,1)}, u32[]{:S(2)}) copy-start(bf16[256,512]{1,0:T(8,128)(2,1)} %param.16) | copy-start | bytes 786436
Sparse Core Ops, SparseCore 0:
  17.8 25.0 all-gather.5
  47.1 153.6 all-gather.3
  209.6 204.9 all-gather.7
  437.7 30.2 reduce-scatter.1

commit v2 on v1

--- a/solution.py
+++ b/solution.py
@@ -1,6 +1,7 @@
 import jax
 import jax.numpy as jnp
 from jax import lax
+from jax.sharding import Mesh
 from jax.sharding import PartitionSpec as P
 
 HEAD_SIZE = 128
@@ -32,6 +33,15 @@
     return jnp.concatenate(
         [former * cosine - latter * sine_part, latter * cosine + former * sine_part], axis=-1
     )
+
+
+SEQ_PARTS = ("z", "y", "xh")
+
+
+def gather_seq(x):
+    for name in reversed(SEQ_PARTS):
+        x = lax.all_gather(x, name, axis=0, tiled=True)
+    return x
 
 
 def body(
@@ -55,7 +65,7 @@
     q_cols = w_query.shape[1]
     kv_cols = key_matrix.shape[1]
     g_cols = w_gate.shape[1]
-    seq_size = lax.axis_size("seq")
+    seq_size = lax.axis_size(SEQ_PARTS)
     stream = local_rows * seq_size
     request_count = prompt_lengths.shape[0]
 
@@ -65,7 +75,7 @@
     packed = jnp.concatenate(
         [w_query, key_matrix, value_matrix, w_gate, w_out.T, mask_block], axis=1
     )
-    gathered = lax.all_gather(packed, "seq", axis=0, tiled=True)
+    gathered = gather_seq(packed)
     proj_cols = q_cols + 2 * kv_cols + g_cols
     w_proj = gathered[:, :proj_cols]
     w_out_t = gathered[:, proj_cols : proj_cols + w_out.shape[0]]
@@ -87,7 +97,7 @@
     values_raw = projected[:, q_cols + kv_cols : q_cols + 2 * kv_cols]
     gate_logits = projected[:, q_cols + 2 * kv_cols :]
 
-    device_seq = lax.axis_index("seq")
+    device_seq = lax.axis_index(SEQ_PARTS)
     token_ids = device_seq * local_rows + jnp.arange(local_rows, dtype=jnp.int32)
     starts = jnp.cumsum(prompt_lengths) - prompt_lengths
     ends = starts + prompt_lengths
@@ -116,7 +126,7 @@
     )
     values_flat = values_raw.astype(jnp.bfloat16)
     kv_local = jnp.concatenate([k_rot, values_flat], axis=1)
-    kv_all = lax.all_gather(kv_local, "seq", axis=0, tiled=True)
+    kv_all = gather_seq(kv_local)
 
     n_blocks = stream // KEY_BLOCK
     block_ids = jnp.arange(n_blocks, dtype=jnp.int32)
@@ -213,26 +223,28 @@
 
 
 def solution(mesh):
+    seq = SEQ_PARTS
+    split = Mesh(mesh.devices.reshape(8, 4, 2, mesh.shape["mdl"]), SEQ_PARTS + ("mdl",))
     placed = (
-        P("seq", "mdl"),
+        P(seq, "mdl"),
         P("mdl"),
-        P("seq", "mdl"),
-        P("seq", "mdl"),
-        P("seq", "mdl"),
-        P("seq", "mdl"),
-        P(),
-        P(),
-        P("mdl", "seq"),
-        P(),
-        P("seq"),
-        P(),
-        P("seq"),
+        P(seq, "mdl"),
+        P(seq, "mdl"),
+        P(seq, "mdl"),
+        P(seq, "mdl"),
+        P(),
+        P(),
+        P("mdl", seq),
+        P(),
+        P(seq),
+        P(),
+        P(seq),
         P(),
     )
     return jax.shard_map(
         body,
-        mesh=mesh,
+        mesh=split,
         in_specs=placed,
-        out_specs=(P("seq", "mdl"), P("seq", None, "mdl"), P("seq", None, "mdl")),
+        out_specs=(P(seq, "mdl"), P(seq, None, "mdl"), P(seq, None, "mdl")),
         check_vma=False,
     )

time: 480 us -> 458 us (0.954)
  waiting for transfers between devices: 383 us -> 355 us
  blocking collectives: 6.9 us -> 23.9 us
    all_gather x2 -> x4, waiting for transfers between devices: 354 us -> 316 us  [gather_seq(): x = lax.all_gather(x, name, axis=0, tiled=True)]
    all_gather x0 -> x2, blocking collectives: none -> 18.2 us  [gather_seq(): x = lax.all_gather(x, name, axis=0, tiled=True)]
    all_gather x1, waiting for transfers between devices: 12.2 us -> 19.5 us  [body(): lax.all_gather(scaled.astype(jnp.bfloat16), 'mdl', axis=1, tiled=True)]
  transfers between devices with their start and end apart: 4 -> 6, of which waited for: 4 -> 6; matrix products, arithmetic and copies ran while one was open for 7% -> 7% of each run, Pallas kernels for 0% -> 0%
where the time goes in v2:
time: 458 us; the launch traced here: 455 us
  waiting for transfers between devices  355 us (78%)
  blocking collectives  23.9 us (5%)
  local copies, waits for them, and re-layouts  23.3 us (5%)
  other arithmetic  21.7 us (5%)
  between operations  17.1 us (4%)
  matrix products  10.1 us (2%)
    all_gather x4, waiting for transfers between devices, gather_seq(): x = lax.all_gather(x, name, axis=0, tiled=True)  316 us
    all_gather x1, waiting for transfers between devices, body(): lax.all_gather(scaled.astype(jnp.bfloat16), 'mdl', axis=1, tiled=True)  19.5 us
    reduce_scatter x1, waiting for transfers between devices, body(): lax.psum_scatter(partial_out.astype(jnp.bfloat16), 'mdl', scatter_dimensi...  19.5 us
    all_gather x2, blocking collectives, gather_seq(): x = lax.all_gather(x, name, axis=0, tiled=True)  18.2 us
    gather x1, local copies, waits for them, and re-layouts, body(): jnp.take(kv_all, source, axis=0)  9.91 us
  transfers between devices with their start and end apart: 6, of which 6 were waited for; matrix products, arithmetic and copies ran while one was open for 7% of the time, Pallas kernels for 0%

profile of v2, /device:TPU:72, one launch (start us, length us, event | category | flops | bytes accessed | tf_op | source)
XLA Modules:
  0.0 454.9 jit_solution(3728250144088888251)
XLA Ops:
  11.7 7.7 %all_gather.21 = bf16[64,2176]{1,0:T(8,128)(2,1)} all-gather(bf16[32,2176]{1,0:T(8,128)(2,1)S(1)} %constant_dynamic-update-slice_fusion), channel_id=1, replica_groups=mesh['z'=8,'y'=4,'xh'=2,'mdl'=4] {'xh'}, dimensions={0}, use_global_device_ids=true | all-gather | bytes 417792 | tf_op jit(solution)/shard_map/all_gather | solution.py:43
  20.2 1.1 fusion.15
  21.3 5.7 %psum.7 = f32[256]{0:T(256)S(1)} all-reduce(f32[256]{0:T(256)S(1)} %fusion.15), channel_id=1, replica_groups=mesh['z'=8,'y'=4,'xh'=2,'mdl'=4] {'mdl'}, use_global_device_ids=true, to_apply=%region_12.13 | all-reduce | flops 256 | bytes 2048 | tf_op jit(solution)/shard_map/psum | solution.py:87
  27.0 1.8 fusion.17
  28.8 18.6 %all-gather.6.cloned.1.call-done = bf16[256,2176]{1,0:T(8,128)(2,1)} async-done(((bf16[64,2176]{1,0:T(8,128)(2,1)}), bf16[256,2176]{1,0:T(8,128)(2,1)}) %all-gather.6.cloned.1.call-update) | async-done | bytes 1114128 | tf_op jit(solution)/shard_map/all_gather | solution.py:43
  48.5 1.3 fusion.36
  51.4 2.0 fusion.34
  55.3 19.5 %all-gather.10.cloned.1.call-done = bf16[256,2048]{1,0:T(8,128)(2,1)} async-done(((bf16[256,512]{1,0:T(8,128)(2,1)}), bf16[256,2048]{1,0:T(8,128)(2,1)}) %all-gather.10.cloned.1.call-update) | async-done | bytes 1048592 | tf_op jit(solution)/shard_map/all_gather | solution.py:93
  74.8 100.1 %all-gather.8.cloned.1.call-done = bf16[2048,2176]{1,0:T(8,128)(2,1)} async-done(((bf16[256,2176]{1,0:T(8,128)(2,1)}), bf16[2048,2176]{1,0:T(8,128)(2,1)}) %all-gather.8.cloned.1.call-update) | async-done | bytes 8912912 | tf_op jit(solution)/shard_map/all_gather | solution.py:43
  174.9 4.9 %fusion.12 = f32[256,1536]{1,0:T(8,128)S(1)} fusion(bf16[256,2048]{1,0:T(8,128)(2,1)} %all-gather.10.cloned.1.call-done, bf16[2048,2176]{1,0:T(8,128)(2,1)} %all-gather.8.cloned.1.call-done), kind=kOutput, calls=%fused_computation.23 | convolution fusion | flops 1610612736 | bytes 8912896 | tf_op jit(solution)/shard_map/dot_general | solution.py:94
  179.9 1.1 copy-done.1
  182.8 10.5 %all_gather.25 = bf16[512,512]{1,0:T(8,128)(2,1)} all-gather(bf16[256,512]{1,0:T(8,128)(2,1)S(1)} %pad_maximum_fusion), channel_id=1, replica_groups=mesh['z'=8,'y'=4,'xh'=2,'mdl'=4] {'xh'}, dimensions={0}, use_global_device_ids=true | all-gather | bytes 786432 | tf_op jit(solution)/shard_map/all_gather | solution.py:43
  193.3 32.9 %all-gather.12.cloned.1.call-done = bf16[2048,512]{1,0:T(8,128)(2,1)} async-done(((bf16[512,512]{1,0:T(8,128)(2,1)}), bf16[2048,512]{1,0:T(8,128)(2,1)}) %all-gather.12.cloned.1.call-update) | async-done | bytes 2097168 | tf_op jit(solution)/shard_map/all_gather | solution.py:43
  229.7 1.0 scatter_custom_fusion
  232.3 1.1 slice.80
  235.6 164.3 %all-gather.14.cloned.1.call-done = bf16[16384,512]{1,0:T(8,128)(2,1)} async-done(((bf16[2048,512]{1,0:T(8,128)(2,1)}), bf16[16384,512]{1,0:T(8,128)(2,1)}) %all-gather.14.cloned.1.call-update) | async-done | bytes 16777232 | tf_op jit(solution)/shard_map/all_gather | solution.py:43
  400.0 10.0 %while.15 = (s32[]{:T(128)}, f32[256,2,2]{0,2,1:T(2,128)S(1)}, f32[256,2,2]{0,2,1:T(2,128)S(1)}, f32[256,2,2,128]{0,3,2,1:T(8,128)S(1)}, s32[]{:T(128)}, /*index...) while((s32[]{:T(128)}, f32[256,2,2]{0,2,1:T(2,128)S(1)}, ...), condition=%wide.region_21.22_spmd.clone, body=%wide.region_17.21_spmd.clone.sunk | while | flops 137415680 | bytes 6105641 | solution.py:197
  402.3 1.0 fusion.60
  406.9 1.0 fusion.60
  410.3 3.6 convolution_convert_fusion
  413.9 1.3 fusion.28
  415.9 9.9 %gather_fusion = bf16[512,512]{1,0:T(8,128)(2,1)S(1)} fusion(bf16[16384,512]{1,0:T(8,128)(2,1)} %get-tuple-element.392, s32[1024]{0:T(1024)S(1)} %pad_clamp_fusion), kind=kCustom, calls=%fused_computation | custom fusion | bytes 1050624 | tf_op jit(solution)/shard_map/jit(_take)/gather | solution.py:206
  426.9 19.5 %reduce-scatter.2.cloned.1.call-done = bf16[256,512]{1,0:T(8,128)(2,1)} async-done(((bf16[256,2048]{1,0:T(8,128)(2,1)}), bf16[256,512]{1,0:T(8,128)(2,1)}) %reduce-scatter.2.cloned.1.call-update) | async-done | bytes 262160 | tf_op jit(solution)/shard_map/reduce_scatter | solution.py:218
  446.3 1.7 fusion.18
  (112 shorter events, 22.7 us)
Async XLA Ops:
  7.2 40.3 %all-gather.6.cloned.1.call-start = ((), (), s32[]{:S(2)}) async-start(), calls=%async_computation.1 | async-start | bytes 1392640 | tf_op jit(solution)/shard_map/all_gather | solution.py:43
  19.5 55.4 %all-gather.10.cloned.1.call-start = ((), (), s32[]{:S(2)}) async-start(), calls=%async_computation.3 | async-start | bytes 1310720 | tf_op jit(solution)/shard_map/all_gather | solution.py:93
  28.8 146.1 %all-gather.8.cloned.1.call-start = ((), (), s32[]{:S(2)}) async-start(), calls=%async_computation.2 | async-start | bytes 10027008 | tf_op jit(solution)/shard_map/all_gather | solution.py:43
  47.5 178.8 %all-gather.12.cloned.1.call-start = ((), (), s32[]{:S(2)}) async-start(), calls=%async_computation.4 | async-start | bytes 2621440 | tf_op jit(solution)/shard_map/all_gather | solution.py:43
  55.3 126.2 %copy-start.4 = (f32[128]{0:T(128)S(1)}, f32[128]{0:T(128)}, u32[]{:S(2)}) copy-start(f32[128]{0:T(128)} %param.23) | copy-start | bytes 1540
  179.8 1.1 copy-start.1
  179.8 49.3 %copy-start.2 = (s32[256]{0:T(256)S(1)}, s32[256]{0:T(256)}, u32[]{:S(2)}) copy-start(s32[256]{0:T(256)} %param.26) | copy-start | bytes 3076
  179.8 54.2 %copy-start.3 = (f32[128]{0:T(128)S(1)}, f32[128]{0:T(128)}, u32[]{:S(2)}) copy-start(f32[128]{0:T(128)} %param.22) | copy-start | bytes 1540
  182.7 52.2 %slice-start = ((bf16[2048,2176]{1,0:T(8,128)(2,1)}), bf16[2048,8]{1,0:T(8,128)(2,1)S(1)}, s32[]{:S(2)}) async-start(bf16[2048,2176]{1,0:T(8,128)(2,1)} %all-gather.8.cloned.1.call-done), calls=%async_computation.7 | async-start | bytes 1048576 | tf_op jit(solution)/shard_map/slice | solution.py:82
  193.3 206.7 %all-gather.14.cloned.1.call-start = ((), (), s32[]{:S(2)}) async-start(), calls=%async_computation.5 | async-start | bytes 18874368 | tf_op jit(solution)/shard_map/all_gather | solution.py:43
  226.3 220.0 %reduce-scatter.2.cloned.1.call-start = ((), (), s32[]{:S(2)}) async-start(), calls=%async_computation.6 | async-start | bytes 1310720 | tf_op jit(solution)/shard_map/reduce_scatter | solution.py:218
  410.3 36.0 %copy-start = (bf16[256,512]{1,0:T(8,128)(2,1)S(1)}, bf16[256,512]{1,0:T(8,128)(2,1)}, u32[]{:S(2)}) copy-start(bf16[256,512]{1,0:T(8,128)(2,1)} %param.16) | copy-start | bytes 786436
Sparse Core Ops, SparseCore 0:
  19.6 27.8 all-gather.5
  49.8 24.9 all-gather.9
  76.6 98.2 all-gather.7
  193.4 32.8 all-gather.11
  227.9 171.9 all-gather.13
  414.0 32.2 reduce-scatter.1

commit v3 on v2

--- a/solution.py
+++ b/solution.py
@@ -42,6 +42,24 @@
     for name in reversed(SEQ_PARTS):
         x = lax.all_gather(x, name, axis=0, tiled=True)
     return x
+
+
+def gather_z_xh(x):
+    x = lax.all_gather(x, "z", axis=0, tiled=True)
+    return lax.all_gather(x, "xh", axis=0, tiled=True)
+
+
+def ring_y(x):
+    ny = 4
+    right = [(i, (i + 1) % ny) for i in range(ny)]
+    left = [(i, (i - 1) % ny) for i in range(ny)]
+    from_minus = lax.ppermute(x, "y", right)
+    from_plus = lax.ppermute(x, "y", left)
+    half = x.shape[0] // 2
+    opp_a = lax.ppermute(from_minus[:half], "y", right)
+    opp_b = lax.ppermute(from_plus[half:], "y", left)
+    opposite = jnp.concatenate([opp_a, opp_b], axis=0)
+    return jnp.stack([x, from_plus, opposite, from_minus])
 
 
 def body(
@@ -72,15 +90,17 @@
     mask_cols = local_rows // weight_rows
     mask_block = key_mask.astype(jnp.bfloat16).reshape(weight_rows, mask_cols)
     mask_block = jnp.pad(mask_block, ((0, 0), (0, 128 - mask_cols)))
-    packed = jnp.concatenate(
-        [w_query, key_matrix, value_matrix, w_gate, w_out.T, mask_block], axis=1
-    )
+    gate_part = gather_z_xh(w_gate)
+    packed = jnp.concatenate([w_query, key_matrix, value_matrix, w_out.T, mask_block], axis=1)
+    packed, gate_part = lax.optimization_barrier((packed, gate_part))
+    gate_ring = ring_y(gate_part)
     gathered = gather_seq(packed)
-    proj_cols = q_cols + 2 * kv_cols + g_cols
+    proj_cols = q_cols + 2 * kv_cols
     w_proj = gathered[:, :proj_cols]
     w_out_t = gathered[:, proj_cols : proj_cols + w_out.shape[0]]
     all_mask = gathered[:, proj_cols + w_out.shape[0] : proj_cols + w_out.shape[0] + mask_cols]
     all_mask = all_mask.reshape(stream)
+    w_gate_perm = gate_ring.reshape(-1, g_cols)
 
     wide_tokens = tokens.astype(jnp.float32)
     full_width = tokens.shape[1] * lax.axis_size("mdl")
@@ -95,7 +115,11 @@
     query_rows = projected[:, :q_cols]
     unprojected_keys = projected[:, q_cols : q_cols + kv_cols]
     values_raw = projected[:, q_cols + kv_cols : q_cols + 2 * kv_cols]
-    gate_logits = projected[:, q_cols + 2 * kv_cols :]
+    my_y = lax.axis_index("y")
+    input_perm = normalized_input.reshape(local_rows, 8, 4, 2, weight_rows)
+    input_perm = jnp.roll(input_perm, -my_y, axis=2)
+    input_perm = input_perm.transpose(0, 2, 3, 1, 4).reshape(local_rows, -1)
+    gate_logits = jnp.dot(input_perm, w_gate_perm, preferred_element_type=jnp.float32)
 
     device_seq = lax.axis_index(SEQ_PARTS)
     token_ids = device_seq * local_rows + jnp.arange(local_rows, dtype=jnp.int32)
@@ -125,8 +149,17 @@
         .reshape(local_rows, kv_cols)
     )
     values_flat = values_raw.astype(jnp.bfloat16)
-    kv_local = jnp.concatenate([k_rot, values_flat], axis=1)
-    kv_all = gather_seq(kv_local)
+    v_part = gather_z_xh(values_flat)
+    k_rot, v_part = lax.optimization_barrier((k_rot, v_part))
+    v_ring = ring_y(v_part)
+    k_all = gather_seq(k_rot)
+    v_ring = v_ring.reshape(-1, kv_cols)
+
+    def v_row_of(token):
+        block = token // local_rows
+        rel = (block // 2 % 4 - my_y) % 4
+        place = (block % 2) * 8 + block // 8
+        return (rel * 16 + place) * local_rows + token % local_rows
 
     n_blocks = stream // KEY_BLOCK
     block_ids = jnp.arange(n_blocks, dtype=jnp.int32)
@@ -159,9 +192,12 @@
         old_top, old_totals, old_summed = loop_state
         block = block_list[i]
         offset = block * KEY_BLOCK
-        kv_part = lax.dynamic_slice_in_dim(kv_all, offset, KEY_BLOCK, 0)
-        keys_part = kv_part[:, :kv_cols].reshape(KEY_BLOCK, kv_heads, HEAD_SIZE)
-        values_part = kv_part[:, kv_cols:].reshape(KEY_BLOCK, kv_heads, HEAD_SIZE)
+        keys_part = lax.dynamic_slice_in_dim(k_all, offset, KEY_BLOCK, 0).reshape(
+            KEY_BLOCK, kv_heads, HEAD_SIZE
+        )
+        values_part = lax.dynamic_slice_in_dim(v_ring, v_row_of(offset), KEY_BLOCK, 0).reshape(
+            KEY_BLOCK, kv_heads, HEAD_SIZE
+        )
         mask_part = lax.dynamic_slice_in_dim(all_mask, offset, KEY_BLOCK, 0)
         columns = offset + jnp.arange(KEY_BLOCK, dtype=jnp.int32)
         col_segs = jnp.sum((columns[:, None] >= ends[None, :]).astype(jnp.int32), axis=1)
@@ -203,9 +239,9 @@
     wanted = my_start + offsets
     in_window = ((wanted < stream) & (offsets < my_length))[:, None]
     source = jnp.clip(wanted, 0, stream - 1)
-    cache_rows = jnp.where(in_window, jnp.take(kv_all, source, axis=0), jnp.zeros((), jnp.bfloat16))
-    cache_k = cache_rows[:, :kv_cols]
-    cache_v = cache_rows[:, kv_cols:]
+    zero = jnp.zeros((), jnp.bfloat16)
+    cache_k = jnp.where(in_window, jnp.take(k_all, source, axis=0), zero)
+    cache_v = jnp.where(in_window, jnp.take(v_ring, v_row_of(source), axis=0), zero)
 
     attended = (summed / totals[..., None]).reshape(local_rows, query_heads * HEAD_SIZE)
     gated_heads = (attended * jax.nn.sigmoid(gate_logits)).astype(jnp.bfloat16)

time: 458 us -> 442 us (0.965)
  waiting for transfers between devices: 355 us -> 249 us
  blocking collectives: 23.9 us -> 71.5 us
  local copies, waits for them, and re-layouts: 23.3 us -> 36.5 us
  other arithmetic: 21.7 us -> 34.3 us
  starting transfers between devices: 0.24 us -> 10 us
    all_gather x4 -> x3, waiting for transfers between devices: 316 us -> 103 us  [gather_seq(): x = lax.all_gather(x, name, axis=0, tiled=True)]
    all_gather x0 -> x2, waiting for transfers between devices: none -> 73.5 us  [the longest x1 36.9 us: gather_z_xh(): return lax.all_gather(x, 'xh', axis=0, tiled=True)]
    ppermute x0 -> x8, waiting for transfers between devices: none -> 71.3 us  [the longest x2 49.5 us: ring_y(): from_minus = lax.ppermute(x, 'y', right)]
    all_gather x0 -> x2, blocking collectives: none -> 35.8 us  [the longest x1 26.8 us: gather_z_xh(): x = lax.all_gather(x, 'z', axis=0, tiled=True)]
    all_gather x1, waiting for transfers between devices: 19.5 us -> 0.02 us  [body(): lax.all_gather(scaled.astype(jnp.bfloat16), 'mdl', axis=1, tiled=True)]
    reduce_scatter x1, waiting for transfers between devices: 19.5 us -> 1.71 us  [body(): lax.psum_scatter(partial_out.astype(jnp.bfloat16), 'mdl', scatter_dimensi...]
    another operation x7 -> x11, other arithmetic: 1.49 us -> 12.6 us  [the longest x4 11.1 us: ring_y(): return jnp.stack([x, from_plus, opposite, from_minus])]
    all_gather x2 -> x3, blocking collectives: 18.2 us -> 28.8 us  [gather_seq(): x = lax.all_gather(x, name, axis=0, tiled=True)]
  transfers between devices with their start and end apart: 6 -> 15, of which waited for: 6 -> 10; matrix products, arithmetic and copies ran while one was open for 7% -> 12% of each run, Pallas kernels for 0% -> 0%
where the time goes in v3:
time: 442 us; the launch traced here: 439 us
  waiting for transfers between devices  249 us (56%)
  blocking collectives  71.5 us (16%)
  local copies, waits for them, and re-layouts  36.5 us (8%)
  other arithmetic  34.3 us (8%)
  between operations  17.2 us (4%)
  matrix products  12.1 us (3%)
  starting transfers between devices  10 us (2%)
  loops' own time  7.57 us (2%)
    all_gather x3, waiting for transfers between devices, gather_seq(): x = lax.all_gather(x, name, axis=0, tiled=True)  103 us
    ppermute x2, waiting for transfers between devices, ring_y(): from_minus = lax.ppermute(x, 'y', right)  49.5 us
    all_gather x1, waiting for transfers between devices, gather_z_xh(): return lax.all_gather(x, 'xh', axis=0, tiled=True)  36.9 us
    all_gather x1, waiting for transfers between devices, gather_z_xh(): x = lax.all_gather(x, 'z', axis=0, tiled=True)  36.6 us
    all_gather x3, blocking collectives, gather_seq(): x = lax.all_gather(x, name, axis=0, tiled=True)  28.8 us
    all_gather x1, blocking collectives, gather_z_xh(): x = lax.all_gather(x, 'z', axis=0, tiled=True)  26.8 us
    ppermute x2, waiting for transfers between devices, ring_y(): opp_a = lax.ppermute(from_minus[:half], 'y', right)  14.6 us
    another operation x4, other arithmetic, ring_y(): return jnp.stack([x, from_plus, opposite, from_minus])  11.1 us
  transfers between devices with their start and end apart: 15, of which 10 were waited for; matrix products, arithmetic and copies ran while one was open for 12% of the time, Pallas kernels for 0%

profile of v3, /device:TPU:72, one launch (start us, length us, event | category | flops | bytes accessed | tf_op | source)
XLA Modules:
  0.0 438.6 jit_solution(7276092003855053308)
XLA Ops:
  8.3 6.9 %psum.7 = f32[256]{0:T(256)S(1)} all-reduce(f32[256]{0:T(256)S(1)} %fusion.22), channel_id=1, replica_groups=mesh['z'=8,'y'=4,'xh'=2,'mdl'=4] {'mdl'}, use_global_device_ids=true, to_apply=%region_12.13 | all-reduce | flops 256 | bytes 2048 | tf_op jit(solution)/shard_map/psum | solution.py:107
  15.9 1.8 fusion.24
  21.5 26.8 %all_gather.33 = bf16[256,512]{1,0:T(8,128)(2,1)S(1)} all-gather(bf16[32,512]{1,0:T(8,128)(2,1)} %param.23), channel_id=1, replica_groups=mesh['z'=8,'y'=4,'xh'=2,'mdl'=4] {'z'}, dimensions={0}, use_global_device_ids=true | all-gather | bytes 294912 | tf_op jit(solution)/shard_map/all_gather | solution.py:48
  48.3 9.0 %all_gather.34 = bf16[512,512]{1,0:T(8,128)(2,1)S(1)} all-gather(bf16[256,512]{1,0:T(8,128)(2,1)S(1)} %all_gather.33), channel_id=1, replica_groups=mesh['z'=8,'y'=4,'xh'=2,'mdl'=4] {'xh'}, dimensions={0}, use_global_device_ids=true | all-gather | bytes 786432 | tf_op jit(solution)/shard_map/all_gather | solution.py:49
  57.3 6.9 %all_gather.35 = bf16[64,1664]{1,0:T(8,128)(2,1)S(1)} all-gather(bf16[32,1664]{1,0:T(8,128)(2,1)S(1)} %constant_dynamic-update-slice_fusion), channel_id=1, replica_groups=mesh['z'=8,'y'=4,'xh'=2,'mdl'=4] {'xh'}, dimensions={0}, use_global_device_ids=true | all-gather | bytes 319488 | tf_op jit(solution)/shard_map/all_gather | solution.py:43
  64.2 14.4 %all_gather.36 = bf16[256,1664]{1,0:T(8,128)(2,1)} all-gather(bf16[64,1664]{1,0:T(8,128)(2,1)S(1)} %all_gather.35), channel_id=1, replica_groups=mesh['z'=8,'y'=4,'xh'=2,'mdl'=4] {'y'}, dimensions={0}, use_global_device_ids=true | all-gather | bytes 1064960 | tf_op jit(solution)/shard_map/all_gather | solution.py:43
  78.7 77.4 %all-gather.7.cloned.1.call-done = bf16[2048,1664]{1,0:T(8,128)(2,1)} async-done(((bf16[256,1664]{1,0:T(8,128)(2,1)}), bf16[2048,1664]{1,0:T(8,128)(2,1)}) %all-gather.7.cloned.1.call-update) | async-done | bytes 6815760 | tf_op jit(solution)/shard_map/all_gather | solution.py:43
  156.2 3.8 fusion.12
  161.7 36.6 %all-gather.11.cloned.1.call-done = bf16[2048,256]{1,0:T(8,128)(2,1)} async-done(((bf16[256,256]{1,0:T(8,128)(2,1)}), bf16[2048,256]{1,0:T(8,128)(2,1)}) %all-gather.11.cloned.1.call-update) | async-done | bytes 1048592 | tf_op jit(solution)/shard_map/all_gather | solution.py:48
  202.9 36.9 %all-gather.13.cloned.1.call-done = bf16[4096,256]{1,0:T(8,128)(2,1)} async-done(((bf16[2048,256]{1,0:T(8,128)(2,1)}), bf16[4096,256]{1,0:T(8,128)(2,1)}) %all-gather.13.cloned.1.call-update) | async-done | bytes 2097168 | tf_op jit(solution)/shard_map/all_gather | solution.py:49
  239.8 7.5 %all_gather.41 = bf16[512,256]{1,0:T(8,128)(2,1)} all-gather(bf16[256,256]{1,0:T(8,128)(2,1)S(1)} %bitcast.93), channel_id=1, replica_groups=mesh['z'=8,'y'=4,'xh'=2,'mdl'=4] {'xh'}, dimensions={0}, use_global_device_ids=true | all-gather | bytes 393216 | tf_op jit(solution)/shard_map/all_gather | solution.py:43
  247.4 25.2 %all-gather.15.cloned.1.call-done = bf16[2048,256]{1,0:T(8,128)(2,1)} async-done(((bf16[512,256]{1,0:T(8,128)(2,1)}), bf16[2048,256]{1,0:T(8,128)(2,1)}) %all-gather.15.cloned.1.call-update) | async-done | bytes 1048592 | tf_op jit(solution)/shard_map/all_gather | solution.py:43
  280.8 49.5 %collective-permute-done.5 = bf16[512,512]{1,0:T(8,128)(2,1)S(1)} collective-permute-done((bf16[512,512]{1,0:T(8,128)(2,1)S(1)}, bf16[512,512]{1,0:T(8,128)(2,1)S(1)}, u32[]{:S(2)}, u32[]{:S(2)}) %collective-permute-start.5) | collective-permute-done | bytes 524320 | tf_op jit(solution)/shard_map/ppermute | solution.py:56
  331.1 1.8 collective-permute-start.6
  338.8 2.4 collective-permute-done.7
  342.3 2.7 pad_maximum_fusion.1
  349.4 2.3 slice.82
  356.1 14.0 %collective-permute-done.2 = bf16[2048,256]{1,0:T(8,128)(2,1)} collective-permute-done((bf16[2048,256]{1,0:T(8,128)(2,1)}, bf16[2048,256]{1,0:T(8,128)(2,1)}, u32[]{:S(2)}, u32[]{:S(2)}) %collective-permute-start.2) | collective-permute-done | bytes 1048608 | tf_op jit(solution)/shard_map/ppermute | solution.py:59
  370.1 4.8 %collective-permute-done.3 = bf16[2048,256]{1,0:T(8,128)(2,1)} collective-permute-done((bf16[2048,256]{1,0:T(8,128)(2,1)}, bf16[2048,256]{1,0:T(8,128)(2,1)}, u32[]{:S(2)}, u32[]{:S(2)}) %collective-permute-start.3) | collective-permute-done | bytes 1048608 | tf_op jit(solution)/shard_map/ppermute | solution.py:60
  376.6 5.7 %pad_maximum_fusion = bf16[4,4096,256]{2,1,0:T(8,128)(2,1)} fusion(bf16[1,4096,256]{2,1,0:T(8,128)(2,1)S(1)} %bitcast.83, bf16[1,4096,256]{2,1,0:T(8,128)(2,1)S(1)} %maximum_bitcast_fusion, bf16[1,4096,256]{2,1,0:T(8,128)(2,1)} %bitcast.9, bf16[1,4096,256]{2,1,0:T(8,128)(2,1)S(1)} %bitcast.88), kind=kLoop, calls=%fused_computation.25 | loop fusion | flops 12582912 | bytes 16777216 | tf_op jit(solution)/shard_map/stack | solution.py:62
  382.3 23.5 %while.18 = (s32[]{:T(128)}, f32[256,2,2]{0,2,1:T(2,128)S(1)}, f32[256,2,2]{0,2,1:T(2,128)S(1)}, f32[256,2,2,128]{0,3,2,1:T(8,128)S(1)}, s32[]{:T(128)}, /*index...) while((s32[]{:T(128)}, f32[256,2,2]{0,2,1:T(2,128)S(1)}, ...), condition=%wide.region_21.22_spmd.clone, body=%wide.region_17.21_spmd.clone.sunk | while | flops 137415776 | bytes 6106513 | solution.py:233
  407.4 4.3 convolution_convert_fusion
  415.0 6.0 %gather_fusion.1 = bf16[512,256]{1,0:T(8,128)(2,1)S(1)} fusion(bf16[16384,256]{1,0:T(8,128)(2,1)} %get-tuple-element.638, s32[1024]{0:T(1024)S(1)} %get-tuple-element.434), kind=kCustom, calls=%fused_computation.1.clone | custom fusion | bytes 526336 | tf_op jit(solution)/shard_map/jit(_take)/gather | solution.py:244
  421.1 6.1 %gather_fusion = bf16[512,256]{1,0:T(8,128)(2,1)S(1)} fusion(bf16[16384,256]{1,0:T(8,128)(2,1)} %get-tuple-element.663, s32[1024]{0:T(1024)S(1)} %get-tuple-element.435), kind=kCustom, calls=%fused_computation.clone | custom fusion | bytes 526336 | tf_op jit(solution)/shard_map/jit(_take)/gather | solution.py:243
  (202 shorter events, 60.9 us)
Async XLA Ops:
  7.2 71.5 %all-gather.9.cloned.1.call-start = ((), (), s32[]{:S(2)}) async-start(), calls=%async_computation.2 | async-start | bytes 1310720 | tf_op jit(solution)/shard_map/all_gather | solution.py:113
  17.7 138.5 %all-gather.7.cloned.1.call-start = ((), (), s32[]{:S(2)}) async-start(), calls=%async_computation.1 | async-start | bytes 7667712 | tf_op jit(solution)/shard_map/all_gather | solution.py:43
  78.6 82.1 %copy-start.7 = (s32[64]{0:T(128)S(1)}, s32[64]{0:T(128)}, u32[]{:S(2)}) copy-start(s32[64]{0:T(128)} %param.27) | copy-start | bytes 772
  78.6 82.4 %copy-start.11 = (s32[64]{0:T(128)S(1)}, s32[64]{0:T(128)}, u32[]{:S(2)}) copy-start(s32[64]{0:T(128)} %param.31) | copy-start | bytes 772
  78.6 83.1 %copy-start.8 = (s32[4,2]{0,1:T(2,128)S(1)}, s32[4,2]{0,1:T(2,128)}, u32[]{:S(2)}) copy-start(s32[4,2]{0,1:T(2,128)} %param.29) | copy-start | bytes 100
  78.6 121.2 %copy-start.6 = (s32[256]{0:T(256)S(1)}, s32[256]{0:T(256)}, u32[]{:S(2)}) copy-start(s32[256]{0:T(256)} %param.28) | copy-start | bytes 3076
  78.6 119.7 %all-gather.11.cloned.1.call-start = ((), (), s32[]{:S(2)}) async-start(), calls=%async_computation.3 | async-start | bytes 1179648 | tf_op jit(solution)/shard_map/all_gather | solution.py:48
  159.9 41.1 %copy-start.4 = (f32[256,1024]{1,0:T(8,128)}, f32[256,1024]{1,0:T(8,128)S(1)}, u32[]{:S(2)}) copy-start(f32[256,1024]{1,0:T(8,128)S(1)} %fusion.12) | copy-start | bytes 3145732
  159.9 41.7 %copy-start.10 = (f32[128]{0:T(128)S(1)}, f32[128]{0:T(128)}, u32[]{:S(2)}) copy-start(f32[128]{0:T(128)} %param.25) | copy-start | bytes 1540
  160.6 79.1 %all-gather.13.cloned.1.call-start = ((), (), s32[]{:S(2)}) async-start(), calls=%async_computation.4 | async-start | bytes 3145728 | tf_op jit(solution)/shard_map/all_gather | solution.py:49
  198.3 74.2 %all-gather.15.cloned.1.call-start = ((), (), s32[]{:S(2)}) async-start(), calls=%async_computation.5 | async-start | bytes 1310720 | tf_op jit(solution)/shard_map/all_gather | solution.py:43
  247.3 135.0 %all-gather.17.cloned.1.call-start = ((), (), s32[]{:S(2)}) async-start(), calls=%async_computation.6 | async-start | bytes 9437184 | tf_op jit(solution)/shard_map/all_gather | solution.py:43
  272.6 157.4 %reduce-scatter.2.cloned.1.call-start = ((), (), s32[]{:S(2)}) async-start(), calls=%async_computation.7 | async-start | bytes 1310720 | tf_op jit(solution)/shard_map/reduce_scatter | solution.py:254
  272.6 73.8 %collective-permute-start.1 = (bf16[4096,256]{1,0:T(8,128)(2,1)}, bf16[4096,256]{1,0:T(8,128)(2,1)S(1)}, u32[]{:S(2)}, u32[]{:S(2)}) collective-permute-start(bf16[4096,256]{1,0:T(8,128)(2,1)} %all-gather.13.cloned.1.call-done), channel_id=1, source_target_pairs={{0,8},{8,16},{16,24},{24,0},{1,9},{9,17},{17,25},{25,1},{2,10},{10... | collective-permute-start | bytes 6291464 | tf_op jit(solution)/shard_map/ppermute | solution.py:56
  274.2 75.2 %collective-permute-start = (bf16[4096,256]{1,0:T(8,128)(2,1)}, bf16[4096,256]{1,0:T(8,128)(2,1)}, u32[]{:S(2)}, u32[]{:S(2)}) collective-permute-start(bf16[4096,256]{1,0:T(8,128)(2,1)} %all-gather.13.cloned.1.call-done), channel_id=1, source_target_pairs={{0,24},{8,0},{16,8},{24,16},{1,25},{9,1},{17,9},{25,17},{2,26},{10... | collective-permute-start | bytes 6291464 | tf_op jit(solution)/shard_map/ppermute | solution.py:57
  274.7 55.6 %collective-permute-start.5 = (bf16[512,512]{1,0:T(8,128)(2,1)S(1)}, bf16[512,512]{1,0:T(8,128)(2,1)S(1)}, u32[]{:S(2)}, u32[]{:S(2)}) collective-permute-start(bf16[512,512]{1,0:T(8,128)(2,1)S(1)} %all_gather.34), channel_id=1, source_target_pairs={{0,8},{8,16},{16,24},{24,0},{1,9},{9,17},{17,25},{25,1},{2,10},{10... | collective-permute-start | bytes 1572872 | tf_op jit(solution)/shard_map/ppermute | solution.py:56
  276.2 56.7 %collective-permute-start.4 = (bf16[512,512]{1,0:T(8,128)(2,1)S(1)}, bf16[512,512]{1,0:T(8,128)(2,1)}, u32[]{:S(2)}, u32[]{:S(2)}) collective-permute-start(bf16[512,512]{1,0:T(8,128)(2,1)S(1)} %all_gather.34), channel_id=1, source_target_pairs={{0,24},{8,0},{16,8},{24,16},{1,25},{9,1},{17,9},{25,17},{2,26},{10... | collective-permute-start | bytes 1572872 | tf_op jit(solution)/shard_map/ppermute | solution.py:57
  331.1 7.7 %collective-permute-start.6 = (bf16[256,512]{1,0:T(8,128)(2,1)}, bf16[256,512]{1,0:T(8,128)(2,1)}, u32[]{:S(2)}, u32[]{:S(2)}) collective-permute-start(bf16[256,512]{1,0:T(8,128)(2,1)} %slice.83), channel_id=1, source_target_pairs={{0,8},{8,16},{16,24},{24,0},{1,9},{9,17},{17,25},{25,1},{2,10},{10... | collective-permute-start | bytes 786440 | tf_op jit(solution)/shard_map/ppermute | solution.py:59
  334.5 6.7 %collective-permute-start.7 = (bf16[256,512]{1,0:T(8,128)(2,1)}, bf16[256,512]{1,0:T(8,128)(2,1)}, u32[]{:S(2)}, u32[]{:S(2)}) collective-permute-start(bf16[256,512]{1,0:T(8,128)(2,1)} %slice.84), channel_id=1, source_target_pairs={{0,24},{8,0},{16,8},{24,16},{1,25},{9,1},{17,9},{25,17},{2,26},{10... | collective-permute-start | bytes 786440 | tf_op jit(solution)/shard_map/ppermute | solution.py:60
  347.6 22.4 %collective-permute-start.2 = (bf16[2048,256]{1,0:T(8,128)(2,1)}, bf16[2048,256]{1,0:T(8,128)(2,1)}, u32[]{:S(2)}, u32[]{:S(2)}) collective-permute-start(bf16[2048,256]{1,0:T(8,128)(2,1)} %slice.81), channel_id=1, source_target_pairs={{0,8},{8,16},{16,24},{24,0},{1,9},{9,17},{17,25},{25,1},{2,10},{10... | collective-permute-start | bytes 3145736 | tf_op jit(solution)/shard_map/ppermute | solution.py:59
  351.7 23.2 %collective-permute-start.3 = (bf16[2048,256]{1,0:T(8,128)(2,1)}, bf16[2048,256]{1,0:T(8,128)(2,1)}, u32[]{:S(2)}, u32[]{:S(2)}) collective-permute-start(bf16[2048,256]{1,0:T(8,128)(2,1)} %slice.82), channel_id=1, source_target_pairs={{0,24},{8,0},{16,8},{24,16},{1,25},{9,1},{17,9},{25,17},{2,26},{10... | collective-permute-start | bytes 3145736 | tf_op jit(solution)/shard_map/ppermute | solution.py:60
  356.1 20.5 %copy-start.1 = (bf16[4096,256]{1,0:T(8,128)(2,1)S(1)}, bf16[4096,256]{1,0:T(8,128)(2,1)}, u32[]{:S(2)}) copy-start(bf16[4096,256]{1,0:T(8,128)(2,1)} %copy-done) | copy-start | bytes 6291460
  356.1 20.5 %copy-start.5 = (bf16[4096,256]{1,0:T(8,128)(2,1)S(1)}, bf16[4096,256]{1,0:T(8,128)(2,1)}, u32[]{:S(2)}) copy-start(bf16[4096,256]{1,0:T(8,128)(2,1)} %all-gather.13.cloned.1.call-done) | copy-start | bytes 6291460
  421.0 8.9 %copy-start.2 = (bf16[256,512]{1,0:T(8,128)(2,1)S(1)}, bf16[256,512]{1,0:T(8,128)(2,1)}, u32[]{:S(2)}) copy-start(bf16[256,512]{1,0:T(8,128)(2,1)} %param.18) | copy-start | bytes 786436
  (5 other events, 10.7 us)
Sparse Core Ops, SparseCore 0:
  17.8 25.0 all-gather.8
  78.7 77.3 all-gather.6
  160.8 37.4 all-gather.10
  199.9 39.7 all-gather.12
  247.4 25.0 all-gather.14
  274.2 93.5 all-gather.16
  411.9 18.0 reduce-scatter.1

commit v4 on v3

--- a/solution.py
+++ b/solution.py
@@ -44,9 +44,9 @@
     return x
 
 
-def gather_z_xh(x):
-    x = lax.all_gather(x, "z", axis=0, tiled=True)
-    return lax.all_gather(x, "xh", axis=0, tiled=True)
+def gather_xh_z(x):
+    x = lax.all_gather(x, "xh", axis=0, tiled=True)
+    return lax.all_gather(x, "z", axis=0, tiled=True)
 
 
 def ring_y(x):
@@ -90,11 +90,12 @@
     mask_cols = local_rows // weight_rows
     mask_block = key_mask.astype(jnp.bfloat16).reshape(weight_rows, mask_cols)
     mask_block = jnp.pad(mask_block, ((0, 0), (0, 128 - mask_cols)))
-    gate_part = gather_z_xh(w_gate)
     packed = jnp.concatenate([w_query, key_matrix, value_matrix, w_out.T, mask_block], axis=1)
-    packed, gate_part = lax.optimization_barrier((packed, gate_part))
-    gate_ring = ring_y(gate_part)
-    gathered = gather_seq(packed)
+    packed = lax.all_gather(packed, "xh", axis=0, tiled=True)
+    packed = lax.all_gather(packed, "y", axis=0, tiled=True)
+    packed, gate_in = lax.optimization_barrier((packed, w_gate))
+    gate_ring = ring_y(gather_xh_z(gate_in))
+    gathered = lax.all_gather(packed, "z", axis=0, tiled=True)
     proj_cols = q_cols + 2 * kv_cols
     w_proj = gathered[:, :proj_cols]
     w_out_t = gathered[:, proj_cols : proj_cols + w_out.shape[0]]
@@ -118,7 +119,7 @@
     my_y = lax.axis_index("y")
     input_perm = normalized_input.reshape(local_rows, 8, 4, 2, weight_rows)
     input_perm = jnp.roll(input_perm, -my_y, axis=2)
-    input_perm = input_perm.transpose(0, 2, 3, 1, 4).reshape(local_rows, -1)
+    input_perm = input_perm.transpose(0, 2, 1, 3, 4).reshape(local_rows, -1)
     gate_logits = jnp.dot(input_perm, w_gate_perm, preferred_element_type=jnp.float32)
 
     device_seq = lax.axis_index(SEQ_PARTS)
@@ -149,7 +150,7 @@
         .reshape(local_rows, kv_cols)
     )
     values_flat = values_raw.astype(jnp.bfloat16)
-    v_part = gather_z_xh(values_flat)
+    v_part = gather_xh_z(values_flat)
     k_rot, v_part = lax.optimization_barrier((k_rot, v_part))
     v_ring = ring_y(v_part)
     k_all = gather_seq(k_rot)
@@ -158,7 +159,7 @@
     def v_row_of(token):
         block = token // local_rows
         rel = (block // 2 % 4 - my_y) % 4
-        place = (block % 2) * 8 + block // 8
+        place = (block // 8) * 2 + block % 2
         return (rel * 16 + place) * local_rows + token % local_rows
 
     n_blocks = stream // KEY_BLOCK
@@ -251,9 +252,21 @@
         (((1,), (1,)), ((), ())),
         preferred_element_type=jnp.float32,
     )
-    branch_sum = lax.psum_scatter(
-        partial_out.astype(jnp.bfloat16), "mdl", scatter_dimension=1, tiled=True
-    ).astype(jnp.float32)
+    mdl_index = lax.axis_index("mdl")
+    n_mdl = lax.axis_size("mdl")
+    x_lo = mdl_index // 2
+    core = mdl_index % 2
+    half = partial_out.shape[1] // 2
+    quarter = half // 2
+    mine = lax.dynamic_slice_in_dim(partial_out, x_lo * half, half, 1)
+    theirs = lax.dynamic_slice_in_dim(partial_out, (1 - x_lo) * half, half, 1)
+    across = lax.ppermute(
+        theirs.astype(jnp.bfloat16), "mdl", [(m, m ^ 2) for m in range(n_mdl)]
+    )
+    half_sum = mine + across.astype(jnp.float32)
+    mine = lax.dynamic_slice_in_dim(half_sum, core * quarter, quarter, 1)
+    theirs = lax.dynamic_slice_in_dim(half_sum, (1 - core) * quarter, quarter, 1)
+    branch_sum = mine + lax.ppermute(theirs, "mdl", [(m, m ^ 1) for m in range(n_mdl)])
     layer_out = (wide_tokens + branch_sum).astype(jnp.bfloat16)
     return (layer_out, cache_k[None], cache_v[None])
 

time: 442 us -> 384 us (0.87)
  waiting for transfers between devices: 249 us -> 185 us
  blocking collectives: 71.5 us -> 76.9 us
    all_gather x3 -> x2, waiting for transfers between devices: 103 us -> 25.6 us  [gather_seq(): x = lax.all_gather(x, name, axis=0, tiled=True)]
    all_gather x2, waiting for transfers between devices: 73.5 us -> 115 us  [the longest x1 80.6 us: body(): gathered = lax.all_gather(packed, 'z', axis=0, tiled=True)]
    ppermute x2, waiting for transfers between devices: 49.5 us -> 15.4 us  [ring_y(): from_minus = lax.ppermute(x, 'y', right)]
    all_gather x2 -> x5, blocking collectives: 35.8 us -> 62.7 us  [the longest x1 27.9 us: gather_xh_z(): return lax.all_gather(x, 'z', axis=0, tiled=True)]
    all_gather x3 -> x1, blocking collectives: 28.8 us -> 7.24 us  [gather_seq(): x = lax.all_gather(x, name, axis=0, tiled=True)]
    ppermute x0 -> x2, waiting for transfers between devices: none -> 6.66 us  [the longest x1 6.66 us: body(): lax.ppermute(theirs.astype(jnp.bfloat16), 'mdl', [(m, m ^ 2) for m in ran...]
  transfers between devices with their start and end apart: 15 -> 15, of which waited for: 10 -> 9; matrix products, arithmetic and copies ran while one was open for 12% -> 13% of each run, Pallas kernels for 0% -> 0%
where the time goes in v4:
time: 384 us; the launch traced here: 378 us
  waiting for transfers between devices  185 us (48%)
  blocking collectives  76.9 us (20%)
  local copies, waits for them, and re-layouts  35.4 us (9%)
  other arithmetic  34.2 us (9%)
  between operations  17 us (4%)
  starting transfers between devices  11.8 us (3%)
  matrix products  11.7 us (3%)
  loops' own time  6.17 us (2%)
    all_gather x1, waiting for transfers between devices, body(): gathered = lax.all_gather(packed, 'z', axis=0, tiled=True)  80.6 us
    all_gather x1, waiting for transfers between devices, gather_xh_z(): return lax.all_gather(x, 'z', axis=0, tiled=True)  34.8 us
    all_gather x1, blocking collectives, gather_xh_z(): return lax.all_gather(x, 'z', axis=0, tiled=True)  27.9 us
    all_gather x2, waiting for transfers between devices, gather_seq(): x = lax.all_gather(x, name, axis=0, tiled=True)  25.6 us
    ppermute x2, waiting for transfers between devices, ring_y(): from_minus = lax.ppermute(x, 'y', right)  15.4 us
    ppermute x2, waiting for transfers between devices, ring_y(): opp_a = lax.ppermute(from_minus[:half], 'y', right)  14.5 us
    all_gather x1, blocking collectives, body(): packed = lax.all_gather(packed, 'y', axis=0, tiled=True)  14.4 us
    all_gather x2, blocking collectives, gather_xh_z(): x = lax.all_gather(x, 'xh', axis=0, tiled=True)  13.6 us
  transfers between devices with their start and end apart: 15, of which 9 were waited for; matrix products, arithmetic and copies ran while one was open for 13% of the time, Pallas kernels for 0%

profile of v4, /device:TPU:72, one launch (start us, length us, event | category | flops | bytes accessed | tf_op | source)
XLA Modules:
  0.0 377.9 jit_solution(5261714137230889997)
XLA Ops:
  8.3 6.9 %psum.7 = f32[256]{0:T(256)S(1)} all-reduce(f32[256]{0:T(256)S(1)} %fusion.23), channel_id=1, replica_groups=mesh['z'=8,'y'=4,'xh'=2,'mdl'=4] {'mdl'}, use_global_device_ids=true, to_apply=%region_12.13 | all-reduce | flops 256 | bytes 2048 | tf_op jit(solution)/shard_map/psum | solution.py:108
  21.5 6.9 %all_gather.33 = bf16[64,1664]{1,0:T(8,128)(2,1)S(1)} all-gather(bf16[32,1664]{1,0:T(8,128)(2,1)S(1)} %constant_dynamic-update-slice_fusion), channel_id=1, replica_groups=mesh['z'=8,'y'=4,'xh'=2,'mdl'=4] {'xh'}, dimensions={0}, use_global_device_ids=true | all-gather | bytes 319488 | tf_op jit(solution)/shard_map/all_gather | solution.py:94
  28.4 14.4 %all_gather.34 = bf16[256,1664]{1,0:T(8,128)(2,1)} all-gather(bf16[64,1664]{1,0:T(8,128)(2,1)S(1)} %all_gather.33), channel_id=1, replica_groups=mesh['z'=8,'y'=4,'xh'=2,'mdl'=4] {'y'}, dimensions={0}, use_global_device_ids=true | all-gather | bytes 1064960 | tf_op jit(solution)/shard_map/all_gather | solution.py:95
  42.9 80.6 %all-gather.6.cloned.1.call-done = bf16[2048,1664]{1,0:T(8,128)(2,1)} async-done(((bf16[256,1664]{1,0:T(8,128)(2,1)}), bf16[2048,1664]{1,0:T(8,128)(2,1)}) %all-gather.6.cloned.1.call-update) | async-done | bytes 6815760 | tf_op jit(solution)/shard_map/all_gather | solution.py:98
  123.5 3.8 fusion.12
  127.3 7.5 %all_gather.37 = bf16[512,256]{1,0:T(8,128)(2,1)} all-gather(bf16[256,256]{1,0:T(8,128)(2,1)S(1)} %slice.103), channel_id=1, replica_groups=mesh['z'=8,'y'=4,'xh'=2,'mdl'=4] {'xh'}, dimensions={0}, use_global_device_ids=true | all-gather | bytes 393216 | tf_op jit(solution)/shard_map/all_gather | solution.py:48
  140.4 34.8 %all-gather.10.cloned.1.call-done = bf16[4096,256]{1,0:T(8,128)(2,1)} async-done(((bf16[512,256]{1,0:T(8,128)(2,1)}), bf16[4096,256]{1,0:T(8,128)(2,1)}) %all-gather.10.cloned.1.call-update) | async-done | bytes 2097168 | tf_op jit(solution)/shard_map/all_gather | solution.py:49
  175.2 7.2 %all_gather.39 = bf16[512,256]{1,0:T(8,128)(2,1)} all-gather(bf16[256,256]{1,0:T(8,128)(2,1)S(1)} %bitcast.93), channel_id=1, replica_groups=mesh['z'=8,'y'=4,'xh'=2,'mdl'=4] {'xh'}, dimensions={0}, use_global_device_ids=true | all-gather | bytes 393216 | tf_op jit(solution)/shard_map/all_gather | solution.py:43
  182.5 25.6 %all-gather.12.cloned.1.call-done = bf16[2048,256]{1,0:T(8,128)(2,1)} async-done(((bf16[512,256]{1,0:T(8,128)(2,1)}), bf16[2048,256]{1,0:T(8,128)(2,1)}) %all-gather.12.cloned.1.call-update) | async-done | bytes 1048592 | tf_op jit(solution)/shard_map/all_gather | solution.py:43
  210.2 6.1 %all_gather.42 = bf16[64,512]{1,0:T(8,128)(2,1)S(1)} all-gather(bf16[32,512]{1,0:T(8,128)(2,1)S(1)} %copy-done.7), channel_id=1, replica_groups=mesh['z'=8,'y'=4,'xh'=2,'mdl'=4] {'xh'}, dimensions={0}, use_global_device_ids=true | all-gather | bytes 98304 | tf_op jit(solution)/shard_map/all_gather | solution.py:48
  216.3 27.9 %all_gather.43 = bf16[512,512]{1,0:T(8,128)(2,1)S(1)} all-gather(bf16[64,512]{1,0:T(8,128)(2,1)S(1)} %all_gather.42), channel_id=1, replica_groups=mesh['z'=8,'y'=4,'xh'=2,'mdl'=4] {'z'}, dimensions={0}, use_global_device_ids=true | all-gather | bytes 589824 | tf_op jit(solution)/shard_map/all_gather | solution.py:49
  250.5 15.4 %collective-permute-done.5 = bf16[512,512]{1,0:T(8,128)(2,1)S(1)} collective-permute-done((bf16[512,512]{1,0:T(8,128)(2,1)S(1)}, bf16[512,512]{1,0:T(8,128)(2,1)S(1)}, u32[]{:S(2)}, u32[]{:S(2)}) %collective-permute-start.5) | collective-permute-done | bytes 524320 | tf_op jit(solution)/shard_map/ppermute | solution.py:56
  266.6 1.8 collective-permute-start.6
  274.3 2.4 collective-permute-done.7
  277.8 2.7 pad_maximum_fusion.1
  284.9 2.3 slice.82
  291.6 13.9 %collective-permute-done.2 = bf16[2048,256]{1,0:T(8,128)(2,1)} collective-permute-done((bf16[2048,256]{1,0:T(8,128)(2,1)}, bf16[2048,256]{1,0:T(8,128)(2,1)}, u32[]{:S(2)}, u32[]{:S(2)}) %collective-permute-start.2) | collective-permute-done | bytes 1048608 | tf_op jit(solution)/shard_map/ppermute | solution.py:59
  305.5 4.8 %collective-permute-done.3 = bf16[2048,256]{1,0:T(8,128)(2,1)} collective-permute-done((bf16[2048,256]{1,0:T(8,128)(2,1)}, bf16[2048,256]{1,0:T(8,128)(2,1)}, u32[]{:S(2)}, u32[]{:S(2)}) %collective-permute-start.3) | collective-permute-done | bytes 1048608 | tf_op jit(solution)/shard_map/ppermute | solution.py:60
  312.0 5.7 %pad_maximum_fusion = bf16[4,4096,256]{2,1,0:T(8,128)(2,1)} fusion(bf16[1,4096,256]{2,1,0:T(8,128)(2,1)S(1)} %bitcast.83, bf16[1,4096,256]{2,1,0:T(8,128)(2,1)S(1)} %maximum_bitcast_fusion, bf16[1,4096,256]{2,1,0:T(8,128)(2,1)} %bitcast.9, bf16[1,4096,256]{2,1,0:T(8,128)(2,1)S(1)} %bitcast.88), kind=kLoop, calls=%fused_computation.25 | loop fusion | flops 12582912 | bytes 16777216 | tf_op jit(solution)/shard_map/stack | solution.py:62
  317.8 18.9 %while.18 = (s32[]{:T(128)}, f32[256,2,2]{0,2,1:T(2,128)S(1)}, f32[256,2,2]{0,2,1:T(2,128)S(1)}, f32[256,2,2,128]{0,3,2,1:T(8,128)S(1)}, s32[]{:T(128)}, /*index...) while((s32[]{:T(128)}, f32[256,2,2]{0,2,1:T(2,128)S(1)}, ...), condition=%wide.region_21.22_spmd.clone, body=%wide.region_17.21_spmd.clone.sunk | while | flops 137415776 | bytes 6106513 | solution.py:234
  338.3 4.7 %fusion.14 = f32[256,2048]{1,0:T(8,128)} fusion(bf16[2048,1664]{1,0:T(8,128)(2,1)} %all-gather.6.cloned.1.call-done, f32[256,512]{1,0:T(8,128)S(1)} %copy.80, bf16[256,2048]{0,1:T(8,128)(2,1)} %bitcast.92, bf16[2048,512]{1,0:T(8,128)(2,1)S(1)} %bitcast.85), kind=kOutput, calls=%fused_computation.28 | convolution fusion | flops 1074397184 | bytes 7864320 | tf_op jit(solution)/shard_map/dot_general | solution.py:249
  347.2 6.7 %collective-permute-done.8 = bf16[256,1024]{1,0:T(8,128)(2,1)S(1)} collective-permute-done((bf16[256,1024]{1,0:T(8,128)(2,1)S(1)}, bf16[256,1024]{1,0:T(8,128)(2,1)S(1)}, u32[]{:S(2)}, u32[]{:S(2)}) %collective-permute-start.8) | collective-permute-done | bytes 524320 | tf_op jit(solution)/shard_map/ppermute | solution.py:263
  357.3 6.0 %gather_fusion.1 = bf16[512,256]{1,0:T(8,128)(2,1)S(1)} fusion(bf16[16384,256]{1,0:T(8,128)(2,1)} %get-tuple-element.636, s32[1024]{0:T(1024)S(1)} %get-tuple-element.434), kind=kCustom, calls=%fused_computation.1.clone | custom fusion | bytes 526336 | tf_op jit(solution)/shard_map/jit(_take)/gather | solution.py:245
  363.4 6.1 %gather_fusion = bf16[512,256]{1,0:T(8,128)(2,1)S(1)} fusion(bf16[16384,256]{1,0:T(8,128)(2,1)} %get-tuple-element.658, s32[1024]{0:T(1024)S(1)} %get-tuple-element.435), kind=kCustom, calls=%fused_computation.clone | custom fusion | bytes 526336 | tf_op jit(solution)/shard_map/jit(_take)/gather | solution.py:244
  (192 shorter events, 60.7 us)
Async XLA Ops:
  7.2 35.8 %all-gather.8.cloned.1.call-start = ((), (), s32[]{:S(2)}) async-start(), calls=%async_computation.1 | async-start | bytes 1310720 | tf_op jit(solution)/shard_map/all_gather | solution.py:114
  17.7 105.8 %all-gather.6.cloned.1.call-start = ((), (), s32[]{:S(2)}) async-start(), calls=%async_computation | async-start | bytes 7667712 | tf_op jit(solution)/shard_map/all_gather | solution.py:98
  42.8 92.1 %copy-start.8 = (s32[64]{0:T(128)S(1)}, s32[64]{0:T(128)}, u32[]{:S(2)}) copy-start(s32[64]{0:T(128)} %param.27) | copy-start | bytes 772
  42.8 92.4 %copy-start.12 = (s32[64]{0:T(128)S(1)}, s32[64]{0:T(128)}, u32[]{:S(2)}) copy-start(s32[64]{0:T(128)} %param.31) | copy-start | bytes 772
  42.8 93.1 %copy-start.9 = (s32[4,2]{0,1:T(2,128)S(1)}, s32[4,2]{0,1:T(2,128)}, u32[]{:S(2)}) copy-start(s32[4,2]{0,1:T(2,128)} %param.29) | copy-start | bytes 100
  42.8 94.5 %copy-start.6 = (s32[256]{0:T(256)S(1)}, s32[256]{0:T(256)}, u32[]{:S(2)}) copy-start(s32[256]{0:T(256)} %param.28) | copy-start | bytes 3076
  42.9 132.4 %all-gather.10.cloned.1.call-start = ((), (), s32[]{:S(2)}) async-start(), calls=%async_computation.2 | async-start | bytes 2359296 | tf_op jit(solution)/shard_map/all_gather | solution.py:49
  127.2 11.4 %copy-start.4 = (f32[256,1024]{1,0:T(8,128)}, f32[256,1024]{1,0:T(8,128)S(1)}, u32[]{:S(2)}) copy-start(f32[256,1024]{1,0:T(8,128)S(1)} %fusion.12) | copy-start | bytes 3145732
  127.3 11.9 %copy-start.11 = (f32[128]{0:T(128)S(1)}, f32[128]{0:T(128)}, u32[]{:S(2)}) copy-start(f32[128]{0:T(128)} %param.25) | copy-start | bytes 1540
  134.8 73.2 %all-gather.12.cloned.1.call-start = ((), (), s32[]{:S(2)}) async-start(), calls=%async_computation.3 | async-start | bytes 1310720 | tf_op jit(solution)/shard_map/all_gather | solution.py:43
  139.2 71.0 %copy-start.7 = (bf16[32,512]{1,0:T(8,128)(2,1)S(1)}, bf16[32,512]{1,0:T(8,128)(2,1)}, u32[]{:S(2)}) copy-start(bf16[32,512]{1,0:T(8,128)(2,1)} %param.23) | copy-start | bytes 98308
  182.5 135.3 %all-gather.14.cloned.1.call-start = ((), (), s32[]{:S(2)}) async-start(), calls=%async_computation.4 | async-start | bytes 9437184 | tf_op jit(solution)/shard_map/all_gather | solution.py:43
  208.1 73.8 %collective-permute-start.1 = (bf16[4096,256]{1,0:T(8,128)(2,1)}, bf16[4096,256]{1,0:T(8,128)(2,1)S(1)}, u32[]{:S(2)}, u32[]{:S(2)}) collective-permute-start(bf16[4096,256]{1,0:T(8,128)(2,1)} %all-gather.10.cloned.1.call-done), channel_id=1, source_target_pairs={{0,8},{8,16},{16,24},{24,0},{1,9},{9,17},{17,25},{25,1},{2,10},{10... | collective-permute-start | bytes 6291464 | tf_op jit(solution)/shard_map/ppermute | solution.py:56
  209.6 75.2 %collective-permute-start = (bf16[4096,256]{1,0:T(8,128)(2,1)}, bf16[4096,256]{1,0:T(8,128)(2,1)}, u32[]{:S(2)}, u32[]{:S(2)}) collective-permute-start(bf16[4096,256]{1,0:T(8,128)(2,1)} %all-gather.10.cloned.1.call-done), channel_id=1, source_target_pairs={{0,24},{8,0},{16,8},{24,16},{1,25},{9,1},{17,9},{25,17},{2,26},{10... | collective-permute-start | bytes 6291464 | tf_op jit(solution)/shard_map/ppermute | solution.py:57
  244.2 21.7 %collective-permute-start.5 = (bf16[512,512]{1,0:T(8,128)(2,1)S(1)}, bf16[512,512]{1,0:T(8,128)(2,1)S(1)}, u32[]{:S(2)}, u32[]{:S(2)}) collective-permute-start(bf16[512,512]{1,0:T(8,128)(2,1)S(1)} %all_gather.43), channel_id=1, source_target_pairs={{0,8},{8,16},{16,24},{24,0},{1,9},{9,17},{17,25},{25,1},{2,10},{10... | collective-permute-start | bytes 1572872 | tf_op jit(solution)/shard_map/ppermute | solution.py:56
  245.6 22.7 %collective-permute-start.4 = (bf16[512,512]{1,0:T(8,128)(2,1)S(1)}, bf16[512,512]{1,0:T(8,128)(2,1)}, u32[]{:S(2)}, u32[]{:S(2)}) collective-permute-start(bf16[512,512]{1,0:T(8,128)(2,1)S(1)} %all_gather.43), channel_id=1, source_target_pairs={{0,24},{8,0},{16,8},{24,16},{1,25},{9,1},{17,9},{25,17},{2,26},{10... | collective-permute-start | bytes 1572872 | tf_op jit(solution)/shard_map/ppermute | solution.py:57
  266.6 7.7 %collective-permute-start.6 = (bf16[256,512]{1,0:T(8,128)(2,1)}, bf16[256,512]{1,0:T(8,128)(2,1)}, u32[]{:S(2)}, u32[]{:S(2)}) collective-permute-start(bf16[256,512]{1,0:T(8,128)(2,1)} %slice.83), channel_id=1, source_target_pairs={{0,8},{8,16},{16,24},{24,0},{1,9},{9,17},{17,25},{25,1},{2,10},{10... | collective-permute-start | bytes 786440 | tf_op jit(solution)/shard_map/ppermute | solution.py:59
  270.0 6.7 %collective-permute-start.7 = (bf16[256,512]{1,0:T(8,128)(2,1)}, bf16[256,512]{1,0:T(8,128)(2,1)}, u32[]{:S(2)}, u32[]{:S(2)}) collective-permute-start(bf16[256,512]{1,0:T(8,128)(2,1)} %slice.84), channel_id=1, source_target_pairs={{0,24},{8,0},{16,8},{24,16},{1,25},{9,1},{17,9},{25,17},{2,26},{10... | collective-permute-start | bytes 786440 | tf_op jit(solution)/shard_map/ppermute | solution.py:60
  283.1 22.4 %collective-permute-start.2 = (bf16[2048,256]{1,0:T(8,128)(2,1)}, bf16[2048,256]{1,0:T(8,128)(2,1)}, u32[]{:S(2)}, u32[]{:S(2)}) collective-permute-start(bf16[2048,256]{1,0:T(8,128)(2,1)} %slice.81), channel_id=1, source_target_pairs={{0,8},{8,16},{16,24},{24,0},{1,9},{9,17},{17,25},{25,1},{2,10},{10... | collective-permute-start | bytes 3145736 | tf_op jit(solution)/shard_map/ppermute | solution.py:59
  287.2 23.2 %collective-permute-start.3 = (bf16[2048,256]{1,0:T(8,128)(2,1)}, bf16[2048,256]{1,0:T(8,128)(2,1)}, u32[]{:S(2)}, u32[]{:S(2)}) collective-permute-start(bf16[2048,256]{1,0:T(8,128)(2,1)} %slice.82), channel_id=1, source_target_pairs={{0,24},{8,0},{16,8},{24,16},{1,25},{9,1},{17,9},{25,17},{2,26},{10... | collective-permute-start | bytes 3145736 | tf_op jit(solution)/shard_map/ppermute | solution.py:60
  291.6 20.4 %copy-start.1 = (bf16[4096,256]{1,0:T(8,128)(2,1)S(1)}, bf16[4096,256]{1,0:T(8,128)(2,1)}, u32[]{:S(2)}) copy-start(bf16[4096,256]{1,0:T(8,128)(2,1)} %copy-done) | copy-start | bytes 6291460
  291.6 20.4 %copy-start.5 = (bf16[4096,256]{1,0:T(8,128)(2,1)S(1)}, bf16[4096,256]{1,0:T(8,128)(2,1)}, u32[]{:S(2)}) copy-start(bf16[4096,256]{1,0:T(8,128)(2,1)} %all-gather.10.cloned.1.call-done) | copy-start | bytes 6291460
  344.3 9.6 %collective-permute-start.8 = (bf16[256,1024]{1,0:T(8,128)(2,1)S(1)}, bf16[256,1024]{1,0:T(8,128)(2,1)S(1)}, u32[]{:S(2)}, u32[]{:S(2)}) collective-permute-start(bf16[256,1024]{1,0:T(8,128)(2,1)S(1)} %dynamic-slice_convert_fusion), channel_id=1, source_target_pairs={{0,2},{1,3},{2,0},{3,1},{4,6},{5,7},{6,4},{7,5},{8,10},{9,11},{10,... | collective-permute-start | bytes 1572872 | tf_op jit(solution)/shard_map/ppermute | solution.py:263
  355.3 15.2 %collective-permute-start.9 = (f32[256,512]{1,0:T(8,128)S(1)}, f32[256,512]{1,0:T(8,128)S(1)}, u32[]{:S(2)}, u32[]{:S(2)}) collective-permute-start(f32[256,512]{1,0:T(8,128)S(1)} %constant_dynamic-slice_fusion.2), channel_id=1, source_target_pairs={{0,1},{1,0},{2,3},{3,2},{4,5},{5,4},{6,7},{7,6},{8,9},{9,8},{10,11... | collective-permute-start | bytes 1572872 | tf_op jit(solution)/shard_map/ppermute | solution.py:269
  (6 other events, 17.9 us)
Sparse Core Ops, SparseCore 0:
  17.8 25.0 all-gather.7
  44.7 78.7 all-gather.5
  135.0 40.1 all-gather.9
  182.6 25.4 all-gather.11
  209.7 97.1 all-gather.13

commit v5 on v4

--- a/solution.py
+++ b/solution.py
@@ -1,6 +1,8 @@
 import jax
 import jax.numpy as jnp
 from jax import lax
+from jax.experimental import pallas as pl
+from jax.experimental.pallas import tpu as pltpu
 from jax.sharding import Mesh
 from jax.sharding import PartitionSpec as P
 
@@ -36,6 +38,70 @@
 
 
 SEQ_PARTS = ("z", "y", "xh")
+MESH_ID = pl.DeviceIdType.MESH
+AXES = SEQ_PARTS + ("mdl",)
+
+
+def _ring_kernel(x_ref, out_ref, send_sem, recv_sem, local_sem):
+    ny = 4
+    me = {name: lax.axis_index(name) for name in AXES}
+    my_y = me["y"]
+
+    def dev(yy):
+        return tuple(yy if name == "y" else me[name] for name in AXES)
+
+    plus = dev(lax.rem(my_y + 1, ny))
+    minus = dev(lax.rem(my_y + ny - 1, ny))
+    barrier = pltpu.get_barrier_semaphore()
+    for d in (plus, minus):
+        pl.semaphore_signal(barrier, inc=1, device_id=d, device_id_type=MESH_ID)
+    pl.semaphore_wait(barrier, 2)
+
+    rows = x_ref.shape[0]
+    half = rows // 2
+    to_minus = pltpu.make_async_remote_copy(
+        src_ref=x_ref, dst_ref=out_ref.at[1], send_sem=send_sem.at[0], recv_sem=recv_sem.at[0],
+        device_id=minus, device_id_type=MESH_ID)
+    to_plus = pltpu.make_async_remote_copy(
+        src_ref=x_ref, dst_ref=out_ref.at[3], send_sem=send_sem.at[1], recv_sem=recv_sem.at[1],
+        device_id=plus, device_id_type=MESH_ID)
+    own = pltpu.make_async_copy(x_ref, out_ref.at[0], local_sem.at[0])
+    to_minus.start()
+    to_plus.start()
+    own.start()
+    to_minus.wait_recv()
+    on_minus = pltpu.make_async_remote_copy(
+        src_ref=out_ref.at[1, pl.ds(0, half)], dst_ref=out_ref.at[2, pl.ds(0, half)],
+        send_sem=send_sem.at[2], recv_sem=recv_sem.at[2], device_id=minus, device_id_type=MESH_ID)
+    on_minus.start()
+    to_plus.wait_recv()
+    on_plus = pltpu.make_async_remote_copy(
+        src_ref=out_ref.at[3, pl.ds(half, rows - half)], dst_ref=out_ref.at[2, pl.ds(half, rows - half)],
+        send_sem=send_sem.at[3], recv_sem=recv_sem.at[3], device_id=plus, device_id_type=MESH_ID)
+    on_plus.start()
+    to_minus.wait_send()
+    to_plus.wait_send()
+    own.wait()
+    on_minus.wait_send()
+    on_plus.wait_send()
+    on_minus.wait_recv()
+    on_plus.wait_recv()
+
+
+def ring_y_kernel(x, collective_id):
+    rows, width = x.shape
+    return pl.pallas_call(
+        _ring_kernel,
+        out_shape=jax.ShapeDtypeStruct((4, rows, width), x.dtype),
+        in_specs=[pl.BlockSpec(memory_space=pl.ANY)],
+        out_specs=pl.BlockSpec(memory_space=pl.ANY),
+        scratch_shapes=[
+            pltpu.SemaphoreType.DMA((4,)),
+            pltpu.SemaphoreType.DMA((4,)),
+            pltpu.SemaphoreType.DMA((1,)),
+        ],
+        compiler_params=pltpu.CompilerParams(collective_id=collective_id, has_side_effects=True),
+    )(x)
 
 
 def gather_seq(x):
@@ -94,7 +160,7 @@
     packed = lax.all_gather(packed, "xh", axis=0, tiled=True)
     packed = lax.all_gather(packed, "y", axis=0, tiled=True)
     packed, gate_in = lax.optimization_barrier((packed, w_gate))
-    gate_ring = ring_y(gather_xh_z(gate_in))
+    gate_ring = ring_y_kernel(gather_xh_z(gate_in), 1)
     gathered = lax.all_gather(packed, "z", axis=0, tiled=True)
     proj_cols = q_cols + 2 * kv_cols
     w_proj = gathered[:, :proj_cols]
@@ -150,11 +216,18 @@
         .reshape(local_rows, kv_cols)
     )
     values_flat = values_raw.astype(jnp.bfloat16)
-    v_part = gather_xh_z(values_flat)
-    k_rot, v_part = lax.optimization_barrier((k_rot, v_part))
-    v_ring = ring_y(v_part)
-    k_all = gather_seq(k_rot)
-    v_ring = v_ring.reshape(-1, kv_cols)
+    kv_pair = lax.all_gather(jnp.concatenate([k_rot, values_flat], axis=1), "xh", axis=0, tiled=True)
+    v_part = lax.all_gather(kv_pair[:, kv_cols:], "z", axis=0, tiled=True)
+    k_part = ring_y_kernel(kv_pair[:, :kv_cols], 2).reshape(-1, kv_cols)
+    k_part, v_part = lax.optimization_barrier((k_part, v_part))
+    k_all = lax.all_gather(k_part, "z", axis=0, tiled=True)
+    v_ring = ring_y_kernel(v_part, 3).reshape(-1, kv_cols)
+
+    def k_row_of(token):
+        block = token // local_rows
+        rel = (block // 2 % 4 - my_y) % 4
+        place = ((block // 8) * 4 + rel) * 2 + block % 2
+        return place * local_rows + token % local_rows
 
     def v_row_of(token):
         block = token // local_rows
@@ -193,7 +266,7 @@
         old_top, old_totals, old_summed = loop_state
         block = block_list[i]
         offset = block * KEY_BLOCK
-        keys_part = lax.dynamic_slice_in_dim(k_all, offset, KEY_BLOCK, 0).reshape(
+        keys_part = lax.dynamic_slice_in_dim(k_all, k_row_of(offset), KEY_BLOCK, 0).reshape(
             KEY_BLOCK, kv_heads, HEAD_SIZE
         )
         values_part = lax.dynamic_slice_in_dim(v_ring, v_row_of(offset), KEY_BLOCK, 0).reshape(
@@ -241,7 +314,7 @@
     in_window = ((wanted < stream) & (offsets < my_length))[:, None]
     source = jnp.clip(wanted, 0, stream - 1)
     zero = jnp.zeros((), jnp.bfloat16)
-    cache_k = jnp.where(in_window, jnp.take(k_all, source, axis=0), zero)
+    cache_k = jnp.where(in_window, jnp.take(k_all, k_row_of(source), axis=0), zero)
     cache_v = jnp.where(in_window, jnp.take(v_ring, v_row_of(source), axis=0), zero)
 
     attended = (summed / totals[..., None]).reshape(local_rows, query_heads * HEAD_SIZE)

time: 384 us -> 391 us (1.018)
  the two profiles are of different devices: /device:TPU:72 before, /device:TPU:113 now
where the time goes in v5:
time: 391 us; the launch traced here: 390 us
  waiting for transfers between devices  118 us (30%)
  Pallas kernels  115 us (29%)
  blocking collectives  59.6 us (15%)
  local copies, waits for them, and re-layouts  31.4 us (8%)
  other arithmetic  23.6 us (6%)
  between operations  17 us (4%)
  matrix products  12.5 us (3%)
  loops' own time  8.11 us (2%)
  starting transfers between devices  4.4 us (1%)
    pallas_call x3, Pallas kernels, ring_y_kernel(): pl.pallas_call(_ring_kernel, out_shape=jax.ShapeDtypeStruct((4, rows, wid...  115 us
    all_gather x1, waiting for transfers between devices, body(): gathered = lax.all_gather(packed, 'z', axis=0, tiled=True)  81.3 us
    all_gather x1, waiting for transfers between devices, body(): v_part = lax.all_gather(kv_pair[:, kv_cols:], 'z', axis=0, tiled=True)  24.7 us
    all_gather x1, blocking collectives, gather_xh_z(): return lax.all_gather(x, 'z', axis=0, tiled=True)  23.3 us
    all_gather x1, blocking collectives, body(): packed = lax.all_gather(packed, 'y', axis=0, tiled=True)  10.5 us
    all_gather x1, blocking collectives, body(): lax.all_gather(jnp.concatenate([k_rot, values_flat], axis=1), 'xh', axis=...  9.36 us
    ppermute x1, waiting for transfers between devices, body(): lax.ppermute(theirs.astype(jnp.bfloat16), 'mdl', [(m, m ^ 2) for m in ran...  9.22 us
    another operation x1, loops' own time, body(): top_now, totals, summed = lax.fori_loop(0, n_needed, key_block, start_state)  8.11 us
  transfers between devices with their start and end apart: 6, of which 4 were waited for; matrix products, arithmetic and copies ran while one was open for 8% of the time, Pallas kernels for 30%

profile of v5, /device:TPU:113, one launch (start us, length us, event | category | flops | bytes accessed | tf_op | source)
XLA Modules:
  0.0 389.7 jit_solution(17566463728110971485)
XLA Ops:
  8.3 5.7 %psum.7 = f32[256]{0:T(256)S(1)} all-reduce(f32[256]{0:T(256)S(1)} %fusion.23), channel_id=1, replica_groups=mesh['z'=8,'y'=4,'xh'=2,'mdl'=4] {'mdl'}, use_global_device_ids=true, to_apply=%region_12.13 | all-reduce | flops 256 | bytes 2048 | tf_op jit(solution)/shard_map/psum | solution.py:174
  14.7 1.8 fusion.25
  20.3 5.7 %all_gather.27 = bf16[64,1664]{1,0:T(8,128)(2,1)S(1)} all-gather(bf16[32,1664]{1,0:T(8,128)(2,1)S(1)} %constant_dynamic-update-slice_fusion), channel_id=1, replica_groups=mesh['z'=8,'y'=4,'xh'=2,'mdl'=4] {'xh'}, dimensions={0}, use_global_device_ids=true | all-gather | bytes 319488 | tf_op jit(solution)/shard_map/all_gather | solution.py:160
  26.1 10.5 %all_gather.28 = bf16[256,1664]{1,0:T(8,128)(2,1)} all-gather(bf16[64,1664]{1,0:T(8,128)(2,1)S(1)} %all_gather.27), channel_id=1, replica_groups=mesh['z'=8,'y'=4,'xh'=2,'mdl'=4] {'y'}, dimensions={0}, use_global_device_ids=true | all-gather | bytes 1064960 | tf_op jit(solution)/shard_map/all_gather | solution.py:161
  37.8 1.3 fusion.46
  40.4 2.5 all-gather.7.cloned.1.call-done
  43.0 81.3 %all-gather.5.cloned.1.call-done = bf16[2048,1664]{1,0:T(8,128)(2,1)} async-done(((bf16[256,1664]{1,0:T(8,128)(2,1)}), bf16[2048,1664]{1,0:T(8,128)(2,1)}) %all-gather.5.cloned.1.call-update) | async-done | bytes 6815760 | tf_op jit(solution)/shard_map/all_gather | solution.py:164
  124.3 3.8 fusion.12
  129.9 9.4 %all_gather.31 = bf16[512,512]{1,0:T(8,128)(2,1)S(1)} all-gather(bf16[256,512]{1,0:T(8,128)(2,1)S(1)} %pad_maximum_fusion), channel_id=1, replica_groups=mesh['z'=8,'y'=4,'xh'=2,'mdl'=4] {'xh'}, dimensions={0}, use_global_device_ids=true | all-gather | bytes 786432 | tf_op jit(solution)/shard_map/all_gather | solution.py:219
  140.1 11.5 %shard_map.157 = bf16[4,512,256]{2,1,0:T(8,128)(2,1)} custom-call(bf16[512,256]{1,0:T(8,128)(2,1)} %get-tuple-element.420.x_ref), custom_call_target="tpu_custom_call" | custom-call | tf_op jit(solution)/shard_map/pallas_call | solution.py:93
  151.6 24.7 %all-gather.9.cloned.1.call-done.x_ref = bf16[4096,256]{1,0:T(8,128)(2,1)} async-done(((bf16[512,256]{1,0:T(8,128)(2,1)}), bf16[4096,256]{1,0:T(8,128)(2,1)}) %all-gather.9.cloned.1.call-update) | async-done | bytes 2097168 | tf_op jit(solution)/shard_map/all_gather | solution.py:220
  181.1 4.9 %all_gather.34 = bf16[64,512]{1,0:T(8,128)(2,1)S(1)} all-gather(bf16[32,512]{1,0:T(8,128)(2,1)S(1)} %copy-done.4), channel_id=1, replica_groups=mesh['z'=8,'y'=4,'xh'=2,'mdl'=4] {'xh'}, dimensions={0}, use_global_device_ids=true | all-gather | bytes 98304 | tf_op jit(solution)/shard_map/all_gather | solution.py:114
  186.1 23.3 %all_gather.35.x_ref = bf16[512,512]{1,0:T(8,128)(2,1)} all-gather(bf16[64,512]{1,0:T(8,128)(2,1)S(1)} %all_gather.34), channel_id=1, replica_groups=mesh['z'=8,'y'=4,'xh'=2,'mdl'=4] {'z'}, dimensions={0}, use_global_device_ids=true | all-gather | bytes 589824 | tf_op jit(solution)/shard_map/all_gather | solution.py:115
  209.3 31.8 %shard_map.159 = bf16[4,512,512]{2,1,0:T(8,128)(2,1)} custom-call(bf16[512,512]{1,0:T(8,128)(2,1)} %all_gather.35.x_ref), custom_call_target="tpu_custom_call" | custom-call | tf_op jit(solution)/shard_map/pallas_call | solution.py:93
  247.1 72.1 %shard_map.158 = bf16[4,4096,256]{2,1,0:T(8,128)(2,1)} custom-call(bf16[4096,256]{1,0:T(8,128)(2,1)} %all-gather.9.cloned.1.call-done.x_ref), custom_call_target="tpu_custom_call" | custom-call | tf_op jit(solution)/shard_map/pallas_call | solution.py:93
  319.3 24.3 %while.18 = (s32[]{:T(128)}, f32[256,2,2]{0,2,1:T(2,128)S(1)}, f32[256,2,2]{0,2,1:T(2,128)S(1)}, f32[256,2,2,128]{0,3,2,1:T(8,128)S(1)}, s32[]{:T(128)}, /*index...) while((s32[]{:T(128)}, f32[256,2,2]{0,2,1:T(2,128)S(1)}, ...), condition=%wide.region_21.22_spmd.clone, body=%wide.region_17.21_spmd.clone.sunk | while | flops 137415776 | bytes 6106619 | solution.py:307
  343.9 1.3 copy-done.1
  345.2 4.7 %fusion.14 = f32[256,2048]{1,0:T(8,128)} fusion(bf16[2048,1664]{1,0:T(8,128)(2,1)} %all-gather.5.cloned.1.call-done, f32[256,512]{1,0:T(8,128)S(1)} %copy.80, bf16[256,2048]{0,1:T(8,128)(2,1)} %bitcast.80, bf16[2048,512]{1,0:T(8,128)(2,1)S(1)} %bitcast.76), kind=kOutput, calls=%fused_computation.27 | convolution fusion | flops 1074397184 | bytes 7864320 | tf_op jit(solution)/shard_map/dot_general | solution.py:322
  351.3 1.5 collective-permute-start
  353.9 9.2 %collective-permute-done = bf16[256,1024]{1,0:T(8,128)(2,1)S(1)} collective-permute-done((bf16[256,1024]{1,0:T(8,128)(2,1)S(1)}, bf16[256,1024]{1,0:T(8,128)(2,1)S(1)}, u32[]{:S(2)}, u32[]{:S(2)}) %collective-permute-start) | collective-permute-done | bytes 524320 | tf_op jit(solution)/shard_map/ppermute | solution.py:336
  363.2 1.4 convert_add_fusion
  364.6 2.8 collective-permute-start.1
  369.2 6.0 %gather_fusion.1 = bf16[512,256]{1,0:T(8,128)(2,1)S(1)} fusion(bf16[16384,256]{1,0:T(8,128)(2,1)} %get-tuple-element.637, s32[1024]{0:T(1024)S(1)} %get-tuple-element.436), kind=kCustom, calls=%fused_computation.1.clone | custom fusion | bytes 526336 | tf_op jit(solution)/shard_map/jit(_take)/gather | solution.py:318
  375.2 6.1 %gather_fusion = bf16[512,256]{1,0:T(8,128)(2,1)S(1)} fusion(bf16[16384,256]{1,0:T(8,128)(2,1)} %get-tuple-element.650, s32[1024]{0:T(1024)S(1)} %get-tuple-element.437), kind=kCustom, calls=%fused_computation.clone | custom fusion | bytes 526336 | tf_op jit(solution)/shard_map/jit(_take)/gather | solution.py:317
  (176 shorter events, 41.4 us)
Async XLA Ops:
  7.2 29.5 %copy-start.5 = (s32[64]{0:T(128)S(1)}, s32[64]{0:T(128)}, u32[]{:S(2)}) copy-start(s32[64]{0:T(128)} %param.27) | copy-start | bytes 772
  7.2 29.9 %copy-start.9 = (s32[64]{0:T(128)S(1)}, s32[64]{0:T(128)}, u32[]{:S(2)}) copy-start(s32[64]{0:T(128)} %param.31) | copy-start | bytes 772
  7.2 30.5 %copy-start.6 = (s32[4,2]{0,1:T(2,128)S(1)}, s32[4,2]{0,1:T(2,128)}, u32[]{:S(2)}) copy-start(s32[4,2]{0,1:T(2,128)} %param.29) | copy-start | bytes 100
  7.2 31.9 %copy-start.3 = (s32[256]{0:T(256)S(1)}, s32[256]{0:T(256)}, u32[]{:S(2)}) copy-start(s32[256]{0:T(256)} %param.28) | copy-start | bytes 3076
  7.2 35.8 %all-gather.7.cloned.1.call-start = ((), (), s32[]{:S(2)}) async-start(), calls=%async_computation.1 | async-start | bytes 1310720 | tf_op jit(solution)/shard_map/all_gather | solution.py:180
  16.5 107.8 %all-gather.5.cloned.1.call-start = ((), (), s32[]{:S(2)}) async-start(), calls=%async_computation | async-start | bytes 7667712 | tf_op jit(solution)/shard_map/all_gather | solution.py:164
  36.6 139.6 %all-gather.9.cloned.1.call-start = ((), (), s32[]{:S(2)}) async-start(), calls=%async_computation.2 | async-start | bytes 2359296 | tf_op jit(solution)/shard_map/all_gather | solution.py:220
  40.4 88.2 %copy-start.8 = (f32[128]{0:T(128)S(1)}, f32[128]{0:T(128)}, u32[]{:S(2)}) copy-start(f32[128]{0:T(128)} %param.25) | copy-start | bytes 1540
  139.2 41.9 %copy-start.4 = (bf16[32,512]{1,0:T(8,128)(2,1)S(1)}, bf16[32,512]{1,0:T(8,128)(2,1)}, u32[]{:S(2)}) copy-start(bf16[32,512]{1,0:T(8,128)(2,1)} %param.23) | copy-start | bytes 98308
  140.1 179.1 %all-gather.11.cloned.1.call-start = ((), (), s32[]{:S(2)}) async-start(), calls=%async_computation.3 | async-start | bytes 9437184 | tf_op jit(solution)/shard_map/all_gather | solution.py:223
  176.3 66.1 %copy-start.2 = (bf16[256,2048]{1,0:T(8,128)(2,1)S(1)}, bf16[256,2048]{1,0:T(8,128)(2,1)}, u32[]{:S(2)}) copy-start(bf16[256,2048]{1,0:T(8,128)(2,1)} %all-gather.7.cloned.1.call-done) | copy-start | bytes 3145732
  243.4 1.7 copy-start.7
  245.4 1.0 slice-start
  343.6 1.6 copy-start.1
  351.3 11.9 %collective-permute-start = (bf16[256,1024]{1,0:T(8,128)(2,1)S(1)}, bf16[256,1024]{1,0:T(8,128)(2,1)S(1)}, u32[]{:S(2)}, u32[]{:S(2)}) collective-permute-start(bf16[256,1024]{1,0:T(8,128)(2,1)S(1)} %dynamic-slice_convert_fusion), channel_id=1, source_target_pairs={{0,2},{1,3},{2,0},{3,1},{4,6},{5,7},{6,4},{7,5},{8,10},{9,11},{10,... | collective-permute-start | bytes 1572872 | tf_op jit(solution)/shard_map/ppermute | solution.py:336
  364.6 17.8 %collective-permute-start.1 = (f32[256,512]{1,0:T(8,128)S(1)}, f32[256,512]{1,0:T(8,128)S(1)}, u32[]{:S(2)}, u32[]{:S(2)}) collective-permute-start(f32[256,512]{1,0:T(8,128)S(1)} %constant_dynamic-slice_fusion.2), channel_id=1, source_target_pairs={{0,1},{1,0},{2,3},{3,2},{4,5},{5,4},{6,7},{7,6},{8,9},{9,8},{10,11... | collective-permute-start | bytes 1572872 | tf_op jit(solution)/shard_map/ppermute | solution.py:342
  375.2 7.2 %copy-start = (bf16[256,512]{1,0:T(8,128)(2,1)S(1)}, bf16[256,512]{1,0:T(8,128)(2,1)}, u32[]{:S(2)}) copy-start(bf16[256,512]{1,0:T(8,128)(2,1)} %param.18) | copy-start | bytes 786436
Sparse Core Ops, SparseCore 0:
  16.6 26.2 all-gather.6
  44.8 79.4 all-gather.4
  140.2 36.0 all-gather.8
  177.9 101.2 all-gather.10

commit v6 on v5

--- a/solution.py
+++ b/solution.py
@@ -128,6 +128,23 @@
     return jnp.stack([x, from_plus, opposite, from_minus])
 
 
+def gather_mdl(x):
+    mdl_index = lax.axis_index("mdl")
+    n_mdl = lax.axis_size("mdl")
+    other = lax.ppermute(x, "mdl", [(m, m ^ 1) for m in range(n_mdl)])
+    pair = jnp.where(
+        mdl_index % 2 == 0,
+        jnp.concatenate([x, other], axis=1),
+        jnp.concatenate([other, x], axis=1),
+    )
+    other = lax.ppermute(pair, "mdl", [(m, m ^ 2) for m in range(n_mdl)])
+    return jnp.where(
+        mdl_index // 2 == 0,
+        jnp.concatenate([pair, other], axis=1),
+        jnp.concatenate([other, pair], axis=1),
+    )
+
+
 def body(
     tokens,
     norm_gain,
@@ -162,6 +179,7 @@
     packed, gate_in = lax.optimization_barrier((packed, w_gate))
     gate_ring = ring_y_kernel(gather_xh_z(gate_in), 1)
     gathered = lax.all_gather(packed, "z", axis=0, tiled=True)
+    gathered, gate_ring = lax.optimization_barrier((gathered, gate_ring))
     proj_cols = q_cols + 2 * kv_cols
     w_proj = gathered[:, :proj_cols]
     w_out_t = gathered[:, proj_cols : proj_cols + w_out.shape[0]]
@@ -177,7 +195,7 @@
         * lax.rsqrt(square_total / full_width + epsilon)[:, None]
         * norm_gain.astype(jnp.float32)
     )
-    normalized_input = lax.all_gather(scaled.astype(jnp.bfloat16), "mdl", axis=1, tiled=True)
+    normalized_input = gather_mdl(scaled.astype(jnp.bfloat16))
     projected = jnp.dot(normalized_input, w_proj, preferred_element_type=jnp.float32)
     query_rows = projected[:, :q_cols]
     unprojected_keys = projected[:, q_cols : q_cols + kv_cols]

time: 391 us -> 349 us (0.89)
  the two profiles are of different devices: /device:TPU:113 before, /device:TPU:72 now
where the time goes in v6:
time: 349 us; the launch traced here: 346 us
  Pallas kernels  129 us (37%)
  blocking collectives  75 us (21%)
  waiting for transfers between devices  53.3 us (15%)
  local copies, waits for them, and re-layouts  29 us (8%)
  other arithmetic  20.9 us (6%)
  between operations  16.9 us (5%)
  matrix products  11.4 us (3%)
  loops' own time  6.8 us (2%)
  starting transfers between devices  3.67 us (1%)
    pallas_call x3, Pallas kernels, ring_y_kernel(): pl.pallas_call(_ring_kernel, out_shape=jax.ShapeDtypeStruct((4, rows, wid...  129 us
    all_gather x1, blocking collectives, gather_xh_z(): return lax.all_gather(x, 'z', axis=0, tiled=True)  30.8 us
    all_gather x1, waiting for transfers between devices, body(): v_part = lax.all_gather(kv_pair[:, kv_cols:], 'z', axis=0, tiled=True)  27.4 us
    all_gather x1, waiting for transfers between devices, body(): gathered = lax.all_gather(packed, 'z', axis=0, tiled=True)  17.7 us
    all_gather x1, blocking collectives, body(): packed = lax.all_gather(packed, 'y', axis=0, tiled=True)  15.3 us
    all_gather x1, blocking collectives, body(): lax.all_gather(jnp.concatenate([k_rot, values_flat], axis=1), 'xh', axis=...  10.2 us
    ppermute x1, waiting for transfers between devices, body(): lax.ppermute(theirs.astype(jnp.bfloat16), 'mdl', [(m, m ^ 2) for m in ran...  8.07 us
  transfers between devices with their start and end apart: 7, of which 3 were waited for; matrix products, arithmetic and copies ran while one was open for 8% of the time, Pallas kernels for 37%

profile of v6, /device:TPU:72, one launch (start us, length us, event | category | flops | bytes accessed | tf_op | source)
XLA Modules:
  0.0 345.7 jit_solution(11099673734824797323)
XLA Ops:
  11.0 6.9 %all_gather.24 = bf16[64,1664]{1,0:T(8,128)(2,1)S(1)} all-gather(bf16[32,1664]{1,0:T(8,128)(2,1)S(1)} %constant_dynamic-update-slice_fusion), channel_id=1, replica_groups=mesh['z'=8,'y'=4,'xh'=2,'mdl'=4] {'xh'}, dimensions={0}, use_global_device_ids=true | all-gather | bytes 319488 | tf_op jit(solution)/shard_map/all_gather | solution.py:177
  17.9 15.3 %all_gather.25 = bf16[256,1664]{1,0:T(8,128)(2,1)} all-gather(bf16[64,1664]{1,0:T(8,128)(2,1)S(1)} %all_gather.24), channel_id=1, replica_groups=mesh['z'=8,'y'=4,'xh'=2,'mdl'=4] {'y'}, dimensions={0}, use_global_device_ids=true | all-gather | bytes 1064960 | tf_op jit(solution)/shard_map/all_gather | solution.py:178
  33.5 5.7 %psum.7 = f32[256]{0:T(256)S(1)} all-reduce(f32[256]{0:T(256)S(1)} %fusion.29), channel_id=1, replica_groups=mesh['z'=8,'y'=4,'xh'=2,'mdl'=4] {'mdl'}, use_global_device_ids=true, to_apply=%region_12.13 | all-reduce | flops 256 | bytes 2048 | tf_op jit(solution)/shard_map/psum | solution.py:192
  39.4 6.1 %all_gather.27 = bf16[64,512]{1,0:T(8,128)(2,1)S(1)} all-gather(bf16[32,512]{1,0:T(8,128)(2,1)S(1)} %copy-done.3), channel_id=1, replica_groups=mesh['z'=8,'y'=4,'xh'=2,'mdl'=4] {'xh'}, dimensions={0}, use_global_device_ids=true | all-gather | bytes 98304 | tf_op jit(solution)/shard_map/all_gather | solution.py:114
  45.5 30.8 %all_gather.28.x_ref = bf16[512,512]{1,0:T(8,128)(2,1)} all-gather(bf16[64,512]{1,0:T(8,128)(2,1)S(1)} %all_gather.27), channel_id=1, replica_groups=mesh['z'=8,'y'=4,'xh'=2,'mdl'=4] {'z'}, dimensions={0}, use_global_device_ids=true | all-gather | bytes 589824 | tf_op jit(solution)/shard_map/all_gather | solution.py:115
  76.4 17.9 %shard_map.157 = bf16[4,512,512]{2,1,0:T(8,128)(2,1)} custom-call(bf16[512,512]{1,0:T(8,128)(2,1)} %all_gather.28.x_ref), custom_call_target="tpu_custom_call" | custom-call | tf_op jit(solution)/shard_map/pallas_call | solution.py:93
  95.3 1.3 fusion.52
  96.9 1.8 collective-permute-start.1
  99.9 17.7 %all-gather.4.cloned.1.call-done = bf16[2048,1664]{1,0:T(8,128)(2,1)} async-done(((bf16[256,1664]{1,0:T(8,128)(2,1)}), bf16[2048,1664]{1,0:T(8,128)(2,1)}) %all-gather.4.cloned.1.call-update) | async-done | bytes 6815760 | tf_op jit(solution)/shard_map/all_gather | solution.py:181
  117.6 3.4 fusion.12
  122.9 10.2 %all_gather.29 = bf16[512,512]{1,0:T(8,128)(2,1)S(1)} all-gather(bf16[256,512]{1,0:T(8,128)(2,1)S(1)} %pad_maximum_fusion), channel_id=1, replica_groups=mesh['z'=8,'y'=4,'xh'=2,'mdl'=4] {'xh'}, dimensions={0}, use_global_device_ids=true | all-gather | bytes 786432 | tf_op jit(solution)/shard_map/all_gather | solution.py:237
  134.0 13.0 %shard_map.158 = bf16[4,512,256]{2,1,0:T(8,128)(2,1)} custom-call(bf16[512,256]{1,0:T(8,128)(2,1)} %get-tuple-element.424.x_ref), custom_call_target="tpu_custom_call" | custom-call | tf_op jit(solution)/shard_map/pallas_call | solution.py:93
  147.0 27.4 %all-gather.6.cloned.1.call-done.x_ref = bf16[4096,256]{1,0:T(8,128)(2,1)} async-done(((bf16[512,256]{1,0:T(8,128)(2,1)}), bf16[4096,256]{1,0:T(8,128)(2,1)}) %all-gather.6.cloned.1.call-update) | async-done | bytes 2097168 | tf_op jit(solution)/shard_map/all_gather | solution.py:238
  185.0 97.8 %shard_map.159 = bf16[4,4096,256]{2,1,0:T(8,128)(2,1)} custom-call(bf16[4096,256]{1,0:T(8,128)(2,1)} %all-gather.6.cloned.1.call-done.x_ref), custom_call_target="tpu_custom_call" | custom-call | tf_op jit(solution)/shard_map/pallas_call | solution.py:93
  283.0 19.8 %while.18 = (s32[]{:T(128)}, f32[256,2,2]{0,2,1:T(2,128)S(1)}, f32[256,2,2]{0,2,1:T(2,128)S(1)}, f32[256,2,2,128]{0,3,2,1:T(8,128)S(1)}, s32[]{:T(128)}, /*index...) while((s32[]{:T(128)}, f32[256,2,2]{0,2,1:T(2,128)S(1)}, ...), condition=%wide.region_21.22_spmd.clone, body=%wide.region_17.21_spmd.clone.sunk | while | flops 137415776 | bytes 6106619 | solution.py:325
  303.7 1.2 copy.88
  304.9 4.7 %fusion.14 = f32[256,2048]{1,0:T(8,128)} fusion(bf16[2048,1664]{1,0:T(8,128)(2,1)} %all-gather.4.cloned.1.call-done, f32[256,512]{1,0:T(8,128)S(1)} %copy.88, bf16[256,2048]{0,1:T(8,128)(2,1)} %bitcast.81, bf16[2048,512]{1,0:T(8,128)(2,1)S(1)} %bitcast.76), kind=kOutput, calls=%fused_computation.29 | convolution fusion | flops 1074397184 | bytes 7864320 | tf_op jit(solution)/shard_map/dot_general | solution.py:340
  309.7 1.3 dynamic-slice_convert_fusion
  311.0 1.6 collective-permute-start.2
  313.8 8.1 %collective-permute-done.2 = bf16[256,1024]{1,0:T(8,128)(2,1)S(1)} collective-permute-done((bf16[256,1024]{1,0:T(8,128)(2,1)S(1)}, bf16[256,1024]{1,0:T(8,128)(2,1)S(1)}, u32[]{:S(2)}, u32[]{:S(2)}) %collective-permute-start.2) | collective-permute-done | bytes 524320 | tf_op jit(solution)/shard_map/ppermute | solution.py:354
  321.8 1.4 convert_add_fusion
  323.3 1.2 fusion.45
  325.2 6.0 %gather_fusion.1 = bf16[512,256]{1,0:T(8,128)(2,1)S(1)} fusion(bf16[16384,256]{1,0:T(8,128)(2,1)} %get-tuple-element.640, s32[1024]{0:T(1024)S(1)} %get-tuple-element.440), kind=kCustom, calls=%fused_computation.1.clone | custom fusion | bytes 526336 | tf_op jit(solution)/shard_map/jit(_take)/gather | solution.py:336
  331.2 6.0 %gather_fusion = bf16[512,256]{1,0:T(8,128)(2,1)S(1)} fusion(bf16[16384,256]{1,0:T(8,128)(2,1)} %get-tuple-element.652, s32[1024]{0:T(1024)S(1)} %get-tuple-element.441), kind=kCustom, calls=%fused_computation.clone | custom fusion | bytes 526336 | tf_op jit(solution)/shard_map/jit(_take)/gather | solution.py:335
  (168 shorter events, 35.1 us)
Async XLA Ops:
  7.2 32.2 %copy-start.3 = (bf16[32,512]{1,0:T(8,128)(2,1)S(1)}, bf16[32,512]{1,0:T(8,128)(2,1)}, u32[]{:S(2)}) copy-start(bf16[32,512]{1,0:T(8,128)(2,1)} %param.23) | copy-start | bytes 98308
  7.2 26.1 %copy-start.5 = (bf16[512]{0:T(512)(128)(2,1)S(1)}, bf16[512]{0:T(512)(128)(2,1)}, u32[]{:S(2)}) copy-start(bf16[512]{0:T(512)(128)(2,1)} %param.19) | copy-start | bytes 3076
  7.2 26.1 %copy-start = (bf16[256,512]{1,0:T(8,128)(2,1)S(1)}, bf16[256,512]{1,0:T(8,128)(2,1)}, u32[]{:S(2)}) copy-start(bf16[256,512]{1,0:T(8,128)(2,1)} %param.18) | copy-start | bytes 786436
  7.2 110.4 %all-gather.4.cloned.1.call-start = ((), (), s32[]{:S(2)}) async-start(), calls=%async_computation | async-start | bytes 7667712 | tf_op jit(solution)/shard_map/all_gather | solution.py:181
  33.2 61.1 %copy-start.4 = (s32[64]{0:T(128)S(1)}, s32[64]{0:T(128)}, u32[]{:S(2)}) copy-start(s32[64]{0:T(128)} %param.27) | copy-start | bytes 772
  33.2 141.2 %all-gather.6.cloned.1.call-start = ((), (), s32[]{:S(2)}) async-start(), calls=%async_computation.1 | async-start | bytes 2359296 | tf_op jit(solution)/shard_map/all_gather | solution.py:238
  33.3 61.3 %copy-start.9 = (s32[64]{0:T(128)S(1)}, s32[64]{0:T(128)}, u32[]{:S(2)}) copy-start(s32[64]{0:T(128)} %param.31) | copy-start | bytes 772
  33.3 61.9 %copy-start.6 = (s32[4,2]{0,1:T(2,128)S(1)}, s32[4,2]{0,1:T(2,128)}, u32[]{:S(2)}) copy-start(s32[4,2]{0,1:T(2,128)} %param.29) | copy-start | bytes 100
  33.5 63.2 %copy-start.2 = (s32[256]{0:T(256)S(1)}, s32[256]{0:T(256)}, u32[]{:S(2)}) copy-start(s32[256]{0:T(256)} %param.28) | copy-start | bytes 3076
  39.3 57.5 %collective-permute-start = (bf16[256,512]{1,0:T(8,128)(2,1)S(1)}, bf16[256,512]{1,0:T(8,128)(2,1)S(1)}, u32[]{:S(2)}, u32[]{:S(2)}) collective-permute-start(bf16[256,512]{1,0:T(8,128)(2,1)S(1)} %fusion.31), channel_id=1, source_target_pairs={{0,1},{1,0},{2,3},{3,2},{4,5},{5,4},{6,7},{7,6},{8,9},{9,8},{10,11... | collective-permute-start | bytes 786440 | tf_op jit(solution)/shard_map/ppermute | solution.py:134
  96.9 20.7 %collective-permute-start.1 = (bf16[256,1024]{1,0:T(8,128)(2,1)S(1)}, bf16[256,1024]{1,0:T(8,128)(2,1)S(1)}, u32[]{:S(2)}, u32[]{:S(2)}) collective-permute-start(bf16[256,1024]{1,0:T(8,128)(2,1)S(1)} %maximum_select_fusion.3), channel_id=1, source_target_pairs={{0,2},{1,3},{2,0},{3,1},{4,6},{5,7},{6,4},{7,5},{8,10},{9,11},{10,... | collective-permute-start | bytes 1572872 | tf_op jit(solution)/shard_map/ppermute | solution.py:140
  99.9 21.8 %copy-start.8 = (f32[128]{0:T(128)S(1)}, f32[128]{0:T(128)}, u32[]{:S(2)}) copy-start(f32[128]{0:T(128)} %param.25) | copy-start | bytes 1540
  134.0 148.9 %all-gather.8.cloned.1.call-start = ((), (), s32[]{:S(2)}) async-start(), calls=%async_computation.2 | async-start | bytes 9437184 | tf_op jit(solution)/shard_map/all_gather | solution.py:241
  182.7 0.7 copy-start.7
  183.3 1.0 slice-start
  302.7 2.2 copy-start.1
  311.0 10.9 %collective-permute-start.2 = (bf16[256,1024]{1,0:T(8,128)(2,1)S(1)}, bf16[256,1024]{1,0:T(8,128)(2,1)S(1)}, u32[]{:S(2)}, u32[]{:S(2)}) collective-permute-start(bf16[256,1024]{1,0:T(8,128)(2,1)S(1)} %dynamic-slice_convert_fusion), channel_id=1, source_target_pairs={{0,2},{1,3},{2,0},{3,1},{4,6},{5,7},{6,4},{7,5},{8,10},{9,11},{10,... | collective-permute-start | bytes 1572872 | tf_op jit(solution)/shard_map/ppermute | solution.py:354
  323.2 15.1 %collective-permute-start.3 = (f32[256,512]{1,0:T(8,128)S(1)}, f32[256,512]{1,0:T(8,128)S(1)}, u32[]{:S(2)}, u32[]{:S(2)}) collective-permute-start(f32[256,512]{1,0:T(8,128)S(1)} %constant_dynamic-slice_fusion.2), channel_id=1, source_target_pairs={{0,1},{1,0},{2,3},{3,2},{4,5},{5,4},{6,7},{7,6},{8,9},{9,8},{10,11... | collective-permute-start | bytes 1572872 | tf_op jit(solution)/shard_map/ppermute | solution.py:360
Sparse Core Ops, SparseCore 0:
  33.3 84.2 all-gather.3
  134.1 40.2 all-gather.5
  176.2 92.1 all-gather.7

commit v7 on v6

--- a/solution.py
+++ b/solution.py
@@ -40,6 +40,7 @@
 SEQ_PARTS = ("z", "y", "xh")
 MESH_ID = pl.DeviceIdType.MESH
 AXES = SEQ_PARTS + ("mdl",)
+RING_CHUNKS = 4
 
 
 def _ring_kernel(x_ref, out_ref, send_sem, recv_sem, local_sem):
@@ -58,34 +59,48 @@
     pl.semaphore_wait(barrier, 2)
 
     rows = x_ref.shape[0]
-    half = rows // 2
-    to_minus = pltpu.make_async_remote_copy(
-        src_ref=x_ref, dst_ref=out_ref.at[1], send_sem=send_sem.at[0], recv_sem=recv_sem.at[0],
-        device_id=minus, device_id_type=MESH_ID)
-    to_plus = pltpu.make_async_remote_copy(
-        src_ref=x_ref, dst_ref=out_ref.at[3], send_sem=send_sem.at[1], recv_sem=recv_sem.at[1],
-        device_id=plus, device_id_type=MESH_ID)
+    n = RING_CHUNKS
+    step = rows // n
+
+    def rows_of(c):
+        return pl.ds(c * step, step)
+
+    def remote(src, dst, k, device):
+        return pltpu.make_async_remote_copy(
+            src_ref=src, dst_ref=dst, send_sem=send_sem.at[k], recv_sem=recv_sem.at[k],
+            device_id=device, device_id_type=MESH_ID)
+
+    to_minus = [remote(x_ref.at[rows_of(c)], out_ref.at[1, rows_of(c)], c, minus) for c in range(n)]
+    to_plus = [
+        remote(x_ref.at[rows_of(c)], out_ref.at[3, rows_of(c)], n + c, plus) for c in range(n)
+    ]
     own = pltpu.make_async_copy(x_ref, out_ref.at[0], local_sem.at[0])
-    to_minus.start()
-    to_plus.start()
+    for i in range(n):
+        to_minus[i].start()
+        to_plus[n - 1 - i].start()
     own.start()
-    to_minus.wait_recv()
-    on_minus = pltpu.make_async_remote_copy(
-        src_ref=out_ref.at[1, pl.ds(0, half)], dst_ref=out_ref.at[2, pl.ds(0, half)],
-        send_sem=send_sem.at[2], recv_sem=recv_sem.at[2], device_id=minus, device_id_type=MESH_ID)
-    on_minus.start()
-    to_plus.wait_recv()
-    on_plus = pltpu.make_async_remote_copy(
-        src_ref=out_ref.at[3, pl.ds(half, rows - half)], dst_ref=out_ref.at[2, pl.ds(half, rows - half)],
-        send_sem=send_sem.at[3], recv_sem=recv_sem.at[3], device_id=plus, device_id_type=MESH_ID)
-    on_plus.start()
-    to_minus.wait_send()
-    to_plus.wait_send()
+    forwards = []
+    for i in range(n // 2):
+        c = i
+        to_minus[c].wait_recv()
+        f = remote(out_ref.at[1, rows_of(c)], out_ref.at[2, rows_of(c)], 2 * n + c, minus)
+        f.start()
+        forwards.append(f)
+        c = n - 1 - i
+        to_plus[c].wait_recv()
+        f = remote(out_ref.at[3, rows_of(c)], out_ref.at[2, rows_of(c)], 2 * n + c, plus)
+        f.start()
+        forwards.append(f)
+    for i in range(n // 2, n):
+        to_minus[i].wait_recv()
+        to_plus[n - 1 - i].wait_recv()
+    for copy in to_minus + to_plus:
+        copy.wait_send()
     own.wait()
-    on_minus.wait_send()
-    on_plus.wait_send()
-    on_minus.wait_recv()
-    on_plus.wait_recv()
+    for f in forwards:
+        f.wait_send()
+    for f in forwards:
+        f.wait_recv()
 
 
 def ring_y_kernel(x, collective_id):
@@ -96,8 +111,8 @@
         in_specs=[pl.BlockSpec(memory_space=pl.ANY)],
         out_specs=pl.BlockSpec(memory_space=pl.ANY),
         scratch_shapes=[
-            pltpu.SemaphoreType.DMA((4,)),
-            pltpu.SemaphoreType.DMA((4,)),
+            pltpu.SemaphoreType.DMA((3 * RING_CHUNKS,)),
+            pltpu.SemaphoreType.DMA((3 * RING_CHUNKS,)),
             pltpu.SemaphoreType.DMA((1,)),
         ],
         compiler_params=pltpu.CompilerParams(collective_id=collective_id, has_side_effects=True),

time: 349 us -> 350 us (level)
  the two profiles are of different devices: /device:TPU:72 before, /device:TPU:229 now
where the time goes in v7:
time: 350 us; the launch traced here: 349 us
  Pallas kernels  98.8 us (28%)
  waiting for transfers between devices  86.4 us (25%)
  blocking collectives  67.1 us (19%)
  local copies, waits for them, and re-layouts  30.8 us (9%)
  other arithmetic  21.5 us (6%)
  between operations  16.9 us (5%)
  matrix products  12.2 us (3%)
  loops' own time  8.29 us (2%)
  starting transfers between devices  7.42 us (2%)
    pallas_call x3, Pallas kernels, ring_y_kernel(): pl.pallas_call(_ring_kernel, out_shape=jax.ShapeDtypeStruct((4, rows, wid...  98.8 us
    all_gather x1, waiting for transfers between devices, body(): k_all = lax.all_gather(k_part, 'z', axis=0, tiled=True)  31.8 us
    all_gather x1, waiting for transfers between devices, body(): v_part = lax.all_gather(kv_pair[:, kv_cols:], 'z', axis=0, tiled=True)  25.6 us
    all_gather x1, blocking collectives, gather_xh_z(): return lax.all_gather(x, 'z', axis=0, tiled=True)  25 us
    all_gather x1, waiting for transfers between devices, body(): gathered = lax.all_gather(packed, 'z', axis=0, tiled=True)  21.2 us
    all_gather x1, blocking collectives, body(): packed = lax.all_gather(packed, 'y', axis=0, tiled=True)  13.5 us
    all_gather x1, blocking collectives, body(): lax.all_gather(jnp.concatenate([k_rot, values_flat], axis=1), 'xh', axis=...  9.36 us
    psum x1, blocking collectives, body(): square_total = lax.psum(jnp.sum(wide_tokens * wide_tokens, axis=1), 'mdl')  8.63 us
  transfers between devices with their start and end apart: 7, of which 4 were waited for; matrix products, arithmetic and copies ran while one was open for 8% of the time, Pallas kernels for 28%

profile of v7, /device:TPU:229, one launch (start us, length us, event | category | flops | bytes accessed | tf_op | source)
XLA Modules:
  0.0 349.4 jit_solution(10562661111632914259)
XLA Ops:
  11.0 5.7 %all_gather.24 = bf16[64,1664]{1,0:T(8,128)(2,1)S(1)} all-gather(bf16[32,1664]{1,0:T(8,128)(2,1)S(1)} %constant_dynamic-update-slice_fusion), channel_id=1, replica_groups=mesh['z'=8,'y'=4,'xh'=2,'mdl'=4] {'xh'}, dimensions={0}, use_global_device_ids=true | all-gather | bytes 319488 | tf_op jit(solution)/shard_map/all_gather | solution.py:192
  16.8 13.5 %all_gather.25 = bf16[256,1664]{1,0:T(8,128)(2,1)} all-gather(bf16[64,1664]{1,0:T(8,128)(2,1)S(1)} %all_gather.24), channel_id=1, replica_groups=mesh['z'=8,'y'=4,'xh'=2,'mdl'=4] {'y'}, dimensions={0}, use_global_device_ids=true | all-gather | bytes 1064960 | tf_op jit(solution)/shard_map/all_gather | solution.py:193
  30.6 8.6 %psum.7 = f32[256]{0:T(256)S(1)} all-reduce(f32[256]{0:T(256)S(1)} %fusion.29), channel_id=1, replica_groups=mesh['z'=8,'y'=4,'xh'=2,'mdl'=4] {'mdl'}, use_global_device_ids=true, to_apply=%region_12.13 | all-reduce | flops 256 | bytes 2048 | tf_op jit(solution)/shard_map/psum | solution.py:207
  40.1 4.9 %all_gather.27 = bf16[64,512]{1,0:T(8,128)(2,1)S(1)} all-gather(bf16[32,512]{1,0:T(8,128)(2,1)S(1)} %copy-done.3), channel_id=1, replica_groups=mesh['z'=8,'y'=4,'xh'=2,'mdl'=4] {'xh'}, dimensions={0}, use_global_device_ids=true | all-gather | bytes 98304 | tf_op jit(solution)/shard_map/all_gather | solution.py:129
  45.0 25.0 %all_gather.28.x_ref = bf16[512,512]{1,0:T(8,128)(2,1)} all-gather(bf16[64,512]{1,0:T(8,128)(2,1)S(1)} %all_gather.27), channel_id=1, replica_groups=mesh['z'=8,'y'=4,'xh'=2,'mdl'=4] {'z'}, dimensions={0}, use_global_device_ids=true | all-gather | bytes 589824 | tf_op jit(solution)/shard_map/all_gather | solution.py:130
  70.0 19.7 %shard_map.157 = bf16[4,512,512]{2,1,0:T(8,128)(2,1)} custom-call(bf16[512,512]{1,0:T(8,128)(2,1)} %all_gather.28.x_ref), custom_call_target="tpu_custom_call" | custom-call | tf_op jit(solution)/shard_map/pallas_call | solution.py:108
  90.7 1.3 fusion.52
  94.5 21.2 %all-gather.4.cloned.1.call-done = bf16[2048,1664]{1,0:T(8,128)(2,1)} async-done(((bf16[256,1664]{1,0:T(8,128)(2,1)}), bf16[2048,1664]{1,0:T(8,128)(2,1)}) %all-gather.4.cloned.1.call-update) | async-done | bytes 6815760 | tf_op jit(solution)/shard_map/all_gather | solution.py:196
  115.7 3.4 fusion.12
  121.0 9.4 %all_gather.29 = bf16[512,512]{1,0:T(8,128)(2,1)S(1)} all-gather(bf16[256,512]{1,0:T(8,128)(2,1)S(1)} %pad_maximum_fusion), channel_id=1, replica_groups=mesh['z'=8,'y'=4,'xh'=2,'mdl'=4] {'xh'}, dimensions={0}, use_global_device_ids=true | all-gather | bytes 786432 | tf_op jit(solution)/shard_map/all_gather | solution.py:252
  131.2 11.8 %shard_map.158 = bf16[4,512,256]{2,1,0:T(8,128)(2,1)} custom-call(bf16[512,256]{1,0:T(8,128)(2,1)} %get-tuple-element.424.x_ref), custom_call_target="tpu_custom_call" | custom-call | tf_op jit(solution)/shard_map/pallas_call | solution.py:108
  143.0 25.6 %all-gather.6.cloned.1.call-done.x_ref = bf16[4096,256]{1,0:T(8,128)(2,1)} async-done(((bf16[512,256]{1,0:T(8,128)(2,1)}), bf16[4096,256]{1,0:T(8,128)(2,1)}) %all-gather.6.cloned.1.call-update) | async-done | bytes 2097168 | tf_op jit(solution)/shard_map/all_gather | solution.py:253
  179.2 67.3 %shard_map.159 = bf16[4,4096,256]{2,1,0:T(8,128)(2,1)} custom-call(bf16[4096,256]{1,0:T(8,128)(2,1)} %all-gather.6.cloned.1.call-done.x_ref), custom_call_target="tpu_custom_call" | custom-call | tf_op jit(solution)/shard_map/pallas_call | solution.py:108
  246.6 31.8 %all-gather.8.cloned.1.call-done = bf16[16384,256]{1,0:T(8,128)(2,1)} async-done(((bf16[2048,256]{1,0:T(8,128)(2,1)}), bf16[16384,256]{1,0:T(8,128)(2,1)}) %all-gather.8.cloned.1.call-update) | async-done | bytes 8388624 | tf_op jit(solution)/shard_map/all_gather | solution.py:256
  278.5 24.5 %while.18 = (s32[]{:T(128)}, f32[256,2,2]{0,2,1:T(2,128)S(1)}, f32[256,2,2]{0,2,1:T(2,128)S(1)}, f32[256,2,2,128]{0,3,2,1:T(8,128)S(1)}, s32[]{:T(128)}, /*index...) while((s32[]{:T(128)}, f32[256,2,2]{0,2,1:T(2,128)S(1)}, ...), condition=%wide.region_21.22_spmd.clone, body=%wide.region_17.21_spmd.clone.sunk | while | flops 137415776 | bytes 6106619 | solution.py:340
  303.9 1.2 copy.88
  305.2 4.7 %fusion.14 = f32[256,2048]{1,0:T(8,128)} fusion(bf16[2048,1664]{1,0:T(8,128)(2,1)} %all-gather.4.cloned.1.call-done, f32[256,512]{1,0:T(8,128)S(1)} %copy.88, bf16[256,2048]{0,1:T(8,128)(2,1)} %bitcast.81, bf16[2048,512]{1,0:T(8,128)(2,1)S(1)} %bitcast.76), kind=kOutput, calls=%fused_computation.29 | convolution fusion | flops 1074397184 | bytes 7864320 | tf_op jit(solution)/shard_map/dot_general | solution.py:355
  309.9 1.3 dynamic-slice_convert_fusion
  313.4 7.7 %collective-permute-done.2 = bf16[256,1024]{1,0:T(8,128)(2,1)S(1)} collective-permute-done((bf16[256,1024]{1,0:T(8,128)(2,1)S(1)}, bf16[256,1024]{1,0:T(8,128)(2,1)S(1)}, u32[]{:S(2)}, u32[]{:S(2)}) %collective-permute-start.2) | collective-permute-done | bytes 524320 | tf_op jit(solution)/shard_map/ppermute | solution.py:369
  321.1 1.4 convert_add_fusion
  322.6 4.6 %collective-permute-start.3 = (f32[256,512]{1,0:T(8,128)S(1)}, f32[256,512]{1,0:T(8,128)S(1)}, u32[]{:S(2)}, u32[]{:S(2)}) collective-permute-start(f32[256,512]{1,0:T(8,128)S(1)} %constant_dynamic-slice_fusion.2), channel_id=1, source_target_pairs={{0,1},{1,0},{2,3},{3,2},{4,5},{5,4},{6,7},{7,6},{8,9},{9,8},{10,11... | collective-permute-start | bytes 1572872 | tf_op jit(solution)/shard_map/ppermute | solution.py:375
  327.1 1.2 fusion.45
  328.9 6.0 %gather_fusion.1 = bf16[512,256]{1,0:T(8,128)(2,1)S(1)} fusion(bf16[16384,256]{1,0:T(8,128)(2,1)} %get-tuple-element.640, s32[1024]{0:T(1024)S(1)} %get-tuple-element.440), kind=kCustom, calls=%fused_computation.1.clone | custom fusion | bytes 526336 | tf_op jit(solution)/shard_map/jit(_take)/gather | solution.py:351
  335.0 6.0 %gather_fusion = bf16[512,256]{1,0:T(8,128)(2,1)S(1)} fusion(bf16[16384,256]{1,0:T(8,128)(2,1)} %get-tuple-element.652, s32[1024]{0:T(1024)S(1)} %get-tuple-element.441), kind=kCustom, calls=%fused_computation.clone | custom fusion | bytes 526336 | tf_op jit(solution)/shard_map/jit(_take)/gather | solution.py:350
  (182 shorter events, 40.8 us)
Async XLA Ops:
  7.2 32.9 %copy-start.3 = (bf16[32,512]{1,0:T(8,128)(2,1)S(1)}, bf16[32,512]{1,0:T(8,128)(2,1)}, u32[]{:S(2)}) copy-start(bf16[32,512]{1,0:T(8,128)(2,1)} %param.23) | copy-start | bytes 98308
  7.2 23.2 %copy-start.5 = (bf16[512]{0:T(512)(128)(2,1)S(1)}, bf16[512]{0:T(512)(128)(2,1)}, u32[]{:S(2)}) copy-start(bf16[512]{0:T(512)(128)(2,1)} %param.19) | copy-start | bytes 3076
  7.2 23.2 %copy-start = (bf16[256,512]{1,0:T(8,128)(2,1)S(1)}, bf16[256,512]{1,0:T(8,128)(2,1)}, u32[]{:S(2)}) copy-start(bf16[256,512]{1,0:T(8,128)(2,1)} %param.18) | copy-start | bytes 786436
  7.2 108.5 %all-gather.4.cloned.1.call-start = ((), (), s32[]{:S(2)}) async-start(), calls=%async_computation | async-start | bytes 7667712 | tf_op jit(solution)/shard_map/all_gather | solution.py:196
  30.3 59.4 %copy-start.4 = (s32[64]{0:T(128)S(1)}, s32[64]{0:T(128)}, u32[]{:S(2)}) copy-start(s32[64]{0:T(128)} %param.27) | copy-start | bytes 772
  30.3 138.3 %all-gather.6.cloned.1.call-start = ((), (), s32[]{:S(2)}) async-start(), calls=%async_computation.1 | async-start | bytes 2359296 | tf_op jit(solution)/shard_map/all_gather | solution.py:253
  30.4 59.6 %copy-start.9 = (s32[64]{0:T(128)S(1)}, s32[64]{0:T(128)}, u32[]{:S(2)}) copy-start(s32[64]{0:T(128)} %param.31) | copy-start | bytes 772
  30.4 60.2 %copy-start.6 = (s32[4,2]{0,1:T(2,128)S(1)}, s32[4,2]{0,1:T(2,128)}, u32[]{:S(2)}) copy-start(s32[4,2]{0,1:T(2,128)} %param.29) | copy-start | bytes 100
  30.6 61.5 %copy-start.2 = (s32[256]{0:T(256)S(1)}, s32[256]{0:T(256)}, u32[]{:S(2)}) copy-start(s32[256]{0:T(256)} %param.28) | copy-start | bytes 3076
  39.3 52.8 %collective-permute-start = (bf16[256,512]{1,0:T(8,128)(2,1)S(1)}, bf16[256,512]{1,0:T(8,128)(2,1)S(1)}, u32[]{:S(2)}, u32[]{:S(2)}) collective-permute-start(bf16[256,512]{1,0:T(8,128)(2,1)S(1)} %fusion.31), channel_id=1, source_target_pairs={{0,1},{1,0},{2,3},{3,2},{4,5},{5,4},{6,7},{7,6},{8,9},{9,8},{10,11... | collective-permute-start | bytes 786440 | tf_op jit(solution)/shard_map/ppermute | solution.py:149
  92.3 23.4 %collective-permute-start.1 = (bf16[256,1024]{1,0:T(8,128)(2,1)S(1)}, bf16[256,1024]{1,0:T(8,128)(2,1)S(1)}, u32[]{:S(2)}, u32[]{:S(2)}) collective-permute-start(bf16[256,1024]{1,0:T(8,128)(2,1)S(1)} %maximum_select_fusion.3), channel_id=1, source_target_pairs={{0,2},{1,3},{2,0},{3,1},{4,6},{5,7},{6,4},{7,5},{8,10},{9,11},{10,... | collective-permute-start | bytes 1572872 | tf_op jit(solution)/shard_map/ppermute | solution.py:155
  94.5 25.2 %copy-start.8 = (f32[128]{0:T(128)S(1)}, f32[128]{0:T(128)}, u32[]{:S(2)}) copy-start(f32[128]{0:T(128)} %param.25) | copy-start | bytes 1540
  131.2 147.2 %all-gather.8.cloned.1.call-start = ((), (), s32[]{:S(2)}) async-start(), calls=%async_computation.2 | async-start | bytes 9437184 | tf_op jit(solution)/shard_map/all_gather | solution.py:256
  176.9 0.7 copy-start.7
  177.5 1.0 slice-start
  303.0 2.2 copy-start.1
  311.2 9.9 %collective-permute-start.2 = (bf16[256,1024]{1,0:T(8,128)(2,1)S(1)}, bf16[256,1024]{1,0:T(8,128)(2,1)S(1)}, u32[]{:S(2)}, u32[]{:S(2)}) collective-permute-start(bf16[256,1024]{1,0:T(8,128)(2,1)S(1)} %dynamic-slice_convert_fusion), channel_id=1, source_target_pairs={{0,2},{1,3},{2,0},{3,1},{4,6},{5,7},{6,4},{7,5},{8,10},{9,11},{10,... | collective-permute-start | bytes 1572872 | tf_op jit(solution)/shard_map/ppermute | solution.py:369
  322.6 19.5 %collective-permute-start.3 = (f32[256,512]{1,0:T(8,128)S(1)}, f32[256,512]{1,0:T(8,128)S(1)}, u32[]{:S(2)}, u32[]{:S(2)}) collective-permute-start(f32[256,512]{1,0:T(8,128)S(1)} %constant_dynamic-slice_fusion.2), channel_id=1, source_target_pairs={{0,1},{1,0},{2,3},{3,2},{4,5},{5,4},{6,7},{7,6},{8,9},{9,8},{10,11... | collective-permute-start | bytes 1572872 | tf_op jit(solution)/shard_map/ppermute | solution.py:375
Sparse Core Ops, SparseCore 0:
  30.4 85.2 all-gather.3
  131.3 37.2 all-gather.5
  170.4 107.9 all-gather.7

commit v8 on v6

--- a/solution.py
+++ b/solution.py
@@ -280,6 +280,10 @@
     scale_factor = HEAD_SIZE ** (-0.5)
     head_shape = (local_rows, kv_heads, group)
 
+    stream_ids = jnp.arange(stream, dtype=jnp.int32)
+    key_segs = jnp.sum((stream_ids[:, None] >= ends[None, :]).astype(jnp.int32), axis=1)
+    key_tags = jnp.where(all_mask == 1, key_segs, -2)
+
     def key_block(i, loop_state):
         old_top, old_totals, old_summed = loop_state
         block = block_list[i]
@@ -290,15 +294,13 @@
         values_part = lax.dynamic_slice_in_dim(v_ring, v_row_of(offset), KEY_BLOCK, 0).reshape(
             KEY_BLOCK, kv_heads, HEAD_SIZE
         )
-        mask_part = lax.dynamic_slice_in_dim(all_mask, offset, KEY_BLOCK, 0)
+        tag_part = lax.dynamic_slice_in_dim(key_tags, offset, KEY_BLOCK, 0)
         columns = offset + jnp.arange(KEY_BLOCK, dtype=jnp.int32)
-        col_segs = jnp.sum((columns[:, None] >= ends[None, :]).astype(jnp.int32), axis=1)
-        live = mask_part == 1
-        own = col_segs[None, :] == row_segs[:, None]
-        other = col_segs[None, :] == row_shared[:, None]
+        own = tag_part[None, :] == row_segs[:, None]
+        other = tag_part[None, :] == row_shared[:, None]
         earlier = columns[None, :] <= token_ids[:, None]
         diagonal = columns[None, :] == token_ids[:, None]
-        visible = diagonal | (earlier & live[None, :] & (own | other))
+        visible = diagonal | (earlier & (own | other))
         allowed = visible[:, None, None, :]
         scores = (
             jnp.einsum("qhgd,khd->qhgk", q_rot, keys_part, preferred_element_type=jnp.float32)
@@ -330,10 +332,18 @@
     offsets = jnp.arange(LMAX, dtype=jnp.int32)
     wanted = my_start + offsets
     in_window = ((wanted < stream) & (offsets < my_length))[:, None]
-    source = jnp.clip(wanted, 0, stream - 1)
     zero = jnp.zeros((), jnp.bfloat16)
-    cache_k = jnp.where(in_window, jnp.take(k_all, k_row_of(source), axis=0), zero)
-    cache_v = jnp.where(in_window, jnp.take(v_ring, v_row_of(source), axis=0), zero)
+    first = my_start // KEY_BLOCK
+    shift = my_start % KEY_BLOCK
+    spans = [jnp.clip(first + j, 0, n_blocks - 1) * KEY_BLOCK for j in range(3)]
+
+    def cache_of(table, row_of):
+        pieces = [lax.dynamic_slice_in_dim(table, row_of(b), KEY_BLOCK, 0) for b in spans]
+        window = lax.dynamic_slice_in_dim(jnp.concatenate(pieces, axis=0), shift, LMAX, 0)
+        return jnp.where(in_window, window, zero)
+
+    cache_k = cache_of(k_all, k_row_of)
+    cache_v = cache_of(v_ring, v_row_of)
 
     attended = (summed / totals[..., None]).reshape(local_rows, query_heads * HEAD_SIZE)
     gated_heads = (attended * jax.nn.sigmoid(gate_logits)).astype(jnp.bfloat16)

time: 349 us -> 342 us (0.980)
  local copies, waits for them, and re-layouts: 29 us -> 19.4 us
    gather x2 -> x0, local copies, waits for them, and re-layouts: 12 us -> none  [the longest x1 6.02 us: body(): jnp.take(v_ring, v_row_of(source), axis=0)]
  transfers between devices with their start and end apart: 7 -> 7, of which waited for: 3 -> 3; matrix products, arithmetic and copies ran while one was open for 8% -> 5% of each run, Pallas kernels for 37% -> 37%
where the time goes in v8:
time: 342 us; the launch traced here: 340 us
  Pallas kernels  127 us (37%)
  blocking collectives  75 us (22%)
  waiting for transfers between devices  56.2 us (16%)
  other arithmetic  20.6 us (6%)
  between operations  19.6 us (6%)
  local copies, waits for them, and re-layouts  19.4 us (6%)
  matrix products  11.4 us (3%)
  loops' own time  6.82 us (2%)
  starting transfers between devices  3.68 us (1%)
    pallas_call x3, Pallas kernels, ring_y_kernel(): pl.pallas_call(_ring_kernel, out_shape=jax.ShapeDtypeStruct((4, rows, wid...  127 us
    all_gather x1, blocking collectives, gather_xh_z(): return lax.all_gather(x, 'z', axis=0, tiled=True)  30.8 us
    all_gather x1, waiting for transfers between devices, body(): v_part = lax.all_gather(kv_pair[:, kv_cols:], 'z', axis=0, tiled=True)  27.4 us
    all_gather x1, waiting for transfers between devices, body(): gathered = lax.all_gather(packed, 'z', axis=0, tiled=True)  17.7 us
    all_gather x1, blocking collectives, body(): packed = lax.all_gather(packed, 'y', axis=0, tiled=True)  15.3 us
    ppermute x1, waiting for transfers between devices, body(): lax.ppermute(theirs.astype(jnp.bfloat16), 'mdl', [(m, m ^ 2) for m in ran...  11 us
    all_gather x1, blocking collectives, body(): lax.all_gather(jnp.concatenate([k_rot, values_flat], axis=1), 'xh', axis=...  10.2 us
    all_gather x1, blocking collectives, body(): packed = lax.all_gather(packed, 'xh', axis=0, tiled=True)  6.89 us
  transfers between devices with their start and end apart: 7, of which 3 were waited for; matrix products, arithmetic and copies ran while one was open for 5% of the time, Pallas kernels for 37%

profile of v8, /device:TPU:72, one launch (start us, length us, event | category | flops | bytes accessed | tf_op | source)
XLA Modules:
  0.0 339.7 jit_solution(10584400591110896523)
XLA Ops:
  11.0 6.9 %all_gather.24 = bf16[64,1664]{1,0:T(8,128)(2,1)S(1)} all-gather(bf16[32,1664]{1,0:T(8,128)(2,1)S(1)} %constant_dynamic-update-slice_fusion), channel_id=1, replica_groups=mesh['z'=8,'y'=4,'xh'=2,'mdl'=4] {'xh'}, dimensions={0}, use_global_device_ids=true | all-gather | bytes 319488 | tf_op jit(solution)/shard_map/all_gather | solution.py:177
  17.9 15.3 %all_gather.25 = bf16[256,1664]{1,0:T(8,128)(2,1)} all-gather(bf16[64,1664]{1,0:T(8,128)(2,1)S(1)} %all_gather.24), channel_id=1, replica_groups=mesh['z'=8,'y'=4,'xh'=2,'mdl'=4] {'y'}, dimensions={0}, use_global_device_ids=true | all-gather | bytes 1064960 | tf_op jit(solution)/shard_map/all_gather | solution.py:178
  33.5 5.7 %psum.7 = f32[256]{0:T(256)S(1)} all-reduce(f32[256]{0:T(256)S(1)} %fusion.29), channel_id=1, replica_groups=mesh['z'=8,'y'=4,'xh'=2,'mdl'=4] {'mdl'}, use_global_device_ids=true, to_apply=%region_12.13 | all-reduce | flops 256 | bytes 2048 | tf_op jit(solution)/shard_map/psum | solution.py:192
  39.4 6.1 %all_gather.27 = bf16[64,512]{1,0:T(8,128)(2,1)S(1)} all-gather(bf16[32,512]{1,0:T(8,128)(2,1)S(1)} %copy-done.3), channel_id=1, replica_groups=mesh['z'=8,'y'=4,'xh'=2,'mdl'=4] {'xh'}, dimensions={0}, use_global_device_ids=true | all-gather | bytes 98304 | tf_op jit(solution)/shard_map/all_gather | solution.py:114
  45.5 30.8 %all_gather.28.x_ref = bf16[512,512]{1,0:T(8,128)(2,1)} all-gather(bf16[64,512]{1,0:T(8,128)(2,1)S(1)} %all_gather.27), channel_id=1, replica_groups=mesh['z'=8,'y'=4,'xh'=2,'mdl'=4] {'z'}, dimensions={0}, use_global_device_ids=true | all-gather | bytes 589824 | tf_op jit(solution)/shard_map/all_gather | solution.py:115
  76.3 17.9 %shard_map.157 = bf16[4,512,512]{2,1,0:T(8,128)(2,1)} custom-call(bf16[512,512]{1,0:T(8,128)(2,1)} %all_gather.28.x_ref), custom_call_target="tpu_custom_call" | custom-call | tf_op jit(solution)/shard_map/pallas_call | solution.py:93
  95.3 1.3 fusion.49
  96.9 1.8 collective-permute-start.1
  99.9 17.7 %all-gather.4.cloned.1.call-done = bf16[2048,1664]{1,0:T(8,128)(2,1)} async-done(((bf16[256,1664]{1,0:T(8,128)(2,1)}), bf16[2048,1664]{1,0:T(8,128)(2,1)}) %all-gather.4.cloned.1.call-update) | async-done | bytes 6815760 | tf_op jit(solution)/shard_map/all_gather | solution.py:181
  117.6 3.4 %fusion.12 = f32[256,1024]{1,0:T(8,128)S(1)} fusion(bf16[2048,1664]{1,0:T(8,128)(2,1)} %all-gather.4.cloned.1.call-done, bf16[256,1024]{1,0:T(8,128)(2,1)S(1)} %collective-permute-done.1, bf16[256,1024]{1,0:T(8,128)(2,1)S(1)} %maximum_select_fusion.3, pred[]{:T(512)S(6)} %eq.177), kind=kOutput, calls=%fused_computation.21 | convolution fusion | flops 1078460416 | bytes 6291457 | tf_op jit(solution)/shard_map/dot_general | solution.py:199
  122.9 10.2 %all_gather.29 = bf16[512,512]{1,0:T(8,128)(2,1)S(1)} all-gather(bf16[256,512]{1,0:T(8,128)(2,1)S(1)} %pad_maximum_fusion), channel_id=1, replica_groups=mesh['z'=8,'y'=4,'xh'=2,'mdl'=4] {'xh'}, dimensions={0}, use_global_device_ids=true | all-gather | bytes 786432 | tf_op jit(solution)/shard_map/all_gather | solution.py:237
  134.0 13.0 %shard_map.158 = bf16[4,512,256]{2,1,0:T(8,128)(2,1)} custom-call(bf16[512,256]{1,0:T(8,128)(2,1)} %get-tuple-element.406.x_ref), custom_call_target="tpu_custom_call" | custom-call | tf_op jit(solution)/shard_map/pallas_call | solution.py:93
  147.0 27.4 %all-gather.6.cloned.1.call-done.x_ref = bf16[4096,256]{1,0:T(8,128)(2,1)} async-done(((bf16[512,256]{1,0:T(8,128)(2,1)}), bf16[4096,256]{1,0:T(8,128)(2,1)}) %all-gather.6.cloned.1.call-update) | async-done | bytes 2097168 | tf_op jit(solution)/shard_map/all_gather | solution.py:238
  183.4 1.2 slice_compare_fusion
  186.8 96.1 %shard_map.159 = bf16[4,4096,256]{2,1,0:T(8,128)(2,1)} custom-call(bf16[4096,256]{1,0:T(8,128)(2,1)} %all-gather.6.cloned.1.call-done.x_ref), custom_call_target="tpu_custom_call" | custom-call | tf_op jit(solution)/shard_map/pallas_call | solution.py:93
  283.0 19.4 %while.18 = (s32[]{:T(128)}, f32[256,2,2]{0,2,1:T(2,128)S(1)}, f32[256,2,2]{0,2,1:T(2,128)S(1)}, f32[256,2,2,128]{0,3,2,1:T(8,128)S(1)}, s32[]{:T(128)}, /*index...) while((s32[]{:T(128)}, f32[256,2,2]{0,2,1:T(2,128)S(1)}, ...), condition=%wide.region_21.22_spmd.clone, body=%wide.region_18.21_spmd.clone.sunk | while | flops 137300576 | bytes 6105339 | solution.py:327
  303.3 1.2 copy.88
  304.5 4.7 %fusion.14 = f32[256,2048]{1,0:T(8,128)} fusion(bf16[2048,1664]{1,0:T(8,128)(2,1)} %all-gather.4.cloned.1.call-done, f32[256,512]{1,0:T(8,128)S(1)} %copy.88, bf16[256,2048]{0,1:T(8,128)(2,1)} %bitcast.81, bf16[2048,512]{1,0:T(8,128)(2,1)S(1)} %bitcast.76), kind=kOutput, calls=%fused_computation.27 | convolution fusion | flops 1074397184 | bytes 7864320 | tf_op jit(solution)/shard_map/dot_general | solution.py:350
  309.3 1.3 dynamic-slice_convert_fusion
  310.6 1.6 collective-permute-start.2
  312.1 11.0 %collective-permute-done.2 = bf16[256,1024]{1,0:T(8,128)(2,1)S(1)} collective-permute-done((bf16[256,1024]{1,0:T(8,128)(2,1)S(1)}, bf16[256,1024]{1,0:T(8,128)(2,1)S(1)}, u32[]{:S(2)}, u32[]{:S(2)}) %collective-permute-start.2) | collective-permute-done | bytes 524320 | tf_op jit(solution)/shard_map/ppermute | solution.py:364
  323.2 1.4 convert_add_fusion
  324.7 1.2 fusion.43
  330.8 1.4 fusion.36
  (161 shorter events, 34.5 us)
Async XLA Ops:
  7.2 32.2 %copy-start.3 = (bf16[32,512]{1,0:T(8,128)(2,1)S(1)}, bf16[32,512]{1,0:T(8,128)(2,1)}, u32[]{:S(2)}) copy-start(bf16[32,512]{1,0:T(8,128)(2,1)} %param.21) | copy-start | bytes 98308
  7.2 26.1 %copy-start.5 = (bf16[512]{0:T(512)(128)(2,1)S(1)}, bf16[512]{0:T(512)(128)(2,1)}, u32[]{:S(2)}) copy-start(bf16[512]{0:T(512)(128)(2,1)} %param.17) | copy-start | bytes 3076
  7.2 26.1 %copy-start = (bf16[256,512]{1,0:T(8,128)(2,1)S(1)}, bf16[256,512]{1,0:T(8,128)(2,1)}, u32[]{:S(2)}) copy-start(bf16[256,512]{1,0:T(8,128)(2,1)} %param.16) | copy-start | bytes 786436
  7.2 110.4 %all-gather.4.cloned.1.call-start = ((), (), s32[]{:S(2)}) async-start(), calls=%async_computation | async-start | bytes 7667712 | tf_op jit(solution)/shard_map/all_gather | solution.py:181
  33.2 61.0 %copy-start.4 = (s32[64]{0:T(128)S(1)}, s32[64]{0:T(128)}, u32[]{:S(2)}) copy-start(s32[64]{0:T(128)} %param.25) | copy-start | bytes 772
  33.2 141.2 %all-gather.6.cloned.1.call-start = ((), (), s32[]{:S(2)}) async-start(), calls=%async_computation.1 | async-start | bytes 2359296 | tf_op jit(solution)/shard_map/all_gather | solution.py:238
  33.3 61.3 %copy-start.9 = (s32[64]{0:T(128)S(1)}, s32[64]{0:T(128)}, u32[]{:S(2)}) copy-start(s32[64]{0:T(128)} %param.29) | copy-start | bytes 772
  33.3 61.9 %copy-start.6 = (s32[4,2]{0,1:T(2,128)S(1)}, s32[4,2]{0,1:T(2,128)}, u32[]{:S(2)}) copy-start(s32[4,2]{0,1:T(2,128)} %param.27) | copy-start | bytes 100
  33.5 63.2 %copy-start.2 = (s32[256]{0:T(256)S(1)}, s32[256]{0:T(256)}, u32[]{:S(2)}) copy-start(s32[256]{0:T(256)} %param.26) | copy-start | bytes 3076
  39.3 57.5 %collective-permute-start = (bf16[256,512]{1,0:T(8,128)(2,1)S(1)}, bf16[256,512]{1,0:T(8,128)(2,1)S(1)}, u32[]{:S(2)}, u32[]{:S(2)}) collective-permute-start(bf16[256,512]{1,0:T(8,128)(2,1)S(1)} %fusion.31), channel_id=1, source_target_pairs={{0,1},{1,0},{2,3},{3,2},{4,5},{5,4},{6,7},{7,6},{8,9},{9,8},{10,11... | collective-permute-start | bytes 786440 | tf_op jit(solution)/shard_map/ppermute | solution.py:134
  96.9 20.7 %collective-permute-start.1 = (bf16[256,1024]{1,0:T(8,128)(2,1)S(1)}, bf16[256,1024]{1,0:T(8,128)(2,1)S(1)}, u32[]{:S(2)}, u32[]{:S(2)}) collective-permute-start(bf16[256,1024]{1,0:T(8,128)(2,1)S(1)} %maximum_select_fusion.3), channel_id=1, source_target_pairs={{0,2},{1,3},{2,0},{3,1},{4,6},{5,7},{6,4},{7,5},{8,10},{9,11},{10,... | collective-permute-start | bytes 1572872 | tf_op jit(solution)/shard_map/ppermute | solution.py:140
  99.9 21.7 %copy-start.8 = (f32[128]{0:T(128)S(1)}, f32[128]{0:T(128)}, u32[]{:S(2)}) copy-start(f32[128]{0:T(128)} %param.23) | copy-start | bytes 1540
  134.0 148.9 %all-gather.8.cloned.1.call-start = ((), (), s32[]{:S(2)}) async-start(), calls=%async_computation.2 | async-start | bytes 9437184 | tf_op jit(solution)/shard_map/all_gather | solution.py:241
  183.3 2.3 copy-start.7
  302.3 2.2 copy-start.1
  310.6 12.6 %collective-permute-start.2 = (bf16[256,1024]{1,0:T(8,128)(2,1)S(1)}, bf16[256,1024]{1,0:T(8,128)(2,1)S(1)}, u32[]{:S(2)}, u32[]{:S(2)}) collective-permute-start(bf16[256,1024]{1,0:T(8,128)(2,1)S(1)} %dynamic-slice_convert_fusion), channel_id=1, source_target_pairs={{0,2},{1,3},{2,0},{3,1},{4,6},{5,7},{6,4},{7,5},{8,10},{9,11},{10,... | collective-permute-start | bytes 1572872 | tf_op jit(solution)/shard_map/ppermute | solution.py:364
  324.6 7.7 %collective-permute-start.3 = (f32[256,512]{1,0:T(8,128)S(1)}, f32[256,512]{1,0:T(8,128)S(1)}, u32[]{:S(2)}, u32[]{:S(2)}) collective-permute-start(f32[256,512]{1,0:T(8,128)S(1)} %constant_dynamic-slice_fusion.8), channel_id=1, source_target_pairs={{0,1},{1,0},{2,3},{3,2},{4,5},{5,4},{6,7},{7,6},{8,9},{9,8},{10,11... | collective-permute-start | bytes 1572872 | tf_op jit(solution)/shard_map/ppermute | solution.py:370
Sparse Core Ops, SparseCore 0:
  33.3 84.2 all-gather.3
  134.1 40.2 all-gather.5
  176.2 92.1 all-gather.7

commit v9 on v8

--- a/solution.py
+++ b/solution.py
@@ -9,6 +9,7 @@
 HEAD_SIZE = 128
 LMAX = 512
 KEY_BLOCK = 256
+BATCH_BLOCKS = 8
 
 
 epsilon = 1e-06
@@ -319,12 +320,43 @@
         )
         return (new_top, new_totals, new_summed)
 
-    start_state = (
-        jnp.full(head_shape, masked_score, jnp.float32),
-        jnp.zeros(head_shape, jnp.float32),
-        jnp.zeros(head_shape + (HEAD_SIZE,), jnp.float32),
-    )
-    top_now, totals, summed = lax.fori_loop(0, n_needed, key_block, start_state)
+    slots = block_list[:BATCH_BLOCKS]
+    slot_live = jnp.arange(BATCH_BLOCKS, dtype=jnp.int32) < n_needed
+    slot_offsets = slots * KEY_BLOCK
+    keys_b = jnp.stack(
+        [lax.dynamic_slice_in_dim(k_all, k_row_of(o), KEY_BLOCK, 0) for o in slot_offsets]
+    ).reshape(BATCH_BLOCKS * KEY_BLOCK, kv_heads, HEAD_SIZE)
+    values_b = jnp.stack(
+        [lax.dynamic_slice_in_dim(v_ring, v_row_of(o), KEY_BLOCK, 0) for o in slot_offsets]
+    ).reshape(BATCH_BLOCKS * KEY_BLOCK, kv_heads, HEAD_SIZE)
+    tags_b = jnp.stack(
+        [lax.dynamic_slice_in_dim(key_tags, o, KEY_BLOCK, 0) for o in slot_offsets]
+    ).reshape(-1)
+    columns_b = (slot_offsets[:, None] + jnp.arange(KEY_BLOCK, dtype=jnp.int32)[None, :]).reshape(-1)
+    live_b = jnp.repeat(slot_live, KEY_BLOCK)
+    visible_b = live_b[None, :] & (
+        (columns_b[None, :] == token_ids[:, None])
+        | (
+            (columns_b[None, :] <= token_ids[:, None])
+            & ((tags_b[None, :] == row_segs[:, None]) | (tags_b[None, :] == row_shared[:, None]))
+        )
+    )
+    allowed_b = visible_b[:, None, None, :]
+    scores_b = (
+        jnp.einsum("qhgd,khd->qhgk", q_rot, keys_b, preferred_element_type=jnp.float32)
+        * scale_factor
+    )
+    scores_b = jnp.where(allowed_b, scores_b, masked_score)
+    top_b = jnp.max(scores_b, axis=-1)
+    raw_b = jnp.where(allowed_b, jnp.exp(scores_b - top_b[..., None]), 0.0)
+    totals_b = jnp.sum(raw_b, axis=-1)
+    summed_b = jnp.einsum(
+        "qhgk,khd->qhgd", raw_b.astype(jnp.bfloat16), values_b, preferred_element_type=jnp.float32
+    )
+    start_state = (top_b, totals_b, summed_b)
+    top_now, totals, summed = lax.fori_loop(
+        jnp.minimum(n_needed, BATCH_BLOCKS), n_needed, key_block, start_state
+    )
 
     my_request = jnp.sum(jnp.where(cache_slot == device_seq, requests, 0))
     my_start = jnp.sum(jnp.where(requests == my_request, starts, 0))

time: 342 us -> 350 us (1.023)
  between operations: 19.6 us -> 51.6 us
  Pallas kernels: 127 us -> 99.5 us
  waiting for transfers between devices: 56.2 us -> 46.9 us
  local copies, waits for them, and re-layouts: 19.4 us -> 28.3 us
  other arithmetic: 20.6 us -> 28 us
  loops' own time: 6.82 us -> 0.88 us
    pallas_call x3, Pallas kernels: 127 us -> 99.5 us  [ring_y_kernel(): pl.pallas_call(_ring_kernel, out_shape=jax.ShapeDtypeStruct((4, rows, wid...]
    unnamed x25 -> x29, local copies, waits for them, and re-layouts: 3.08 us -> 16.3 us
    dynamic_slice x20 -> x1, local copies, waits for them, and re-layouts: 7.68 us -> 0.12 us  [body(): lax.dynamic_slice_in_dim(key_tags, o, KEY_BLOCK, 0)]
    all_gather x1, waiting for transfers between devices: 17.7 us -> 10.6 us  [body(): gathered = lax.all_gather(packed, 'z', axis=0, tiled=True)]
    another operation x1, loops' own time: 6.82 us -> 0.88 us  [body(): lax.fori_loop(jnp.minimum(n_needed, BATCH_BLOCKS), n_needed, key_block, s...]
  transfers between devices with their start and end apart: 7 -> 7, of which waited for: 3 -> 3; matrix products, arithmetic and copies ran while one was open for 5% -> 11% of each run, Pallas kernels for 37% -> 29%
where the time goes in v9:
time: 350 us; the launch traced here: 347 us
  Pallas kernels  99.5 us (28%)
  blocking collectives  75.2 us (21%)
  between operations  51.6 us (15%)
  waiting for transfers between devices  46.9 us (13%)
  local copies, waits for them, and re-layouts  28.3 us (8%)
  other arithmetic  28 us (8%)
  matrix products  12.4 us (4%)
  starting transfers between devices  3.94 us (1%)
    pallas_call x3, Pallas kernels, ring_y_kernel(): pl.pallas_call(_ring_kernel, out_shape=jax.ShapeDtypeStruct((4, rows, wid...  99.5 us
    all_gather x1, blocking collectives, gather_xh_z(): return lax.all_gather(x, 'z', axis=0, tiled=True)  30.8 us
    all_gather x1, waiting for transfers between devices, body(): v_part = lax.all_gather(kv_pair[:, kv_cols:], 'z', axis=0, tiled=True)  27.3 us
    unnamed x29, local copies, waits for them, and re-layouts  16.3 us
    all_gather x1, blocking collectives, body(): packed = lax.all_gather(packed, 'y', axis=0, tiled=True)  15.3 us
    all_gather x1, waiting for transfers between devices, body(): gathered = lax.all_gather(packed, 'z', axis=0, tiled=True)  10.6 us
    all_gather x1, blocking collectives, body(): lax.all_gather(jnp.concatenate([k_rot, values_flat], axis=1), 'xh', axis=...  10.2 us
    ppermute x1, waiting for transfers between devices, body(): lax.ppermute(theirs.astype(jnp.bfloat16), 'mdl', [(m, m ^ 2) for m in ran...  8.86 us
  transfers between devices with their start and end apart: 7, of which 3 were waited for; matrix products, arithmetic and copies ran while one was open for 11% of the time, Pallas kernels for 29%

profile of v9, /device:TPU:72, one launch (start us, length us, event | category | flops | bytes accessed | tf_op | source)
XLA Modules:
  0.0 346.7 jit_solution(13928580084885663439)
XLA Ops:
  11.0 6.9 %all_gather.24 = bf16[64,1664]{1,0:T(8,128)(2,1)S(1)} all-gather(bf16[32,1664]{1,0:T(8,128)(2,1)S(1)} %constant_dynamic-update-slice_fusion), channel_id=1, replica_groups=mesh['z'=8,'y'=4,'xh'=2,'mdl'=4] {'xh'}, dimensions={0}, use_global_device_ids=true | all-gather | bytes 319488 | tf_op jit(solution)/shard_map/all_gather | solution.py:178
  17.9 15.3 %all_gather.25 = bf16[256,1664]{1,0:T(8,128)(2,1)} all-gather(bf16[64,1664]{1,0:T(8,128)(2,1)S(1)} %all_gather.24), channel_id=1, replica_groups=mesh['z'=8,'y'=4,'xh'=2,'mdl'=4] {'y'}, dimensions={0}, use_global_device_ids=true | all-gather | bytes 1064960 | tf_op jit(solution)/shard_map/all_gather | solution.py:179
  35.0 5.7 %psum.7 = f32[256]{0:T(256)S(1)} all-reduce(f32[256]{0:T(256)S(1)} %fusion.41), channel_id=1, replica_groups=mesh['z'=8,'y'=4,'xh'=2,'mdl'=4] {'mdl'}, use_global_device_ids=true, to_apply=%region_15.16 | all-reduce | flops 256 | bytes 2048 | tf_op jit(solution)/shard_map/psum | solution.py:193
  41.8 6.3 %all_gather.27 = bf16[64,512]{1,0:T(8,128)(2,1)S(1)} all-gather(bf16[32,512]{1,0:T(8,128)(2,1)} %param.21), channel_id=1, replica_groups=mesh['z'=8,'y'=4,'xh'=2,'mdl'=4] {'xh'}, dimensions={0}, use_global_device_ids=true | all-gather | bytes 98304 | tf_op jit(solution)/shard_map/all_gather | solution.py:115
  48.1 30.8 %all_gather.28.x_ref = bf16[512,512]{1,0:T(8,128)(2,1)} all-gather(bf16[64,512]{1,0:T(8,128)(2,1)S(1)} %all_gather.27), channel_id=1, replica_groups=mesh['z'=8,'y'=4,'xh'=2,'mdl'=4] {'z'}, dimensions={0}, use_global_device_ids=true | all-gather | bytes 589824 | tf_op jit(solution)/shard_map/all_gather | solution.py:116
  79.0 17.9 %shard_map.157 = bf16[4,512,512]{2,1,0:T(8,128)(2,1)} custom-call(bf16[512,512]{1,0:T(8,128)(2,1)} %all_gather.28.x_ref), custom_call_target="tpu_custom_call" | custom-call | tf_op jit(solution)/shard_map/pallas_call | solution.py:94
  97.9 1.3 fusion.63
  100.7 2.0 fusion.61
  103.6 2.1 collective-permute-start.1
  106.9 10.6 %all-gather.4.cloned.1.call-done = bf16[2048,1664]{1,0:T(8,128)(2,1)} async-done(((bf16[256,1664]{1,0:T(8,128)(2,1)}), bf16[2048,1664]{1,0:T(8,128)(2,1)}) %all-gather.4.cloned.1.call-update) | async-done | bytes 6815760 | tf_op jit(solution)/shard_map/all_gather | solution.py:182
  117.6 3.4 fusion.15
  122.8 10.2 %all_gather.29 = bf16[512,512]{1,0:T(8,128)(2,1)S(1)} all-gather(bf16[256,512]{1,0:T(8,128)(2,1)S(1)} %pad_maximum_fusion), channel_id=1, replica_groups=mesh['z'=8,'y'=4,'xh'=2,'mdl'=4] {'xh'}, dimensions={0}, use_global_device_ids=true | all-gather | bytes 786432 | tf_op jit(solution)/shard_map/all_gather | solution.py:238
  134.0 13.0 %shard_map.158 = bf16[4,512,256]{2,1,0:T(8,128)(2,1)} custom-call(bf16[512,256]{1,0:T(8,128)(2,1)} %get-tuple-element.420.x_ref), custom_call_target="tpu_custom_call" | custom-call | tf_op jit(solution)/shard_map/pallas_call | solution.py:94
  147.0 27.3 %all-gather.6.cloned.1.call-done.x_ref = bf16[4096,256]{1,0:T(8,128)(2,1)} async-done(((bf16[512,256]{1,0:T(8,128)(2,1)}), bf16[4096,256]{1,0:T(8,128)(2,1)}) %all-gather.6.cloned.1.call-update) | async-done | bytes 2097168 | tf_op jit(solution)/shard_map/all_gather | solution.py:239
  220.4 1.8 or_and_fusion
  222.2 68.6 %shard_map.159 = bf16[4,4096,256]{2,1,0:T(8,128)(2,1)} custom-call(bf16[4096,256]{1,0:T(8,128)(2,1)} %all-gather.6.cloned.1.call-done.x_ref), custom_call_target="tpu_custom_call" | custom-call | tf_op jit(solution)/shard_map/pallas_call | solution.py:94
  307.6 2.7 fusion.12
  310.3 2.1 fusion.14
  312.4 2.3 fusion.26
  315.8 4.0 %fusion.20 = f32[256,2048]{1,0:T(8,128)S(1)} fusion(bf16[2048,1664]{1,0:T(8,128)(2,1)} %all-gather.4.cloned.1.call-done, f32[256,512]{1,0:T(8,128)S(1)} %copy.132, bf16[256,2048]{0,1:T(8,128)(2,1)} %bitcast.160, bf16[2048,512]{1,0:T(8,128)(2,1)} %bitcast.155), kind=kOutput, calls=%fused_computation.34 | convolution fusion | flops 1074397184 | bytes 7864320 | tf_op jit(solution)/shard_map/dot_general | solution.py:382
  319.9 1.6 collective-permute-start.2
  321.5 8.9 %collective-permute-done.2 = bf16[256,1024]{1,0:T(8,128)(2,1)} collective-permute-done((bf16[256,1024]{1,0:T(8,128)(2,1)S(1)}, bf16[256,1024]{1,0:T(8,128)(2,1)}, u32[]{:S(2)}, u32[]{:S(2)}) %collective-permute-start.2) | collective-permute-done | bytes 524320 | tf_op jit(solution)/shard_map/ppermute | solution.py:396
  330.3 1.2 convert_add_fusion
  337.9 1.4 fusion.48
  (127 shorter events, 47.8 us)
Async XLA Ops:
  7.2 110.4 %all-gather.4.cloned.1.call-start = ((), (), s32[]{:S(2)}) async-start(), calls=%async_computation | async-start | bytes 7667712 | tf_op jit(solution)/shard_map/all_gather | solution.py:182
  33.1 141.1 %all-gather.6.cloned.1.call-start = ((), (), s32[]{:S(2)}) async-start(), calls=%async_computation.1 | async-start | bytes 2359296 | tf_op jit(solution)/shard_map/all_gather | solution.py:239
  41.7 61.7 %collective-permute-start = (bf16[256,512]{1,0:T(8,128)(2,1)S(1)}, bf16[256,512]{1,0:T(8,128)(2,1)S(1)}, u32[]{:S(2)}, u32[]{:S(2)}) collective-permute-start(bf16[256,512]{1,0:T(8,128)(2,1)S(1)} %fusion.43), channel_id=1, source_target_pairs={{0,1},{1,0},{2,3},{3,2},{4,5},{5,4},{6,7},{7,6},{8,9},{9,8},{10,11... | collective-permute-start | bytes 786440 | tf_op jit(solution)/shard_map/ppermute | solution.py:135
  79.0 42.6 %copy-start.3 = (f32[128]{0:T(128)S(1)}, f32[128]{0:T(128)}, u32[]{:S(2)}) copy-start(f32[128]{0:T(128)} %param.23) | copy-start | bytes 1540
  103.6 14.0 %collective-permute-start.1 = (bf16[256,1024]{1,0:T(8,128)(2,1)S(1)}, bf16[256,1024]{1,0:T(8,128)(2,1)S(1)}, u32[]{:S(2)}, u32[]{:S(2)}) collective-permute-start(bf16[256,1024]{1,0:T(8,128)(2,1)S(1)} %maximum_select_fusion.3), channel_id=1, source_target_pairs={{0,2},{1,3},{2,0},{3,1},{4,6},{5,7},{6,4},{7,5},{8,10},{9,11},{10,... | collective-permute-start | bytes 1572872 | tf_op jit(solution)/shard_map/ppermute | solution.py:141
  106.9 70.1 %copy-start.1 = (s32[256]{0:T(256)S(1)}, s32[256]{0:T(256)}, u32[]{:S(2)}) copy-start(s32[256]{0:T(256)} %param.26) | copy-start | bytes 3076
  133.9 164.8 %all-gather.8.cloned.1.call-start = ((), (), s32[]{:S(2)}) async-start(), calls=%async_computation.2 | async-start | bytes 9437184 | tf_op jit(solution)/shard_map/all_gather | solution.py:242
  174.3 45.0 %copy-start.2 = (f32[128]{0:T(128)S(1)}, f32[128]{0:T(128)}, u32[]{:S(2)}) copy-start(f32[128]{0:T(128)} %param.22) | copy-start | bytes 1540
  315.8 23.5 %copy-start = (bf16[256,512]{1,0:T(8,128)(2,1)S(1)}, bf16[256,512]{1,0:T(8,128)(2,1)}, u32[]{:S(2)}) copy-start(bf16[256,512]{1,0:T(8,128)(2,1)} %param.16) | copy-start | bytes 786436
  319.9 10.4 %collective-permute-start.2 = (bf16[256,1024]{1,0:T(8,128)(2,1)S(1)}, bf16[256,1024]{1,0:T(8,128)(2,1)}, u32[]{:S(2)}, u32[]{:S(2)}) collective-permute-start(bf16[256,1024]{1,0:T(8,128)(2,1)S(1)} %dynamic-slice_convert_fusion), channel_id=1, source_target_pairs={{0,2},{1,3},{2,0},{3,1},{4,6},{5,7},{6,4},{7,5},{8,10},{9,11},{10,... | collective-permute-start | bytes 1572872 | tf_op jit(solution)/shard_map/ppermute | solution.py:396
  331.6 7.7 %collective-permute-start.3 = (f32[256,512]{1,0:T(8,128)S(1)}, f32[256,512]{1,0:T(8,128)S(1)}, u32[]{:S(2)}, u32[]{:S(2)}) collective-permute-start(f32[256,512]{1,0:T(8,128)S(1)} %constant_dynamic-slice_fusion.8), channel_id=1, source_target_pairs={{0,1},{1,0},{2,3},{3,2},{4,5},{5,4},{6,7},{7,6},{8,9},{9,8},{10,11... | collective-permute-start | bytes 1572872 | tf_op jit(solution)/shard_map/ppermute | solution.py:402
Sparse Core Ops, SparseCore 0:
  33.3 84.2 all-gather.3
  134.0 40.1 all-gather.5
  176.1 92.2 all-gather.7

commit v10 on v8

--- a/solution.py
+++ b/solution.py
@@ -357,17 +357,20 @@
     n_mdl = lax.axis_size("mdl")
     x_lo = mdl_index // 2
     core = mdl_index % 2
-    half = partial_out.shape[1] // 2
-    quarter = half // 2
-    mine = lax.dynamic_slice_in_dim(partial_out, x_lo * half, half, 1)
-    theirs = lax.dynamic_slice_in_dim(partial_out, (1 - x_lo) * half, half, 1)
+    quarter = partial_out.shape[1] // 4
+
+    def cols_of(block):
+        return lax.dynamic_slice_in_dim(partial_out, block * quarter, quarter, 1)
+
+    mine = jnp.concatenate([cols_of(core), cols_of(2 + core)], axis=1)
+    theirs = jnp.concatenate([cols_of(1 - core), cols_of(3 - core)], axis=1)
+    pair_sum = mine + lax.ppermute(theirs, "mdl", [(m, m ^ 1) for m in range(n_mdl)])
+    mine = lax.dynamic_slice_in_dim(pair_sum, x_lo * quarter, quarter, 1)
+    theirs = lax.dynamic_slice_in_dim(pair_sum, (1 - x_lo) * quarter, quarter, 1)
     across = lax.ppermute(
         theirs.astype(jnp.bfloat16), "mdl", [(m, m ^ 2) for m in range(n_mdl)]
     )
-    half_sum = mine + across.astype(jnp.float32)
-    mine = lax.dynamic_slice_in_dim(half_sum, core * quarter, quarter, 1)
-    theirs = lax.dynamic_slice_in_dim(half_sum, (1 - core) * quarter, quarter, 1)
-    branch_sum = mine + lax.ppermute(theirs, "mdl", [(m, m ^ 1) for m in range(n_mdl)])
+    branch_sum = mine + across.astype(jnp.float32)
     layer_out = (wide_tokens + branch_sum).astype(jnp.bfloat16)
     return (layer_out, cache_k[None], cache_v[None])
 

time: 342 us -> 338 us (0.988)
  waiting for transfers between devices: 56.2 us -> 49.8 us
    ppermute x1, waiting for transfers between devices: 11 us -> 4.61 us  [body(): lax.ppermute(theirs.astype(jnp.bfloat16), 'mdl', [(m, m ^ 2) for m in ran...]
  transfers between devices with their start and end apart: 7 -> 7, of which waited for: 3 -> 3; matrix products, arithmetic and copies ran while one was open for 5% -> 5% of each run, Pallas kernels for 37% -> 38%
where the time goes in v10:
time: 338 us; the launch traced here: 337 us
  Pallas kernels  127 us (38%)
  blocking collectives  75 us (22%)
  waiting for transfers between devices  49.8 us (15%)
  local copies, waits for them, and re-layouts  21.8 us (6%)
  other arithmetic  19.8 us (6%)
  between operations  19.7 us (6%)
  matrix products  12.2 us (4%)
  loops' own time  8.31 us (2%)
  starting transfers between devices  3.68 us (1%)
    pallas_call x3, Pallas kernels, ring_y_kernel(): pl.pallas_call(_ring_kernel, out_shape=jax.ShapeDtypeStruct((4, rows, wid...  127 us
    all_gather x1, blocking collectives, gather_xh_z(): return lax.all_gather(x, 'z', axis=0, tiled=True)  30.8 us
    all_gather x1, waiting for transfers between devices, body(): v_part = lax.all_gather(kv_pair[:, kv_cols:], 'z', axis=0, tiled=True)  27.4 us
    all_gather x1, waiting for transfers between devices, body(): gathered = lax.all_gather(packed, 'z', axis=0, tiled=True)  17.7 us
    all_gather x1, blocking collectives, body(): packed = lax.all_gather(packed, 'y', axis=0, tiled=True)  15.3 us
    all_gather x1, blocking collectives, body(): lax.all_gather(jnp.concatenate([k_rot, values_flat], axis=1), 'xh', axis=...  10.2 us
    another operation x1, loops' own time, body(): top_now, totals, summed = lax.fori_loop(0, n_needed, key_block, start_state)  8.31 us
    all_gather x1, blocking collectives, body(): packed = lax.all_gather(packed, 'xh', axis=0, tiled=True)  6.89 us
  transfers between devices with their start and end apart: 7, of which 3 were waited for; matrix products, arithmetic and copies ran while one was open for 5% of the time, Pallas kernels for 38%

profile of v10, /device:TPU:72, one launch (start us, length us, event | category | flops | bytes accessed | tf_op | source)
XLA Modules:
  0.0 337.2 jit_solution(10294311276729872691)
XLA Ops:
  11.0 6.9 %all_gather.24 = bf16[64,1664]{1,0:T(8,128)(2,1)S(1)} all-gather(bf16[32,1664]{1,0:T(8,128)(2,1)S(1)} %constant_dynamic-update-slice_fusion), channel_id=1, replica_groups=mesh['z'=8,'y'=4,'xh'=2,'mdl'=4] {'xh'}, dimensions={0}, use_global_device_ids=true | all-gather | bytes 319488 | tf_op jit(solution)/shard_map/all_gather | solution.py:177
  17.9 15.3 %all_gather.25 = bf16[256,1664]{1,0:T(8,128)(2,1)} all-gather(bf16[64,1664]{1,0:T(8,128)(2,1)S(1)} %all_gather.24), channel_id=1, replica_groups=mesh['z'=8,'y'=4,'xh'=2,'mdl'=4] {'y'}, dimensions={0}, use_global_device_ids=true | all-gather | bytes 1064960 | tf_op jit(solution)/shard_map/all_gather | solution.py:178
  33.5 5.7 %psum.7 = f32[256]{0:T(256)S(1)} all-reduce(f32[256]{0:T(256)S(1)} %fusion.29), channel_id=1, replica_groups=mesh['z'=8,'y'=4,'xh'=2,'mdl'=4] {'mdl'}, use_global_device_ids=true, to_apply=%region_12.13 | all-reduce | flops 256 | bytes 2048 | tf_op jit(solution)/shard_map/psum | solution.py:192
  39.4 6.1 %all_gather.27 = bf16[64,512]{1,0:T(8,128)(2,1)S(1)} all-gather(bf16[32,512]{1,0:T(8,128)(2,1)S(1)} %copy-done.3), channel_id=1, replica_groups=mesh['z'=8,'y'=4,'xh'=2,'mdl'=4] {'xh'}, dimensions={0}, use_global_device_ids=true | all-gather | bytes 98304 | tf_op jit(solution)/shard_map/all_gather | solution.py:114
  45.5 30.8 %all_gather.28.x_ref = bf16[512,512]{1,0:T(8,128)(2,1)} all-gather(bf16[64,512]{1,0:T(8,128)(2,1)S(1)} %all_gather.27), channel_id=1, replica_groups=mesh['z'=8,'y'=4,'xh'=2,'mdl'=4] {'z'}, dimensions={0}, use_global_device_ids=true | all-gather | bytes 589824 | tf_op jit(solution)/shard_map/all_gather | solution.py:115
  76.3 17.9 %shard_map.157 = bf16[4,512,512]{2,1,0:T(8,128)(2,1)} custom-call(bf16[512,512]{1,0:T(8,128)(2,1)} %all_gather.28.x_ref), custom_call_target="tpu_custom_call" | custom-call | tf_op jit(solution)/shard_map/pallas_call | solution.py:93
  95.3 1.3 fusion.49
  96.9 1.8 collective-permute-start.1
  99.9 17.7 %all-gather.4.cloned.1.call-done = bf16[2048,1664]{1,0:T(8,128)(2,1)} async-done(((bf16[256,1664]{1,0:T(8,128)(2,1)}), bf16[2048,1664]{1,0:T(8,128)(2,1)}) %all-gather.4.cloned.1.call-update) | async-done | bytes 6815760 | tf_op jit(solution)/shard_map/all_gather | solution.py:181
  117.6 3.4 %fusion.12 = f32[256,1024]{1,0:T(8,128)S(1)} fusion(bf16[2048,1664]{1,0:T(8,128)(2,1)} %all-gather.4.cloned.1.call-done, bf16[256,1024]{1,0:T(8,128)(2,1)S(1)} %collective-permute-done.1, bf16[256,1024]{1,0:T(8,128)(2,1)S(1)} %maximum_select_fusion.3, pred[]{:T(512)S(6)} %eq.177), kind=kOutput, calls=%fused_computation.21 | convolution fusion | flops 1078460416 | bytes 6291457 | tf_op jit(solution)/shard_map/dot_general | solution.py:199
  122.9 10.2 %all_gather.29 = bf16[512,512]{1,0:T(8,128)(2,1)S(1)} all-gather(bf16[256,512]{1,0:T(8,128)(2,1)S(1)} %pad_maximum_fusion.1), channel_id=1, replica_groups=mesh['z'=8,'y'=4,'xh'=2,'mdl'=4] {'xh'}, dimensions={0}, use_global_device_ids=true | all-gather | bytes 786432 | tf_op jit(solution)/shard_map/all_gather | solution.py:237
  134.0 13.0 %shard_map.158 = bf16[4,512,256]{2,1,0:T(8,128)(2,1)} custom-call(bf16[512,256]{1,0:T(8,128)(2,1)} %get-tuple-element.410.x_ref), custom_call_target="tpu_custom_call" | custom-call | tf_op jit(solution)/shard_map/pallas_call | solution.py:93
  147.0 27.4 %all-gather.6.cloned.1.call-done.x_ref = bf16[4096,256]{1,0:T(8,128)(2,1)} async-done(((bf16[512,256]{1,0:T(8,128)(2,1)}), bf16[4096,256]{1,0:T(8,128)(2,1)}) %all-gather.6.cloned.1.call-update) | async-done | bytes 2097168 | tf_op jit(solution)/shard_map/all_gather | solution.py:238
  183.4 1.2 slice_compare_fusion
  186.8 96.1 %shard_map.159 = bf16[4,4096,256]{2,1,0:T(8,128)(2,1)} custom-call(bf16[4096,256]{1,0:T(8,128)(2,1)} %all-gather.6.cloned.1.call-done.x_ref), custom_call_target="tpu_custom_call" | custom-call | tf_op jit(solution)/shard_map/pallas_call | solution.py:93
  283.0 24.0 %while.18 = (s32[]{:T(128)}, f32[256,2,2]{0,2,1:T(2,128)S(1)}, f32[256,2,2]{0,2,1:T(2,128)S(1)}, f32[256,2,2,128]{0,3,2,1:T(8,128)S(1)}, s32[]{:T(128)}, /*index...) while((s32[]{:T(128)}, f32[256,2,2]{0,2,1:T(2,128)S(1)}, ...), condition=%wide.region_21.22_spmd.clone, body=%wide.region_18.21_spmd.clone.sunk | while | flops 137300576 | bytes 6105339 | solution.py:327
  307.9 1.2 copy.88
  309.2 4.7 %fusion.14 = f32[256,2048]{1,0:T(8,128)} fusion(bf16[2048,1664]{1,0:T(8,128)(2,1)} %all-gather.4.cloned.1.call-done, f32[256,512]{1,0:T(8,128)S(1)} %copy.88, bf16[256,2048]{0,1:T(8,128)(2,1)} %bitcast.81, bf16[2048,512]{1,0:T(8,128)(2,1)S(1)} %bitcast.76), kind=kOutput, calls=%fused_computation.27 | convolution fusion | flops 1074397184 | bytes 7864320 | tf_op jit(solution)/shard_map/dot_general | solution.py:350
  313.9 1.7 constant_dynamic-slice_fusion.11
  318.5 1.2 fusion.43
  319.7 1.2 constant_dynamic-slice_fusion.2
  321.1 1.6 collective-permute-start.3
  323.8 1.4 fusion.36
  325.2 4.6 %collective-permute-done.3 = bf16[256,512]{1,0:T(8,128)(2,1)S(1)} collective-permute-done((bf16[256,512]{1,0:T(8,128)(2,1)S(1)}, bf16[256,512]{1,0:T(8,128)(2,1)S(1)}, u32[]{:S(2)}, u32[]{:S(2)}) %collective-permute-start.3) | collective-permute-done | bytes 262176 | tf_op jit(solution)/shard_map/ppermute | solution.py:370
  (175 shorter events, 36.7 us)
Async XLA Ops:
  7.2 32.2 %copy-start.3 = (bf16[32,512]{1,0:T(8,128)(2,1)S(1)}, bf16[32,512]{1,0:T(8,128)(2,1)}, u32[]{:S(2)}) copy-start(bf16[32,512]{1,0:T(8,128)(2,1)} %param.21) | copy-start | bytes 98308
  7.2 26.1 %copy-start.5 = (bf16[512]{0:T(512)(128)(2,1)S(1)}, bf16[512]{0:T(512)(128)(2,1)}, u32[]{:S(2)}) copy-start(bf16[512]{0:T(512)(128)(2,1)} %param.17) | copy-start | bytes 3076
  7.2 26.1 %copy-start = (bf16[256,512]{1,0:T(8,128)(2,1)S(1)}, bf16[256,512]{1,0:T(8,128)(2,1)}, u32[]{:S(2)}) copy-start(bf16[256,512]{1,0:T(8,128)(2,1)} %param.16) | copy-start | bytes 786436
  7.2 110.4 %all-gather.4.cloned.1.call-start = ((), (), s32[]{:S(2)}) async-start(), calls=%async_computation | async-start | bytes 7667712 | tf_op jit(solution)/shard_map/all_gather | solution.py:181
  33.2 61.0 %copy-start.4 = (s32[64]{0:T(128)S(1)}, s32[64]{0:T(128)}, u32[]{:S(2)}) copy-start(s32[64]{0:T(128)} %param.25) | copy-start | bytes 772
  33.2 141.2 %all-gather.6.cloned.1.call-start = ((), (), s32[]{:S(2)}) async-start(), calls=%async_computation.1 | async-start | bytes 2359296 | tf_op jit(solution)/shard_map/all_gather | solution.py:238
  33.3 61.3 %copy-start.9 = (s32[64]{0:T(128)S(1)}, s32[64]{0:T(128)}, u32[]{:S(2)}) copy-start(s32[64]{0:T(128)} %param.29) | copy-start | bytes 772
  33.3 61.9 %copy-start.6 = (s32[4,2]{0,1:T(2,128)S(1)}, s32[4,2]{0,1:T(2,128)}, u32[]{:S(2)}) copy-start(s32[4,2]{0,1:T(2,128)} %param.27) | copy-start | bytes 100
  33.5 63.2 %copy-start.2 = (s32[256]{0:T(256)S(1)}, s32[256]{0:T(256)}, u32[]{:S(2)}) copy-start(s32[256]{0:T(256)} %param.26) | copy-start | bytes 3076
  39.3 57.5 %collective-permute-start = (bf16[256,512]{1,0:T(8,128)(2,1)S(1)}, bf16[256,512]{1,0:T(8,128)(2,1)S(1)}, u32[]{:S(2)}, u32[]{:S(2)}) collective-permute-start(bf16[256,512]{1,0:T(8,128)(2,1)S(1)} %fusion.31), channel_id=1, source_target_pairs={{0,1},{1,0},{2,3},{3,2},{4,5},{5,4},{6,7},{7,6},{8,9},{9,8},{10,11... | collective-permute-start | bytes 786440 | tf_op jit(solution)/shard_map/ppermute | solution.py:134
  96.9 20.7 %collective-permute-start.1 = (bf16[256,1024]{1,0:T(8,128)(2,1)S(1)}, bf16[256,1024]{1,0:T(8,128)(2,1)S(1)}, u32[]{:S(2)}, u32[]{:S(2)}) collective-permute-start(bf16[256,1024]{1,0:T(8,128)(2,1)S(1)} %maximum_select_fusion.3), channel_id=1, source_target_pairs={{0,2},{1,3},{2,0},{3,1},{4,6},{5,7},{6,4},{7,5},{8,10},{9,11},{10,... | collective-permute-start | bytes 1572872 | tf_op jit(solution)/shard_map/ppermute | solution.py:140
  99.9 21.7 %copy-start.8 = (f32[128]{0:T(128)S(1)}, f32[128]{0:T(128)}, u32[]{:S(2)}) copy-start(f32[128]{0:T(128)} %param.23) | copy-start | bytes 1540
  134.0 148.9 %all-gather.8.cloned.1.call-start = ((), (), s32[]{:S(2)}) async-start(), calls=%async_computation.2 | async-start | bytes 9437184 | tf_op jit(solution)/shard_map/all_gather | solution.py:241
  183.3 2.3 copy-start.7
  307.0 2.2 copy-start.1
  315.7 5.1 %collective-permute-start.2 = (f32[256,1024]{1,0:T(8,128)S(1)}, f32[256,1024]{1,0:T(8,128)S(1)}, u32[]{:S(2)}, u32[]{:S(2)}) collective-permute-start(f32[256,1024]{1,0:T(8,128)S(1)} %pad_maximum_fusion), channel_id=1, source_target_pairs={{0,1},{1,0},{2,3},{3,2},{4,5},{5,4},{6,7},{7,6},{8,9},{9,8},{10,11... | collective-permute-start | bytes 3145736 | tf_op jit(solution)/shard_map/ppermute | solution.py:367
  321.1 8.8 %collective-permute-start.3 = (bf16[256,512]{1,0:T(8,128)(2,1)S(1)}, bf16[256,512]{1,0:T(8,128)(2,1)S(1)}, u32[]{:S(2)}, u32[]{:S(2)}) collective-permute-start(bf16[256,512]{1,0:T(8,128)(2,1)S(1)} %dynamic-slice_convert_fusion), channel_id=1, source_target_pairs={{0,2},{1,3},{2,0},{3,1},{4,6},{5,7},{6,4},{7,5},{8,10},{9,11},{10,... | collective-permute-start | bytes 786440 | tf_op jit(solution)/shard_map/ppermute | solution.py:370
Sparse Core Ops, SparseCore 0:
  33.3 84.2 all-gather.3
  134.1 40.2 all-gather.5
  176.2 92.1 all-gather.7

commit v11 on v10

--- a/solution.py
+++ b/solution.py
@@ -189,7 +189,14 @@
 
     wide_tokens = tokens.astype(jnp.float32)
     full_width = tokens.shape[1] * lax.axis_size("mdl")
-    square_total = lax.psum(jnp.sum(wide_tokens * wide_tokens, axis=1), "mdl")
+    square_part = jnp.sum(wide_tokens * wide_tokens, axis=1)
+    n_mdl_in = lax.axis_size("mdl")
+    square_part = square_part + lax.ppermute(
+        square_part, "mdl", [(m, m ^ 1) for m in range(n_mdl_in)]
+    )
+    square_total = square_part + lax.ppermute(
+        square_part, "mdl", [(m, m ^ 2) for m in range(n_mdl_in)]
+    )
     scaled = (
         wide_tokens
         * lax.rsqrt(square_total / full_width + epsilon)[:, None]

time: 338 us -> 337 us (level); the launches traced: 337 us -> 332 us
  blocking collectives: 75 us -> 69.2 us
  waiting for transfers between devices: 49.8 us -> 53.9 us
    psum x1 -> x0, blocking collectives: 5.67 us -> none  [body(): square_total = lax.psum(jnp.sum(wide_tokens * wide_tokens, axis=1), 'mdl')]
  transfers between devices with their start and end apart: 7 -> 9, of which waited for: 3 -> 4; matrix products, arithmetic and copies ran while one was open for 5% -> 6% of each run, Pallas kernels for 38% -> 38%
where the time goes in v11:
time: 337 us; the launch traced here: 332 us
  Pallas kernels  127 us (38%)
  blocking collectives  69.2 us (21%)
  waiting for transfers between devices  53.9 us (16%)
  local copies, waits for them, and re-layouts  19.8 us (6%)
  between operations  19.7 us (6%)
  other arithmetic  19.6 us (6%)
  matrix products  11.4 us (3%)
  loops' own time  6.63 us (2%)
  starting transfers between devices  4.17 us (1%)
    pallas_call x3, Pallas kernels, ring_y_kernel(): pl.pallas_call(_ring_kernel, out_shape=jax.ShapeDtypeStruct((4, rows, wid...  127 us
    all_gather x1, blocking collectives, gather_xh_z(): return lax.all_gather(x, 'z', axis=0, tiled=True)  30.7 us
    all_gather x1, waiting for transfers between devices, body(): v_part = lax.all_gather(kv_pair[:, kv_cols:], 'z', axis=0, tiled=True)  27.2 us
    all_gather x1, waiting for transfers between devices, body(): gathered = lax.all_gather(packed, 'z', axis=0, tiled=True)  20.5 us
    all_gather x1, blocking collectives, body(): packed = lax.all_gather(packed, 'y', axis=0, tiled=True)  15.3 us
    all_gather x1, blocking collectives, body(): lax.all_gather(jnp.concatenate([k_rot, values_flat], axis=1), 'xh', axis=...  10.2 us
    all_gather x1, blocking collectives, body(): packed = lax.all_gather(packed, 'xh', axis=0, tiled=True)  6.89 us
  transfers between devices with their start and end apart: 9, of which 4 were waited for; matrix products, arithmetic and copies ran while one was open for 6% of the time, Pallas kernels for 38%

profile of v11, /device:TPU:72, one launch (start us, length us, event | category | flops | bytes accessed | tf_op | source)
XLA Modules:
  0.0 331.5 jit_solution(14092445832275822662)
XLA Ops:
  11.0 6.9 %all_gather.24 = bf16[64,1664]{1,0:T(8,128)(2,1)S(1)} all-gather(bf16[32,1664]{1,0:T(8,128)(2,1)S(1)} %constant_dynamic-update-slice_fusion), channel_id=1, replica_groups=mesh['z'=8,'y'=4,'xh'=2,'mdl'=4] {'xh'}, dimensions={0}, use_global_device_ids=true | all-gather | bytes 319488 | tf_op jit(solution)/shard_map/all_gather | solution.py:177
  17.9 15.3 %all_gather.25 = bf16[256,1664]{1,0:T(8,128)(2,1)} all-gather(bf16[64,1664]{1,0:T(8,128)(2,1)S(1)} %all_gather.24), channel_id=1, replica_groups=mesh['z'=8,'y'=4,'xh'=2,'mdl'=4] {'y'}, dimensions={0}, use_global_device_ids=true | all-gather | bytes 1064960 | tf_op jit(solution)/shard_map/all_gather | solution.py:178
  33.9 6.1 %all_gather.27 = bf16[64,512]{1,0:T(8,128)(2,1)S(1)} all-gather(bf16[32,512]{1,0:T(8,128)(2,1)S(1)} %copy-done.3), channel_id=1, replica_groups=mesh['z'=8,'y'=4,'xh'=2,'mdl'=4] {'xh'}, dimensions={0}, use_global_device_ids=true | all-gather | bytes 98304 | tf_op jit(solution)/shard_map/all_gather | solution.py:114
  40.6 1.3 fusion.49
  41.9 30.7 %all_gather.28.x_ref = bf16[512,512]{1,0:T(8,128)(2,1)} all-gather(bf16[64,512]{1,0:T(8,128)(2,1)S(1)} %all_gather.27), channel_id=1, replica_groups=mesh['z'=8,'y'=4,'xh'=2,'mdl'=4] {'z'}, dimensions={0}, use_global_device_ids=true | all-gather | bytes 589824 | tf_op jit(solution)/shard_map/all_gather | solution.py:115
  72.8 1.6 collective-permute-start.1
  74.3 18.6 %shard_map.157 = bf16[4,512,512]{2,1,0:T(8,128)(2,1)} custom-call(bf16[512,512]{1,0:T(8,128)(2,1)} %all_gather.28.x_ref), custom_call_target="tpu_custom_call" | custom-call | tf_op jit(solution)/shard_map/pallas_call | solution.py:93
  93.4 1.4 collective-permute-done.2
  96.8 20.5 %all-gather.4.cloned.1.call-done = bf16[2048,1664]{1,0:T(8,128)(2,1)} async-done(((bf16[256,1664]{1,0:T(8,128)(2,1)}), bf16[2048,1664]{1,0:T(8,128)(2,1)}) %all-gather.4.cloned.1.call-update) | async-done | bytes 6815760 | tf_op jit(solution)/shard_map/all_gather | solution.py:181
  117.3 3.4 %fusion.12 = f32[256,1024]{1,0:T(8,128)S(1)} fusion(bf16[2048,1664]{1,0:T(8,128)(2,1)} %all-gather.4.cloned.1.call-done, bf16[256,1024]{1,0:T(8,128)(2,1)S(1)} %collective-permute-done.3, bf16[256,1024]{1,0:T(8,128)(2,1)S(1)} %maximum_select_fusion.3, pred[]{:T(512)S(6)} %eq.177), kind=kOutput, calls=%fused_computation.21 | convolution fusion | flops 1078460416 | bytes 6291457 | tf_op jit(solution)/shard_map/dot_general | solution.py:206
  122.6 10.2 %all_gather.29 = bf16[512,512]{1,0:T(8,128)(2,1)S(1)} all-gather(bf16[256,512]{1,0:T(8,128)(2,1)S(1)} %pad_maximum_fusion.1), channel_id=1, replica_groups=mesh['z'=8,'y'=4,'xh'=2,'mdl'=4] {'xh'}, dimensions={0}, use_global_device_ids=true | all-gather | bytes 786432 | tf_op jit(solution)/shard_map/all_gather | solution.py:244
  133.7 12.6 %shard_map.158 = bf16[4,512,256]{2,1,0:T(8,128)(2,1)} custom-call(bf16[512,256]{1,0:T(8,128)(2,1)} %get-tuple-element.410.x_ref), custom_call_target="tpu_custom_call" | custom-call | tf_op jit(solution)/shard_map/pallas_call | solution.py:93
  146.3 27.2 %all-gather.6.cloned.1.call-done.x_ref = bf16[4096,256]{1,0:T(8,128)(2,1)} async-done(((bf16[512,256]{1,0:T(8,128)(2,1)}), bf16[4096,256]{1,0:T(8,128)(2,1)}) %all-gather.6.cloned.1.call-update) | async-done | bytes 2097168 | tf_op jit(solution)/shard_map/all_gather | solution.py:245
  177.0 1.2 scatter_custom_fusion
  182.7 1.2 slice_compare_fusion
  186.1 95.9 %shard_map.159 = bf16[4,4096,256]{2,1,0:T(8,128)(2,1)} custom-call(bf16[4096,256]{1,0:T(8,128)(2,1)} %all-gather.6.cloned.1.call-done.x_ref), custom_call_target="tpu_custom_call" | custom-call | tf_op jit(solution)/shard_map/pallas_call | solution.py:93
  282.1 19.2 %while.18 = (s32[]{:T(128)}, f32[256,2,2]{0,2,1:T(2,128)S(1)}, f32[256,2,2]{0,2,1:T(2,128)S(1)}, f32[256,2,2,128]{0,3,2,1:T(8,128)S(1)}, s32[]{:T(128)}, /*index...) while((s32[]{:T(128)}, f32[256,2,2]{0,2,1:T(2,128)S(1)}, ...), condition=%wide.region_20.21_spmd.clone, body=%wide.region_17.20_spmd.clone.sunk | while | flops 137300576 | bytes 6105339 | solution.py:334
  302.2 1.2 copy.88
  303.5 4.7 %fusion.14 = f32[256,2048]{1,0:T(8,128)} fusion(bf16[2048,1664]{1,0:T(8,128)(2,1)} %all-gather.4.cloned.1.call-done, f32[256,512]{1,0:T(8,128)S(1)} %copy.88, bf16[256,2048]{0,1:T(8,128)(2,1)} %bitcast.81, bf16[2048,512]{1,0:T(8,128)(2,1)S(1)} %bitcast.76), kind=kOutput, calls=%fused_computation.27 | convolution fusion | flops 1074397184 | bytes 7864320 | tf_op jit(solution)/shard_map/dot_general | solution.py:357
  308.2 1.7 constant_dynamic-slice_fusion.11
  312.8 1.2 fusion.43
  315.4 1.6 collective-permute-start.5
  318.1 1.4 fusion.36
  319.5 4.7 %collective-permute-done.5 = bf16[256,512]{1,0:T(8,128)(2,1)S(1)} collective-permute-done((bf16[256,512]{1,0:T(8,128)(2,1)S(1)}, bf16[256,512]{1,0:T(8,128)(2,1)S(1)}, u32[]{:S(2)}, u32[]{:S(2)}) %collective-permute-start.5) | collective-permute-done | bytes 262176 | tf_op jit(solution)/shard_map/ppermute | solution.py:377
  (166 shorter events, 34.5 us)
Async XLA Ops:
  7.2 26.7 %copy-start.3 = (bf16[32,512]{1,0:T(8,128)(2,1)S(1)}, bf16[32,512]{1,0:T(8,128)(2,1)}, u32[]{:S(2)}) copy-start(bf16[32,512]{1,0:T(8,128)(2,1)} %param.21) | copy-start | bytes 98308
  7.2 26.1 %copy-start = (bf16[256,512]{1,0:T(8,128)(2,1)S(1)}, bf16[256,512]{1,0:T(8,128)(2,1)}, u32[]{:S(2)}) copy-start(bf16[256,512]{1,0:T(8,128)(2,1)} %param.16) | copy-start | bytes 786436
  7.2 26.3 %copy-start.4 = (s32[64]{0:T(128)S(1)}, s32[64]{0:T(128)}, u32[]{:S(2)}) copy-start(s32[64]{0:T(128)} %param.25) | copy-start | bytes 772
  7.2 32.8 %copy-start.9 = (s32[64]{0:T(128)S(1)}, s32[64]{0:T(128)}, u32[]{:S(2)}) copy-start(s32[64]{0:T(128)} %param.29) | copy-start | bytes 772
  7.2 33.4 %copy-start.6 = (s32[4,2]{0,1:T(2,128)S(1)}, s32[4,2]{0,1:T(2,128)}, u32[]{:S(2)}) copy-start(s32[4,2]{0,1:T(2,128)} %param.27) | copy-start | bytes 100
  7.2 110.1 %all-gather.4.cloned.1.call-start = ((), (), s32[]{:S(2)}) async-start(), calls=%async_computation | async-start | bytes 7667712 | tf_op jit(solution)/shard_map/all_gather | solution.py:181
  33.2 59.7 %copy-start.5 = (bf16[512]{0:T(512)(128)(2,1)S(1)}, bf16[512]{0:T(512)(128)(2,1)}, u32[]{:S(2)}) copy-start(bf16[512]{0:T(512)(128)(2,1)} %param.17) | copy-start | bytes 3076
  33.2 140.4 %all-gather.6.cloned.1.call-start = ((), (), s32[]{:S(2)}) async-start(), calls=%async_computation.1 | async-start | bytes 2359296 | tf_op jit(solution)/shard_map/all_gather | solution.py:245
  33.4 59.8 %copy-start.2 = (s32[256]{0:T(256)S(1)}, s32[256]{0:T(256)}, u32[]{:S(2)}) copy-start(s32[256]{0:T(256)} %param.26) | copy-start | bytes 3076
  33.4 39.3 %collective-permute-start = (f32[256]{0:T(256)S(1)}, f32[256]{0:T(256)S(1)}, u32[]{:S(2)}, u32[]{:S(2)}) collective-permute-start(f32[256]{0:T(256)S(1)} %fusion.29), channel_id=1, source_target_pairs={{0,1},{1,0},{2,3},{3,2},{4,5},{5,4},{6,7},{7,6},{8,9},{9,8},{10,11... | collective-permute-start | bytes 3080 | tf_op jit(solution)/shard_map/ppermute | solution.py:194
  72.8 20.2 %collective-permute-start.1 = (f32[256]{0:T(256)S(1)}, f32[256]{0:T(256)S(1)}, u32[]{:S(2)}, u32[]{:S(2)}) collective-permute-start(f32[256]{0:T(256)S(1)} %add.479), channel_id=1, source_target_pairs={{0,2},{1,3},{2,0},{3,1},{4,6},{5,7},{6,4},{7,5},{8,10},{9,11},{10,... | collective-permute-start | bytes 3080 | tf_op jit(solution)/shard_map/ppermute | solution.py:197
  93.1 1.6 collective-permute-start.2
  94.9 22.4 %collective-permute-start.3 = (bf16[256,1024]{1,0:T(8,128)(2,1)S(1)}, bf16[256,1024]{1,0:T(8,128)(2,1)S(1)}, u32[]{:S(2)}, u32[]{:S(2)}) collective-permute-start(bf16[256,1024]{1,0:T(8,128)(2,1)S(1)} %maximum_select_fusion.3), channel_id=1, source_target_pairs={{0,2},{1,3},{2,0},{3,1},{4,6},{5,7},{6,4},{7,5},{8,10},{9,11},{10,... | collective-permute-start | bytes 1572872 | tf_op jit(solution)/shard_map/ppermute | solution.py:140
  96.7 24.6 %copy-start.8 = (f32[128]{0:T(128)S(1)}, f32[128]{0:T(128)}, u32[]{:S(2)}) copy-start(f32[128]{0:T(128)} %param.23) | copy-start | bytes 1540
  133.6 148.4 %all-gather.8.cloned.1.call-start = ((), (), s32[]{:S(2)}) async-start(), calls=%async_computation.2 | async-start | bytes 9437184 | tf_op jit(solution)/shard_map/all_gather | solution.py:248
  182.6 2.3 copy-start.7
  301.3 2.2 copy-start.1
  310.0 5.1 %collective-permute-start.4 = (f32[256,1024]{1,0:T(8,128)S(1)}, f32[256,1024]{1,0:T(8,128)S(1)}, u32[]{:S(2)}, u32[]{:S(2)}) collective-permute-start(f32[256,1024]{1,0:T(8,128)S(1)} %pad_maximum_fusion), channel_id=1, source_target_pairs={{0,1},{1,0},{2,3},{3,2},{4,5},{5,4},{6,7},{7,6},{8,9},{9,8},{10,11... | collective-permute-start | bytes 3145736 | tf_op jit(solution)/shard_map/ppermute | solution.py:374
  315.4 8.8 %collective-permute-start.5 = (bf16[256,512]{1,0:T(8,128)(2,1)S(1)}, bf16[256,512]{1,0:T(8,128)(2,1)S(1)}, u32[]{:S(2)}, u32[]{:S(2)}) collective-permute-start(bf16[256,512]{1,0:T(8,128)(2,1)S(1)} %dynamic-slice_convert_fusion), channel_id=1, source_target_pairs={{0,2},{1,3},{2,0},{3,1},{4,6},{5,7},{6,4},{7,5},{8,10},{9,11},{10,... | collective-permute-start | bytes 786440 | tf_op jit(solution)/shard_map/ppermute | solution.py:377
Sparse Core Ops, SparseCore 0:
  33.3 83.9 all-gather.3
  133.8 39.7 all-gather.5
  175.4 92.1 all-gather.7

commit v12 on v11

--- a/solution.py
+++ b/solution.py
@@ -110,8 +110,17 @@
     return x
 
 
+def gather_xh(x):
+    other = lax.ppermute(x, "xh", [(0, 1), (1, 0)])
+    return jnp.where(
+        lax.axis_index("xh") == 0,
+        jnp.concatenate([x, other], axis=0),
+        jnp.concatenate([other, x], axis=0),
+    )
+
+
 def gather_xh_z(x):
-    x = lax.all_gather(x, "xh", axis=0, tiled=True)
+    x = gather_xh(x)
     return lax.all_gather(x, "z", axis=0, tiled=True)
 
 
@@ -174,7 +183,7 @@
     mask_block = key_mask.astype(jnp.bfloat16).reshape(weight_rows, mask_cols)
     mask_block = jnp.pad(mask_block, ((0, 0), (0, 128 - mask_cols)))
     packed = jnp.concatenate([w_query, key_matrix, value_matrix, w_out.T, mask_block], axis=1)
-    packed = lax.all_gather(packed, "xh", axis=0, tiled=True)
+    packed = gather_xh(packed)
     packed = lax.all_gather(packed, "y", axis=0, tiled=True)
     packed, gate_in = lax.optimization_barrier((packed, w_gate))
     gate_ring = ring_y_kernel(gather_xh_z(gate_in), 1)
@@ -241,7 +250,7 @@
         .reshape(local_rows, kv_cols)
     )
     values_flat = values_raw.astype(jnp.bfloat16)
-    kv_pair = lax.all_gather(jnp.concatenate([k_rot, values_flat], axis=1), "xh", axis=0, tiled=True)
+    kv_pair = gather_xh(jnp.concatenate([k_rot, values_flat], axis=1))
     v_part = lax.all_gather(kv_pair[:, kv_cols:], "z", axis=0, tiled=True)
     k_part = ring_y_kernel(kv_pair[:, :kv_cols], 2).reshape(-1, kv_cols)
     k_part, v_part = lax.optimization_barrier((k_part, v_part))

time: 337 us -> 337 us (level)
  the two profiles are of different devices: /device:TPU:72 before, /device:TPU:94 now
where the time goes in v12:
time: 337 us; the launch traced here: 336 us
  Pallas kernels  126 us (37%)
  waiting for transfers between devices  75 us (22%)
  blocking collectives  45.9 us (14%)
  local copies, waits for them, and re-layouts  21.7 us (6%)
  other arithmetic  20.3 us (6%)
  between operations  19.7 us (6%)
  matrix products  12.2 us (4%)
  loops' own time  8.13 us (2%)
  starting transfers between devices  6.99 us (2%)
    pallas_call x3, Pallas kernels, ring_y_kernel(): pl.pallas_call(_ring_kernel, out_shape=jax.ShapeDtypeStruct((4, rows, wid...  126 us
    all_gather x1, blocking collectives, gather_xh_z(): return lax.all_gather(x, 'z', axis=0, tiled=True)  30.9 us
    all_gather x1, waiting for transfers between devices, body(): v_part = lax.all_gather(kv_pair[:, kv_cols:], 'z', axis=0, tiled=True)  28.1 us
    all_gather x1, waiting for transfers between devices, body(): gathered = lax.all_gather(packed, 'z', axis=0, tiled=True)  23 us
    ppermute x3, waiting for transfers between devices, gather_xh(): other = lax.ppermute(x, 'xh', [(0, 1), (1, 0)])  15.9 us
    all_gather x1, blocking collectives, body(): packed = lax.all_gather(packed, 'y', axis=0, tiled=True)  15 us
    another operation x1, loops' own time, body(): top_now, totals, summed = lax.fori_loop(0, n_needed, key_block, start_state)  8.13 us
  transfers between devices with their start and end apart: 12, of which 7 were waited for; matrix products, arithmetic and copies ran while one was open for 6% of the time, Pallas kernels for 38%

profile of v12, /device:TPU:94, one launch (start us, length us, event | category | flops | bytes accessed | tf_op | source)
XLA Modules:
  0.0 336.0 jit_solution(2143569731281466891)
XLA Ops:
  11.1 1.5 collective-permute-start
  12.6 4.8 %collective-permute-done = bf16[32,1664]{1,0:T(8,128)(2,1)S(1)} collective-permute-done((bf16[32,1664]{1,0:T(8,128)(2,1)S(1)}, bf16[32,1664]{1,0:T(8,128)(2,1)S(1)}, u32[]{:S(2)}, u32[]{:S(2)}) %collective-permute-start) | collective-permute-done | bytes 106528 | tf_op jit(solution)/shard_map/ppermute | solution.py:114
  17.4 15.0 %all_gather.15 = bf16[256,1664]{1,0:T(8,128)(2,1)} all-gather(bf16[64,1664]{1,0:T(8,128)(2,1)S(1)} %maximum_select_fusion.6), channel_id=1, replica_groups=mesh['z'=8,'y'=4,'xh'=2,'mdl'=4] {'y'}, dimensions={0}, use_global_device_ids=true | all-gather | bytes 1064960 | tf_op jit(solution)/shard_map/all_gather | solution.py:187
  33.9 1.3 fusion.49
  36.2 2.6 collective-permute-done.3
  39.8 1.4 collective-permute-start.1
  42.2 3.0 collective-permute-done.1
  45.2 30.9 %all_gather.17.x_ref = bf16[512,512]{1,0:T(8,128)(2,1)} all-gather(bf16[64,512]{1,0:T(8,128)(2,1)S(1)} %maximum_select_fusion.7), channel_id=1, replica_groups=mesh['z'=8,'y'=4,'xh'=2,'mdl'=4] {'z'}, dimensions={0}, use_global_device_ids=true | all-gather | bytes 589824 | tf_op jit(solution)/shard_map/all_gather | solution.py:124
  76.1 17.8 %shard_map.157 = bf16[4,512,512]{2,1,0:T(8,128)(2,1)} custom-call(bf16[512,512]{1,0:T(8,128)(2,1)} %all_gather.17.x_ref), custom_call_target="tpu_custom_call" | custom-call | tf_op jit(solution)/shard_map/pallas_call | solution.py:93
  93.9 23.0 %all-gather.4.cloned.1.call-done = bf16[2048,1664]{1,0:T(8,128)(2,1)} async-done(((bf16[256,1664]{1,0:T(8,128)(2,1)}), bf16[2048,1664]{1,0:T(8,128)(2,1)}) %all-gather.4.cloned.1.call-update) | async-done | bytes 6815760 | tf_op jit(solution)/shard_map/all_gather | solution.py:190
  116.9 3.4 %fusion.12 = f32[256,1024]{1,0:T(8,128)S(1)} fusion(bf16[2048,1664]{1,0:T(8,128)(2,1)} %all-gather.4.cloned.1.call-done, bf16[256,1024]{1,0:T(8,128)(2,1)S(1)} %collective-permute-done.5, bf16[256,1024]{1,0:T(8,128)(2,1)S(1)} %maximum_select_fusion.3, pred[]{:T(512)S(6)} %eq.183), kind=kOutput, calls=%fused_computation.21 | convolution fusion | flops 1078460416 | bytes 6291457 | tf_op jit(solution)/shard_map/dot_general | solution.py:215
  122.2 1.5 collective-permute-start.6
  123.7 8.1 %collective-permute-done.6 = bf16[256,512]{1,0:T(8,128)(2,1)S(1)} collective-permute-done((bf16[256,512]{1,0:T(8,128)(2,1)S(1)}, bf16[256,512]{1,0:T(8,128)(2,1)S(1)}, u32[]{:S(2)}, u32[]{:S(2)}) %collective-permute-start.6) | collective-permute-done | bytes 262176 | tf_op jit(solution)/shard_map/ppermute | solution.py:114
  132.9 12.3 %shard_map.158 = bf16[4,512,256]{2,1,0:T(8,128)(2,1)} custom-call(bf16[512,256]{1,0:T(8,128)(2,1)} %get-tuple-element.410.x_ref), custom_call_target="tpu_custom_call" | custom-call | tf_op jit(solution)/shard_map/pallas_call | solution.py:93
  145.2 28.1 %all-gather.6.cloned.1.call-done.x_ref = bf16[4096,256]{1,0:T(8,128)(2,1)} async-done(((bf16[512,256]{1,0:T(8,128)(2,1)}), bf16[4096,256]{1,0:T(8,128)(2,1)}) %all-gather.6.cloned.1.call-update) | async-done | bytes 2097168 | tf_op jit(solution)/shard_map/all_gather | solution.py:254
  182.5 1.2 slice_compare_fusion
  185.9 95.9 %shard_map.159 = bf16[4,4096,256]{2,1,0:T(8,128)(2,1)} custom-call(bf16[4096,256]{1,0:T(8,128)(2,1)} %all-gather.6.cloned.1.call-done.x_ref), custom_call_target="tpu_custom_call" | custom-call | tf_op jit(solution)/shard_map/pallas_call | solution.py:93
  281.9 23.8 %while.18 = (s32[]{:T(128)}, f32[256,2,2]{0,2,1:T(2,128)S(1)}, f32[256,2,2]{0,2,1:T(2,128)S(1)}, f32[256,2,2,128]{0,3,2,1:T(8,128)S(1)}, s32[]{:T(128)}, /*index...) while((s32[]{:T(128)}, f32[256,2,2]{0,2,1:T(2,128)S(1)}, ...), condition=%wide.region_20.21_spmd.clone, body=%wide.region_17.20_spmd.clone.sunk | while | flops 137300576 | bytes 6105339 | solution.py:343
  306.7 1.2 copy.88
  307.9 4.7 %fusion.14 = f32[256,2048]{1,0:T(8,128)} fusion(bf16[2048,1664]{1,0:T(8,128)(2,1)} %all-gather.4.cloned.1.call-done, f32[256,512]{1,0:T(8,128)S(1)} %copy.88, bf16[256,2048]{0,1:T(8,128)(2,1)} %bitcast.83, bf16[2048,512]{1,0:T(8,128)(2,1)S(1)} %bitcast.76), kind=kOutput, calls=%fused_computation.27 | convolution fusion | flops 1074397184 | bytes 7864320 | tf_op jit(solution)/shard_map/dot_general | solution.py:366
  312.7 1.7 constant_dynamic-slice_fusion.11
  317.3 1.2 fusion.43
  321.9 1.4 fusion.36
  323.3 5.3 %collective-permute-done.8 = bf16[256,512]{1,0:T(8,128)(2,1)S(1)} collective-permute-done((bf16[256,512]{1,0:T(8,128)(2,1)S(1)}, bf16[256,512]{1,0:T(8,128)(2,1)S(1)}, u32[]{:S(2)}, u32[]{:S(2)}) %collective-permute-start.8) | collective-permute-done | bytes 262176 | tf_op jit(solution)/shard_map/ppermute | solution.py:386
  (185 shorter events, 40.6 us)
Async XLA Ops:
  7.2 32.6 %copy-start.3 = (bf16[32,512]{1,0:T(8,128)(2,1)S(1)}, bf16[32,512]{1,0:T(8,128)(2,1)}, u32[]{:S(2)}) copy-start(bf16[32,512]{1,0:T(8,128)(2,1)} %param.21) | copy-start | bytes 98308
  7.2 25.4 %copy-start = (bf16[256,512]{1,0:T(8,128)(2,1)S(1)}, bf16[256,512]{1,0:T(8,128)(2,1)}, u32[]{:S(2)}) copy-start(bf16[256,512]{1,0:T(8,128)(2,1)} %param.16) | copy-start | bytes 786436
  7.2 25.6 %copy-start.4 = (s32[64]{0:T(128)S(1)}, s32[64]{0:T(128)}, u32[]{:S(2)}) copy-start(s32[64]{0:T(128)} %param.25) | copy-start | bytes 772
  7.2 25.9 %copy-start.9 = (s32[64]{0:T(128)S(1)}, s32[64]{0:T(128)}, u32[]{:S(2)}) copy-start(s32[64]{0:T(128)} %param.29) | copy-start | bytes 772
  7.2 26.6 %copy-start.6 = (s32[4,2]{0,1:T(2,128)S(1)}, s32[4,2]{0,1:T(2,128)}, u32[]{:S(2)}) copy-start(s32[4,2]{0,1:T(2,128)} %param.27) | copy-start | bytes 100
  7.2 28.9 %copy-start.2 = (s32[256]{0:T(256)S(1)}, s32[256]{0:T(256)}, u32[]{:S(2)}) copy-start(s32[256]{0:T(256)} %param.26) | copy-start | bytes 3076
  7.2 29.0 %copy-start.5 = (bf16[512]{0:T(512)(128)(2,1)S(1)}, bf16[512]{0:T(512)(128)(2,1)}, u32[]{:S(2)}) copy-start(bf16[512]{0:T(512)(128)(2,1)} %param.17) | copy-start | bytes 3076
  7.2 109.7 %all-gather.4.cloned.1.call-start = ((), (), s32[]{:S(2)}) async-start(), calls=%async_computation | async-start | bytes 7667712 | tf_op jit(solution)/shard_map/all_gather | solution.py:190
  11.1 6.3 %collective-permute-start = (bf16[32,1664]{1,0:T(8,128)(2,1)S(1)}, bf16[32,1664]{1,0:T(8,128)(2,1)S(1)}, u32[]{:S(2)}, u32[]{:S(2)}) collective-permute-start(bf16[32,1664]{1,0:T(8,128)(2,1)S(1)} %constant_dynamic-update-slice_fusion), channel_id=1, source_target_pairs={{0,4},{4,0},{1,5},{5,1},{2,6},{6,2},{3,7},{7,3},{8,12},{12,8},{9,1... | collective-permute-start | bytes 319496 | tf_op jit(solution)/shard_map/ppermute | solution.py:114
  32.5 140.9 %all-gather.6.cloned.1.call-start = ((), (), s32[]{:S(2)}) async-start(), calls=%async_computation.1 | async-start | bytes 2359296 | tf_op jit(solution)/shard_map/all_gather | solution.py:254
  32.7 2.5 collective-permute-start.2
  35.2 3.7 %collective-permute-start.3 = (f32[256]{0:T(256)S(1)}, f32[256]{0:T(256)S(1)}, u32[]{:S(2)}, u32[]{:S(2)}) collective-permute-start(f32[256]{0:T(256)S(1)} %add.479), channel_id=1, source_target_pairs={{0,2},{1,3},{2,0},{3,1},{4,6},{5,7},{6,4},{7,5},{8,10},{9,11},{10,... | collective-permute-start | bytes 3080 | tf_op jit(solution)/shard_map/ppermute | solution.py:206
  39.0 2.2 collective-permute-start.4
  39.8 5.4 %collective-permute-start.1 = (bf16[32,512]{1,0:T(8,128)(2,1)S(1)}, bf16[32,512]{1,0:T(8,128)(2,1)S(1)}, u32[]{:S(2)}, u32[]{:S(2)}) collective-permute-start(bf16[32,512]{1,0:T(8,128)(2,1)S(1)} %copy-done.3), channel_id=1, source_target_pairs={{0,4},{4,0},{1,5},{5,1},{2,6},{6,2},{3,7},{7,3},{8,12},{12,8},{9,1... | collective-permute-start | bytes 98312 | tf_op jit(solution)/shard_map/ppermute | solution.py:114
  41.3 75.6 %collective-permute-start.5 = (bf16[256,1024]{1,0:T(8,128)(2,1)S(1)}, bf16[256,1024]{1,0:T(8,128)(2,1)S(1)}, u32[]{:S(2)}, u32[]{:S(2)}) collective-permute-start(bf16[256,1024]{1,0:T(8,128)(2,1)S(1)} %maximum_select_fusion.3), channel_id=1, source_target_pairs={{0,2},{1,3},{2,0},{3,1},{4,6},{5,7},{6,4},{7,5},{8,10},{9,11},{10,... | collective-permute-start | bytes 1572872 | tf_op jit(solution)/shard_map/ppermute | solution.py:149
  93.9 27.0 %copy-start.8 = (f32[128]{0:T(128)S(1)}, f32[128]{0:T(128)}, u32[]{:S(2)}) copy-start(f32[128]{0:T(128)} %param.23) | copy-start | bytes 1540
  122.2 9.6 %collective-permute-start.6 = (bf16[256,512]{1,0:T(8,128)(2,1)S(1)}, bf16[256,512]{1,0:T(8,128)(2,1)S(1)}, u32[]{:S(2)}, u32[]{:S(2)}) collective-permute-start(bf16[256,512]{1,0:T(8,128)(2,1)S(1)} %pad_maximum_fusion.1), channel_id=1, source_target_pairs={{0,4},{4,0},{1,5},{5,1},{2,6},{6,2},{3,7},{7,3},{8,12},{12,8},{9,1... | collective-permute-start | bytes 786440 | tf_op jit(solution)/shard_map/ppermute | solution.py:114
  132.9 148.9 %all-gather.8.cloned.1.call-start = ((), (), s32[]{:S(2)}) async-start(), calls=%async_computation.2 | async-start | bytes 9437184 | tf_op jit(solution)/shard_map/all_gather | solution.py:257
  182.4 2.3 copy-start.7
  305.8 2.2 copy-start.1
  314.5 5.1 %collective-permute-start.7 = (f32[256,1024]{1,0:T(8,128)S(1)}, f32[256,1024]{1,0:T(8,128)S(1)}, u32[]{:S(2)}, u32[]{:S(2)}) collective-permute-start(f32[256,1024]{1,0:T(8,128)S(1)} %pad_maximum_fusion), channel_id=1, source_target_pairs={{0,1},{1,0},{2,3},{3,2},{4,5},{5,4},{6,7},{7,6},{8,9},{9,8},{10,11... | collective-permute-start | bytes 3145736 | tf_op jit(solution)/shard_map/ppermute | solution.py:383
  319.8 8.8 %collective-permute-start.8 = (bf16[256,512]{1,0:T(8,128)(2,1)S(1)}, bf16[256,512]{1,0:T(8,128)(2,1)S(1)}, u32[]{:S(2)}, u32[]{:S(2)}) collective-permute-start(bf16[256,512]{1,0:T(8,128)(2,1)S(1)} %dynamic-slice_convert_fusion), channel_id=1, source_target_pairs={{0,2},{1,3},{2,0},{3,1},{4,6},{5,7},{6,4},{7,5},{8,10},{9,11},{10,... | collective-permute-start | bytes 786440 | tf_op jit(solution)/shard_map/ppermute | solution.py:386
Sparse Core Ops, SparseCore 0:
  32.6 84.2 all-gather.3
  133.0 40.3 all-gather.5
  175.2 92.1 all-gather.7

commit v13 on v9

--- a/solution.py
+++ b/solution.py
@@ -9,7 +9,7 @@
 HEAD_SIZE = 128
 LMAX = 512
 KEY_BLOCK = 256
-BATCH_BLOCKS = 8
+BATCH_BLOCKS = 3
 
 
 epsilon = 1e-06
@@ -190,7 +190,14 @@
 
     wide_tokens = tokens.astype(jnp.float32)
     full_width = tokens.shape[1] * lax.axis_size("mdl")
-    square_total = lax.psum(jnp.sum(wide_tokens * wide_tokens, axis=1), "mdl")
+    square_part = jnp.sum(wide_tokens * wide_tokens, axis=1)
+    n_mdl_in = lax.axis_size("mdl")
+    square_part = square_part + lax.ppermute(
+        square_part, "mdl", [(m, m ^ 1) for m in range(n_mdl_in)]
+    )
+    square_total = square_part + lax.ppermute(
+        square_part, "mdl", [(m, m ^ 2) for m in range(n_mdl_in)]
+    )
     scaled = (
         wide_tokens
         * lax.rsqrt(square_total / full_width + epsilon)[:, None]
@@ -389,17 +396,20 @@
     n_mdl = lax.axis_size("mdl")
     x_lo = mdl_index // 2
     core = mdl_index % 2
-    half = partial_out.shape[1] // 2
-    quarter = half // 2
-    mine = lax.dynamic_slice_in_dim(partial_out, x_lo * half, half, 1)
-    theirs = lax.dynamic_slice_in_dim(partial_out, (1 - x_lo) * half, half, 1)
+    quarter = partial_out.shape[1] // 4
+
+    def cols_of(block):
+        return lax.dynamic_slice_in_dim(partial_out, block * quarter, quarter, 1)
+
+    mine = jnp.concatenate([cols_of(core), cols_of(2 + core)], axis=1)
+    theirs = jnp.concatenate([cols_of(1 - core), cols_of(3 - core)], axis=1)
+    pair_sum = mine + lax.ppermute(theirs, "mdl", [(m, m ^ 1) for m in range(n_mdl)])
+    mine = lax.dynamic_slice_in_dim(pair_sum, x_lo * quarter, quarter, 1)
+    theirs = lax.dynamic_slice_in_dim(pair_sum, (1 - x_lo) * quarter, quarter, 1)
     across = lax.ppermute(
         theirs.astype(jnp.bfloat16), "mdl", [(m, m ^ 2) for m in range(n_mdl)]
     )
-    half_sum = mine + across.astype(jnp.float32)
-    mine = lax.dynamic_slice_in_dim(half_sum, core * quarter, quarter, 1)
-    theirs = lax.dynamic_slice_in_dim(half_sum, (1 - core) * quarter, quarter, 1)
-    branch_sum = mine + lax.ppermute(theirs, "mdl", [(m, m ^ 1) for m in range(n_mdl)])
+    branch_sum = mine + across.astype(jnp.float32)
     layer_out = (wide_tokens + branch_sum).astype(jnp.bfloat16)
     return (layer_out, cache_k[None], cache_v[None])
 

time: 350 us -> 326 us (0.931)
  the two profiles are of different devices: /device:TPU:72 before, /device:TPU:28 now
where the time goes in v13:
time: 326 us; the launch traced here: 325 us
  Pallas kernels  107 us (33%)
  blocking collectives  71.3 us (22%)
  waiting for transfers between devices  53 us (16%)
  between operations  32.3 us (10%)
  other arithmetic  25 us (8%)
  local copies, waits for them, and re-layouts  18.5 us (6%)
  matrix products  10.6 us (3%)
  starting transfers between devices  4.05 us (1%)
  loops' own time  3.55 us (1%)
    pallas_call x3, Pallas kernels, ring_y_kernel(): pl.pallas_call(_ring_kernel, out_shape=jax.ShapeDtypeStruct((4, rows, wid...  107 us
    all_gather x1, blocking collectives, gather_xh_z(): return lax.all_gather(x, 'z', axis=0, tiled=True)  32.7 us
    all_gather x1, waiting for transfers between devices, body(): v_part = lax.all_gather(kv_pair[:, kv_cols:], 'z', axis=0, tiled=True)  27.6 us
    all_gather x1, waiting for transfers between devices, body(): gathered = lax.all_gather(packed, 'z', axis=0, tiled=True)  17.8 us
    all_gather x1, blocking collectives, body(): packed = lax.all_gather(packed, 'y', axis=0, tiled=True)  15.2 us
    all_gather x1, blocking collectives, body(): lax.all_gather(jnp.concatenate([k_rot, values_flat], axis=1), 'xh', axis=...  10.2 us
    all_gather x1, blocking collectives, body(): packed = lax.all_gather(packed, 'xh', axis=0, tiled=True)  6.89 us
  transfers between devices with their start and end apart: 9, of which 5 were waited for; matrix products, arithmetic and copies ran while one was open for 8% of the time, Pallas kernels for 33%

profile of v13, /device:TPU:28, one launch (start us, length us, event | category | flops | bytes accessed | tf_op | source)
XLA Modules:
  0.0 325.4 jit_solution(13945921734935296374)
XLA Ops:
  11.0 6.9 %all_gather.24 = bf16[64,1664]{1,0:T(8,128)(2,1)S(1)} all-gather(bf16[32,1664]{1,0:T(8,128)(2,1)S(1)} %constant_dynamic-update-slice_fusion), channel_id=1, replica_groups=mesh['z'=8,'y'=4,'xh'=2,'mdl'=4] {'xh'}, dimensions={0}, use_global_device_ids=true | all-gather | bytes 319488 | tf_op jit(solution)/shard_map/all_gather | solution.py:178
  17.9 15.2 %all_gather.25 = bf16[256,1664]{1,0:T(8,128)(2,1)} all-gather(bf16[64,1664]{1,0:T(8,128)(2,1)S(1)} %all_gather.24), channel_id=1, replica_groups=mesh['z'=8,'y'=4,'xh'=2,'mdl'=4] {'y'}, dimensions={0}, use_global_device_ids=true | all-gather | bytes 1064960 | tf_op jit(solution)/shard_map/all_gather | solution.py:179
  35.3 6.3 %all_gather.27 = bf16[64,512]{1,0:T(8,128)(2,1)S(1)} all-gather(bf16[32,512]{1,0:T(8,128)(2,1)} %param.21), channel_id=1, replica_groups=mesh['z'=8,'y'=4,'xh'=2,'mdl'=4] {'xh'}, dimensions={0}, use_global_device_ids=true | all-gather | bytes 98304 | tf_op jit(solution)/shard_map/all_gather | solution.py:115
  41.6 1.3 fusion.63
  43.6 2.0 fusion.61
  46.3 32.7 %all_gather.28.x_ref = bf16[512,512]{1,0:T(8,128)(2,1)} all-gather(bf16[64,512]{1,0:T(8,128)(2,1)S(1)} %all_gather.27), channel_id=1, replica_groups=mesh['z'=8,'y'=4,'xh'=2,'mdl'=4] {'z'}, dimensions={0}, use_global_device_ids=true | all-gather | bytes 589824 | tf_op jit(solution)/shard_map/all_gather | solution.py:116
  79.1 1.3 collective-permute-start.1
  80.4 17.8 %shard_map.157 = bf16[4,512,512]{2,1,0:T(8,128)(2,1)} custom-call(bf16[512,512]{1,0:T(8,128)(2,1)} %all_gather.28.x_ref), custom_call_target="tpu_custom_call" | custom-call | tf_op jit(solution)/shard_map/pallas_call | solution.py:94
  98.6 1.4 collective-permute-done.2
  102.2 17.8 %all-gather.4.cloned.1.call-done = bf16[2048,1664]{1,0:T(8,128)(2,1)} async-done(((bf16[256,1664]{1,0:T(8,128)(2,1)}), bf16[2048,1664]{1,0:T(8,128)(2,1)}) %all-gather.4.cloned.1.call-update) | async-done | bytes 6815760 | tf_op jit(solution)/shard_map/all_gather | solution.py:182
  120.0 3.4 %fusion.12 = f32[256,1024]{1,0:T(8,128)S(1)} fusion(bf16[2048,1664]{1,0:T(8,128)(2,1)} %all-gather.4.cloned.1.call-done, bf16[256,1024]{1,0:T(8,128)(2,1)S(1)} %collective-permute-done.3, bf16[256,1024]{1,0:T(8,128)(2,1)S(1)} %maximum_select_fusion.3, pred[]{:T(512)S(6)} %eq.261), kind=kOutput, calls=%fused_computation.21 | convolution fusion | flops 1078460416 | bytes 6291457 | tf_op jit(solution)/shard_map/dot_general | solution.py:207
  125.3 10.2 %all_gather.29 = bf16[512,512]{1,0:T(8,128)(2,1)S(1)} all-gather(bf16[256,512]{1,0:T(8,128)(2,1)S(1)} %pad_maximum_fusion.3), channel_id=1, replica_groups=mesh['z'=8,'y'=4,'xh'=2,'mdl'=4] {'xh'}, dimensions={0}, use_global_device_ids=true | all-gather | bytes 786432 | tf_op jit(solution)/shard_map/all_gather | solution.py:245
  136.5 12.2 %shard_map.158 = bf16[4,512,256]{2,1,0:T(8,128)(2,1)} custom-call(bf16[512,256]{1,0:T(8,128)(2,1)} %get-tuple-element.416.x_ref), custom_call_target="tpu_custom_call" | custom-call | tf_op jit(solution)/shard_map/pallas_call | solution.py:94
  148.7 27.6 %all-gather.6.cloned.1.call-done.x_ref = bf16[4096,256]{1,0:T(8,128)(2,1)} async-done(((bf16[512,256]{1,0:T(8,128)(2,1)}), bf16[4096,256]{1,0:T(8,128)(2,1)}) %all-gather.6.cloned.1.call-update) | async-done | bytes 2097168 | tf_op jit(solution)/shard_map/all_gather | solution.py:246
  203.7 1.2 slice_compare_fusion
  206.4 77.0 %shard_map.159 = bf16[4,4096,256]{2,1,0:T(8,128)(2,1)} custom-call(bf16[4096,256]{1,0:T(8,128)(2,1)} %all-gather.6.cloned.1.call-done.x_ref), custom_call_target="tpu_custom_call" | custom-call | tf_op jit(solution)/shard_map/pallas_call | solution.py:94
  283.4 2.1 constant_dynamic-slice_fusion.2
  285.7 2.1 constant_dynamic-slice_fusion.5
  290.4 9.8 %while.18 = (s32[]{:T(128)}, f32[256,2,2]{0,2,1:T(2,128)S(1)}, f32[256,2,2]{0,2,1:T(2,128)S(1)}, f32[256,2,2,128]{0,3,2,1:T(8,128)S(1)}, s32[]{:T(128)}, /*index...) while((s32[]{:T(128)}, f32[256,2,2]{0,2,1:T(2,128)S(1)}, ...), condition=%wide.region_22.23_spmd.clone, body=%wide.region_19.22_spmd.clone.sunk | while | flops 137300576 | bytes 6105331 | solution.py:364
  300.5 4.0 %fusion.17 = f32[256,2048]{1,0:T(8,128)S(1)} fusion(bf16[2048,1664]{1,0:T(8,128)(2,1)} %all-gather.4.cloned.1.call-done, f32[256,512]{1,0:T(8,128)S(1)} %copy.108, bf16[256,2048]{0,1:T(8,128)(2,1)} %bitcast.118, bf16[2048,512]{1,0:T(8,128)(2,1)} %bitcast.113), kind=kOutput, calls=%fused_computation.32 | convolution fusion | flops 1074397184 | bytes 7864320 | tf_op jit(solution)/shard_map/dot_general | solution.py:389
  305.9 2.5 collective-permute-done.4
  309.6 1.3 collective-permute-start.5
  312.1 2.3 fusion.48
  314.4 3.7 %collective-permute-done.5 = bf16[256,512]{1,0:T(8,128)(2,1)S(1)} collective-permute-done((bf16[256,512]{1,0:T(8,128)(2,1)S(1)}, bf16[256,512]{1,0:T(8,128)(2,1)S(1)}, u32[]{:S(2)}, u32[]{:S(2)}) %collective-permute-start.5) | collective-permute-done | bytes 262176 | tf_op jit(solution)/shard_map/ppermute | solution.py:409
  (153 shorter events, 37.4 us)
Async XLA Ops:
  7.2 91.1 %copy-start = (bf16[256,512]{1,0:T(8,128)(2,1)S(1)}, bf16[256,512]{1,0:T(8,128)(2,1)}, u32[]{:S(2)}) copy-start(bf16[256,512]{1,0:T(8,128)(2,1)} %param.16) | copy-start | bytes 786436
  7.2 73.2 %copy-start.6 = (bf16[512]{0:T(512)(128)(2,1)S(1)}, bf16[512]{0:T(512)(128)(2,1)}, u32[]{:S(2)}) copy-start(bf16[512]{0:T(512)(128)(2,1)} %param.17) | copy-start | bytes 3076
  7.2 112.9 %all-gather.4.cloned.1.call-start = ((), (), s32[]{:S(2)}) async-start(), calls=%async_computation | async-start | bytes 7667712 | tf_op jit(solution)/shard_map/all_gather | solution.py:182
  17.9 80.6 %copy-start.5 = (s32[256]{0:T(256)S(1)}, s32[256]{0:T(256)}, u32[]{:S(2)}) copy-start(s32[256]{0:T(256)} %param.26) | copy-start | bytes 3076
  33.1 143.2 %all-gather.6.cloned.1.call-start = ((), (), s32[]{:S(2)}) async-start(), calls=%async_computation.1 | async-start | bytes 2359296 | tf_op jit(solution)/shard_map/all_gather | solution.py:246
  34.2 44.9 %collective-permute-start = (f32[256]{0:T(256)S(1)}, f32[256]{0:T(256)S(1)}, u32[]{:S(2)}, u32[]{:S(2)}) collective-permute-start(f32[256]{0:T(256)S(1)} %fusion.38), channel_id=1, source_target_pairs={{0,1},{1,0},{2,3},{3,2},{4,5},{5,4},{6,7},{7,6},{8,9},{9,8},{10,11... | collective-permute-start | bytes 3080 | tf_op jit(solution)/shard_map/ppermute | solution.py:195
  79.1 19.1 %collective-permute-start.1 = (f32[256]{0:T(256)S(1)}, f32[256]{0:T(256)S(1)}, u32[]{:S(2)}, u32[]{:S(2)}) collective-permute-start(f32[256]{0:T(256)S(1)} %add.647), channel_id=1, source_target_pairs={{0,2},{1,3},{2,0},{3,1},{4,6},{5,7},{6,4},{7,5},{8,10},{9,11},{10,... | collective-permute-start | bytes 3080 | tf_op jit(solution)/shard_map/ppermute | solution.py:198
  98.4 1.6 collective-permute-start.2
  100.1 19.9 %collective-permute-start.3 = (bf16[256,1024]{1,0:T(8,128)(2,1)S(1)}, bf16[256,1024]{1,0:T(8,128)(2,1)S(1)}, u32[]{:S(2)}, u32[]{:S(2)}) collective-permute-start(bf16[256,1024]{1,0:T(8,128)(2,1)S(1)} %maximum_select_fusion.3), channel_id=1, source_target_pairs={{0,2},{1,3},{2,0},{3,1},{4,6},{5,7},{6,4},{7,5},{8,10},{9,11},{10,... | collective-permute-start | bytes 1572872 | tf_op jit(solution)/shard_map/ppermute | solution.py:141
  102.2 21.8 %copy-start.8 = (f32[128]{0:T(128)S(1)}, f32[128]{0:T(128)}, u32[]{:S(2)}) copy-start(f32[128]{0:T(128)} %param.23) | copy-start | bytes 1540
  136.4 149.3 %all-gather.8.cloned.1.call-start = ((), (), s32[]{:S(2)}) async-start(), calls=%async_computation.2 | async-start | bytes 9437184 | tf_op jit(solution)/shard_map/all_gather | solution.py:249
  200.6 2.1 copy-start.7
  305.5 6.6 %copy-start.1 = (bf16[256,256]{1,0:T(8,128)(2,1)S(1)}, bf16[256,256]{1,0:T(8,128)(2,1)}, u32[]{:S(2)}) copy-start(bf16[256,256]{1,0:T(8,128)(2,1)} %get-tuple-element.398) | copy-start | bytes 393220
  305.5 6.6 %copy-start.2 = (bf16[256,256]{1,0:T(8,128)(2,1)S(1)}, bf16[256,256]{1,0:T(8,128)(2,1)}, u32[]{:S(2)}) copy-start(bf16[256,256]{1,0:T(8,128)(2,1)} %get-tuple-element.399) | copy-start | bytes 393220
  305.5 6.6 %copy-start.3 = (bf16[256,256]{1,0:T(8,128)(2,1)S(1)}, bf16[256,256]{1,0:T(8,128)(2,1)}, u32[]{:S(2)}) copy-start(bf16[256,256]{1,0:T(8,128)(2,1)} %get-tuple-element.403) | copy-start | bytes 393220
  305.5 6.6 %copy-start.4 = (bf16[256,256]{1,0:T(8,128)(2,1)S(1)}, bf16[256,256]{1,0:T(8,128)(2,1)}, u32[]{:S(2)}) copy-start(bf16[256,256]{1,0:T(8,128)(2,1)} %get-tuple-element.404) | copy-start | bytes 393220
  305.6 2.7 collective-permute-start.4
  309.6 8.5 %collective-permute-start.5 = (bf16[256,512]{1,0:T(8,128)(2,1)S(1)}, bf16[256,512]{1,0:T(8,128)(2,1)S(1)}, u32[]{:S(2)}, u32[]{:S(2)}) collective-permute-start(bf16[256,512]{1,0:T(8,128)(2,1)S(1)} %dynamic-slice_convert_fusion), channel_id=1, source_target_pairs={{0,2},{1,3},{2,0},{3,1},{4,6},{5,7},{6,4},{7,5},{8,10},{9,11},{10,... | collective-permute-start | bytes 786440 | tf_op jit(solution)/shard_map/ppermute | solution.py:409
Sparse Core Ops, SparseCore 0:
  33.2 86.7 all-gather.3
  136.5 39.7 all-gather.5
  178.1 92.6 all-gather.7

commit v14 on v13

--- a/solution.py
+++ b/solution.py
@@ -9,7 +9,7 @@
 HEAD_SIZE = 128
 LMAX = 512
 KEY_BLOCK = 256
-BATCH_BLOCKS = 3
+BATCH_BLOCKS = 5
 
 
 epsilon = 1e-06

time: 326 us -> 325 us (level)
  the two profiles are of different devices: /device:TPU:28 before, /device:TPU:72 now
where the time goes in v14:
time: 325 us; the launch traced here: 323 us
  Pallas kernels  103 us (32%)
  blocking collectives  69.5 us (21%)
  waiting for transfers between devices  49.3 us (15%)
  between operations  40.5 us (12%)
  other arithmetic  23.5 us (7%)
  local copies, waits for them, and re-layouts  21.6 us (7%)
  matrix products  9.39 us (3%)
  starting transfers between devices  4.32 us (1%)
    pallas_call x3, Pallas kernels, ring_y_kernel(): pl.pallas_call(_ring_kernel, out_shape=jax.ShapeDtypeStruct((4, rows, wid...  103 us
    all_gather x1, blocking collectives, gather_xh_z(): return lax.all_gather(x, 'z', axis=0, tiled=True)  30.8 us
    all_gather x1, waiting for transfers between devices, body(): v_part = lax.all_gather(kv_pair[:, kv_cols:], 'z', axis=0, tiled=True)  27.3 us
    all_gather x1, waiting for transfers between devices, body(): gathered = lax.all_gather(packed, 'z', axis=0, tiled=True)  16 us
    all_gather x1, blocking collectives, body(): packed = lax.all_gather(packed, 'y', axis=0, tiled=True)  15.3 us
    unnamed x21, local copies, waits for them, and re-layouts  10.6 us
    all_gather x1, blocking collectives, body(): lax.all_gather(jnp.concatenate([k_rot, values_flat], axis=1), 'xh', axis=...  10.2 us
    all_gather x1, blocking collectives, body(): packed = lax.all_gather(packed, 'xh', axis=0, tiled=True)  6.89 us
  transfers between devices with their start and end apart: 9, of which 4 were waited for; matrix products, arithmetic and copies ran while one was open for 10% of the time, Pallas kernels for 32%

profile of v14, /device:TPU:72, one launch (start us, length us, event | category | flops | bytes accessed | tf_op | source)
XLA Modules:
  0.0 322.5 jit_solution(3432344640634622775)
XLA Ops:
  11.0 6.9 %all_gather.24 = bf16[64,1664]{1,0:T(8,128)(2,1)S(1)} all-gather(bf16[32,1664]{1,0:T(8,128)(2,1)S(1)} %constant_dynamic-update-slice_fusion), channel_id=1, replica_groups=mesh['z'=8,'y'=4,'xh'=2,'mdl'=4] {'xh'}, dimensions={0}, use_global_device_ids=true | all-gather | bytes 319488 | tf_op jit(solution)/shard_map/all_gather | solution.py:178
  17.9 15.3 %all_gather.25 = bf16[256,1664]{1,0:T(8,128)(2,1)} all-gather(bf16[64,1664]{1,0:T(8,128)(2,1)S(1)} %all_gather.24), channel_id=1, replica_groups=mesh['z'=8,'y'=4,'xh'=2,'mdl'=4] {'y'}, dimensions={0}, use_global_device_ids=true | all-gather | bytes 1064960 | tf_op jit(solution)/shard_map/all_gather | solution.py:179
  35.4 6.3 %all_gather.27 = bf16[64,512]{1,0:T(8,128)(2,1)S(1)} all-gather(bf16[32,512]{1,0:T(8,128)(2,1)} %param.21), channel_id=1, replica_groups=mesh['z'=8,'y'=4,'xh'=2,'mdl'=4] {'xh'}, dimensions={0}, use_global_device_ids=true | all-gather | bytes 98304 | tf_op jit(solution)/shard_map/all_gather | solution.py:115
  41.7 1.3 fusion.63
  43.7 2.0 fusion.61
  46.4 30.8 %all_gather.28.x_ref = bf16[512,512]{1,0:T(8,128)(2,1)} all-gather(bf16[64,512]{1,0:T(8,128)(2,1)S(1)} %all_gather.27), channel_id=1, replica_groups=mesh['z'=8,'y'=4,'xh'=2,'mdl'=4] {'z'}, dimensions={0}, use_global_device_ids=true | all-gather | bytes 589824 | tf_op jit(solution)/shard_map/all_gather | solution.py:116
  77.4 1.6 collective-permute-start.1
  79.6 18.2 %shard_map.157 = bf16[4,512,512]{2,1,0:T(8,128)(2,1)} custom-call(bf16[512,512]{1,0:T(8,128)(2,1)} %all_gather.28.x_ref), custom_call_target="tpu_custom_call" | custom-call | tf_op jit(solution)/shard_map/pallas_call | solution.py:94
  98.2 1.4 collective-permute-done.2
  101.6 16.0 %all-gather.4.cloned.1.call-done = bf16[2048,1664]{1,0:T(8,128)(2,1)} async-done(((bf16[256,1664]{1,0:T(8,128)(2,1)}), bf16[2048,1664]{1,0:T(8,128)(2,1)}) %all-gather.4.cloned.1.call-update) | async-done | bytes 6815760 | tf_op jit(solution)/shard_map/all_gather | solution.py:182
  117.6 3.4 %fusion.14 = f32[256,1024]{1,0:T(8,128)S(1)} fusion(bf16[2048,1664]{1,0:T(8,128)(2,1)} %all-gather.4.cloned.1.call-done, bf16[256,1024]{1,0:T(8,128)(2,1)S(1)} %collective-permute-done.3, bf16[256,1024]{1,0:T(8,128)(2,1)S(1)} %maximum_select_fusion.3, pred[]{:T(512)S(6)} %eq.277), kind=kOutput, calls=%fused_computation.25 | convolution fusion | flops 1078460416 | bytes 6291457 | tf_op jit(solution)/shard_map/dot_general | solution.py:207
  122.9 10.2 %all_gather.29 = bf16[512,512]{1,0:T(8,128)(2,1)S(1)} all-gather(bf16[256,512]{1,0:T(8,128)(2,1)S(1)} %pad_maximum_fusion.1), channel_id=1, replica_groups=mesh['z'=8,'y'=4,'xh'=2,'mdl'=4] {'xh'}, dimensions={0}, use_global_device_ids=true | all-gather | bytes 786432 | tf_op jit(solution)/shard_map/all_gather | solution.py:245
  134.0 13.0 %shard_map.158 = bf16[4,512,256]{2,1,0:T(8,128)(2,1)} custom-call(bf16[512,256]{1,0:T(8,128)(2,1)} %get-tuple-element.410.x_ref), custom_call_target="tpu_custom_call" | custom-call | tf_op jit(solution)/shard_map/pallas_call | solution.py:94
  147.0 27.3 %all-gather.6.cloned.1.call-done.x_ref = bf16[4096,256]{1,0:T(8,128)(2,1)} async-done(((bf16[512,256]{1,0:T(8,128)(2,1)}), bf16[4096,256]{1,0:T(8,128)(2,1)}) %all-gather.6.cloned.1.call-update) | async-done | bytes 2097168 | tf_op jit(solution)/shard_map/all_gather | solution.py:246
  177.7 1.2 scatter_custom_fusion
  205.8 1.2 slice_compare_fusion
  210.5 72.3 %shard_map.159 = bf16[4,4096,256]{2,1,0:T(8,128)(2,1)} custom-call(bf16[4096,256]{1,0:T(8,128)(2,1)} %all-gather.6.cloned.1.call-done.x_ref), custom_call_target="tpu_custom_call" | custom-call | tf_op jit(solution)/shard_map/pallas_call | solution.py:94
  296.7 4.0 %fusion.21 = f32[256,2048]{1,0:T(8,128)S(1)} fusion(bf16[2048,1664]{1,0:T(8,128)(2,1)} %all-gather.4.cloned.1.call-done, f32[256,512]{1,0:T(8,128)S(1)} %copy.108, bf16[256,2048]{0,1:T(8,128)(2,1)} %bitcast.123, bf16[2048,512]{1,0:T(8,128)(2,1)} %bitcast.118), kind=kOutput, calls=%fused_computation.35 | convolution fusion | flops 1074397184 | bytes 7864320 | tf_op jit(solution)/shard_map/dot_general | solution.py:389
  304.0 1.2 fusion.55
  305.2 1.1 constant_dynamic-slice_fusion.2
  306.5 1.6 collective-permute-start.5
  308.1 1.1 constant_dynamic-slice_fusion.5
  309.2 1.5 fusion.48
  310.7 4.5 %collective-permute-done.5 = bf16[256,512]{1,0:T(8,128)(2,1)S(1)} collective-permute-done((bf16[256,512]{1,0:T(8,128)(2,1)S(1)}, bf16[256,512]{1,0:T(8,128)(2,1)S(1)}, u32[]{:S(2)}, u32[]{:S(2)}) %collective-permute-start.5) | collective-permute-done | bytes 262176 | tf_op jit(solution)/shard_map/ppermute | solution.py:409
  (126 shorter events, 38.7 us)
Async XLA Ops:
  7.2 90.6 %copy-start = (bf16[256,512]{1,0:T(8,128)(2,1)S(1)}, bf16[256,512]{1,0:T(8,128)(2,1)}, u32[]{:S(2)}) copy-start(bf16[256,512]{1,0:T(8,128)(2,1)} %param.16) | copy-start | bytes 786436
  7.2 90.9 %copy-start.1 = (s32[256]{0:T(256)S(1)}, s32[256]{0:T(256)}, u32[]{:S(2)}) copy-start(s32[256]{0:T(256)} %param.26) | copy-start | bytes 3076
  7.2 110.4 %all-gather.4.cloned.1.call-start = ((), (), s32[]{:S(2)}) async-start(), calls=%async_computation | async-start | bytes 7667712 | tf_op jit(solution)/shard_map/all_gather | solution.py:182
  33.2 141.1 %all-gather.6.cloned.1.call-start = ((), (), s32[]{:S(2)}) async-start(), calls=%async_computation.1 | async-start | bytes 2359296 | tf_op jit(solution)/shard_map/all_gather | solution.py:246
  34.3 43.0 %collective-permute-start = (f32[256]{0:T(256)S(1)}, f32[256]{0:T(256)S(1)}, u32[]{:S(2)}, u32[]{:S(2)}) collective-permute-start(f32[256]{0:T(256)S(1)} %fusion.41), channel_id=1, source_target_pairs={{0,1},{1,0},{2,3},{3,2},{4,5},{5,4},{6,7},{7,6},{8,9},{9,8},{10,11... | collective-permute-start | bytes 3080 | tf_op jit(solution)/shard_map/ppermute | solution.py:195
  77.4 20.4 %collective-permute-start.1 = (f32[256]{0:T(256)S(1)}, f32[256]{0:T(256)S(1)}, u32[]{:S(2)}, u32[]{:S(2)}) collective-permute-start(f32[256]{0:T(256)S(1)} %add.741), channel_id=1, source_target_pairs={{0,2},{1,3},{2,0},{3,1},{4,6},{5,7},{6,4},{7,5},{8,10},{9,11},{10,... | collective-permute-start | bytes 3080 | tf_op jit(solution)/shard_map/ppermute | solution.py:198
  98.0 1.6 collective-permute-start.2
  99.7 17.9 %collective-permute-start.3 = (bf16[256,1024]{1,0:T(8,128)(2,1)S(1)}, bf16[256,1024]{1,0:T(8,128)(2,1)S(1)}, u32[]{:S(2)}, u32[]{:S(2)}) collective-permute-start(bf16[256,1024]{1,0:T(8,128)(2,1)S(1)} %maximum_select_fusion.3), channel_id=1, source_target_pairs={{0,2},{1,3},{2,0},{3,1},{4,6},{5,7},{6,4},{7,5},{8,10},{9,11},{10,... | collective-permute-start | bytes 1572872 | tf_op jit(solution)/shard_map/ppermute | solution.py:141
  101.6 20.1 %copy-start.3 = (f32[128]{0:T(128)S(1)}, f32[128]{0:T(128)}, u32[]{:S(2)}) copy-start(f32[128]{0:T(128)} %param.23) | copy-start | bytes 1540
  134.0 153.7 %all-gather.8.cloned.1.call-start = ((), (), s32[]{:S(2)}) async-start(), calls=%async_computation.2 | async-start | bytes 9437184 | tf_op jit(solution)/shard_map/all_gather | solution.py:249
  204.1 4.1 %copy-start.2 = (f32[128]{0:T(128)S(1)}, f32[128]{0:T(128)}, u32[]{:S(2)}) copy-start(f32[128]{0:T(128)} %param.22) | copy-start | bytes 1540
  301.0 5.3 %collective-permute-start.4 = (f32[256,1024]{1,0:T(8,128)S(1)}, f32[256,1024]{1,0:T(8,128)S(1)}, u32[]{:S(2)}, u32[]{:S(2)}) collective-permute-start(f32[256,1024]{1,0:T(8,128)S(1)} %pad_maximum_fusion), channel_id=1, source_target_pairs={{0,1},{1,0},{2,3},{3,2},{4,5},{5,4},{6,7},{7,6},{8,9},{9,8},{10,11... | collective-permute-start | bytes 3145736 | tf_op jit(solution)/shard_map/ppermute | solution.py:406
  306.5 8.6 %collective-permute-start.5 = (bf16[256,512]{1,0:T(8,128)(2,1)S(1)}, bf16[256,512]{1,0:T(8,128)(2,1)S(1)}, u32[]{:S(2)}, u32[]{:S(2)}) collective-permute-start(bf16[256,512]{1,0:T(8,128)(2,1)S(1)} %dynamic-slice_convert_fusion), channel_id=1, source_target_pairs={{0,2},{1,3},{2,0},{3,1},{4,6},{5,7},{6,4},{7,5},{8,10},{9,11},{10,... | collective-permute-start | bytes 786440 | tf_op jit(solution)/shard_map/ppermute | solution.py:409
Sparse Core Ops, SparseCore 0:
  33.3 84.2 all-gather.3
  134.1 40.1 all-gather.5
  176.1 92.1 all-gather.7

commit v15 on v14

--- a/solution.py
+++ b/solution.py
@@ -69,7 +69,6 @@
     own = pltpu.make_async_copy(x_ref, out_ref.at[0], local_sem.at[0])
     to_minus.start()
     to_plus.start()
-    own.start()
     to_minus.wait_recv()
     on_minus = pltpu.make_async_remote_copy(
         src_ref=out_ref.at[1, pl.ds(0, half)], dst_ref=out_ref.at[2, pl.ds(0, half)],
@@ -80,6 +79,7 @@
         src_ref=out_ref.at[3, pl.ds(half, rows - half)], dst_ref=out_ref.at[2, pl.ds(half, rows - half)],
         send_sem=send_sem.at[3], recv_sem=recv_sem.at[3], device_id=plus, device_id_type=MESH_ID)
     on_plus.start()
+    own.start()
     to_minus.wait_send()
     to_plus.wait_send()
     own.wait()

time: 325 us -> 374 us (1.15)
  Pallas kernels: 103 us -> 161 us
  waiting for transfers between devices: 49.3 us -> 39.8 us
    pallas_call x3, Pallas kernels: 103 us -> 161 us  [ring_y_kernel(): pl.pallas_call(_ring_kernel, out_shape=jax.ShapeDtypeStruct((4, rows, wid...]
    all_gather x1, waiting for transfers between devices: 16 us -> 3.56 us  [body(): gathered = lax.all_gather(packed, 'z', axis=0, tiled=True)]
    ppermute x1, waiting for transfers between devices: 0.01 us -> 8.59 us  [gather_mdl(): other = lax.ppermute(pair, 'mdl', [(m, m ^ 2) for m in range(n_mdl)])]
    all_gather x1, waiting for transfers between devices: 27.3 us -> 21.5 us  [body(): v_part = lax.all_gather(kv_pair[:, kv_cols:], 'z', axis=0, tiled=True)]
  transfers between devices with their start and end apart: 9 -> 9, of which waited for: 4 -> 5; matrix products, arithmetic and copies ran while one was open for 10% -> 8% of each run, Pallas kernels for 32% -> 44%
where the time goes in v15:
time: 374 us; the launch traced here: 370 us
  Pallas kernels  161 us (43%)
  blocking collectives  69 us (18%)
  between operations  40.5 us (11%)
  waiting for transfers between devices  39.8 us (11%)
  other arithmetic  23.5 us (6%)
  local copies, waits for them, and re-layouts  21.6 us (6%)
  matrix products  9.39 us (3%)
  starting transfers between devices  4.16 us (1%)
    pallas_call x3, Pallas kernels, ring_y_kernel(): pl.pallas_call(_ring_kernel, out_shape=jax.ShapeDtypeStruct((4, rows, wid...  161 us
    all_gather x1, blocking collectives, gather_xh_z(): return lax.all_gather(x, 'z', axis=0, tiled=True)  30.8 us
    all_gather x1, waiting for transfers between devices, body(): v_part = lax.all_gather(kv_pair[:, kv_cols:], 'z', axis=0, tiled=True)  21.5 us
    all_gather x1, blocking collectives, body(): packed = lax.all_gather(packed, 'y', axis=0, tiled=True)  15.3 us
    unnamed x21, local copies, waits for them, and re-layouts  10.6 us
    all_gather x1, blocking collectives, body(): lax.all_gather(jnp.concatenate([k_rot, values_flat], axis=1), 'xh', axis=...  9.7 us
    ppermute x1, waiting for transfers between devices, gather_mdl(): other = lax.ppermute(pair, 'mdl', [(m, m ^ 2) for m in range(n_mdl)])  8.59 us
  transfers between devices with their start and end apart: 9, of which 5 were waited for; matrix products, arithmetic and copies ran while one was open for 8% of the time, Pallas kernels for 44%

profile of v15, /device:TPU:72, one launch (start us, length us, event | category | flops | bytes accessed | tf_op | source)
XLA Modules:
  0.0 370.3 jit_solution(6920440753451664736)
XLA Ops:
  11.0 6.9 %all_gather.24 = bf16[64,1664]{1,0:T(8,128)(2,1)S(1)} all-gather(bf16[32,1664]{1,0:T(8,128)(2,1)S(1)} %constant_dynamic-update-slice_fusion), channel_id=1, replica_groups=mesh['z'=8,'y'=4,'xh'=2,'mdl'=4] {'xh'}, dimensions={0}, use_global_device_ids=true | all-gather | bytes 319488 | tf_op jit(solution)/shard_map/all_gather | solution.py:178
  17.9 15.3 %all_gather.25 = bf16[256,1664]{1,0:T(8,128)(2,1)} all-gather(bf16[64,1664]{1,0:T(8,128)(2,1)S(1)} %all_gather.24), channel_id=1, replica_groups=mesh['z'=8,'y'=4,'xh'=2,'mdl'=4] {'y'}, dimensions={0}, use_global_device_ids=true | all-gather | bytes 1064960 | tf_op jit(solution)/shard_map/all_gather | solution.py:179
  35.4 6.3 %all_gather.27 = bf16[64,512]{1,0:T(8,128)(2,1)S(1)} all-gather(bf16[32,512]{1,0:T(8,128)(2,1)} %param.21), channel_id=1, replica_groups=mesh['z'=8,'y'=4,'xh'=2,'mdl'=4] {'xh'}, dimensions={0}, use_global_device_ids=true | all-gather | bytes 98304 | tf_op jit(solution)/shard_map/all_gather | solution.py:115
  41.7 1.3 fusion.63
  43.7 2.0 fusion.61
  46.4 30.8 %all_gather.28.x_ref = bf16[512,512]{1,0:T(8,128)(2,1)} all-gather(bf16[64,512]{1,0:T(8,128)(2,1)S(1)} %all_gather.27), channel_id=1, replica_groups=mesh['z'=8,'y'=4,'xh'=2,'mdl'=4] {'z'}, dimensions={0}, use_global_device_ids=true | all-gather | bytes 589824 | tf_op jit(solution)/shard_map/all_gather | solution.py:116
  77.4 1.6 collective-permute-start.1
  79.6 30.6 %shard_map.157 = bf16[4,512,512]{2,1,0:T(8,128)(2,1)} custom-call(bf16[512,512]{1,0:T(8,128)(2,1)} %all_gather.28.x_ref), custom_call_target="tpu_custom_call" | custom-call | tf_op jit(solution)/shard_map/pallas_call | solution.py:94
  110.6 1.4 collective-permute-done.2
  114.1 3.6 all-gather.4.cloned.1.call-done
  117.6 8.6 %collective-permute-done.3 = bf16[256,1024]{1,0:T(8,128)(2,1)S(1)} collective-permute-done((bf16[256,1024]{1,0:T(8,128)(2,1)S(1)}, bf16[256,1024]{1,0:T(8,128)(2,1)S(1)}, u32[]{:S(2)}, u32[]{:S(2)}) %collective-permute-start.3) | collective-permute-done | bytes 524320 | tf_op jit(solution)/shard_map/ppermute | solution.py:141
  126.2 3.4 fusion.14
  131.5 9.7 %all_gather.29 = bf16[512,512]{1,0:T(8,128)(2,1)S(1)} all-gather(bf16[256,512]{1,0:T(8,128)(2,1)S(1)} %pad_maximum_fusion.1), channel_id=1, replica_groups=mesh['z'=8,'y'=4,'xh'=2,'mdl'=4] {'xh'}, dimensions={0}, use_global_device_ids=true | all-gather | bytes 786432 | tf_op jit(solution)/shard_map/all_gather | solution.py:245
  142.1 18.0 %shard_map.158 = bf16[4,512,256]{2,1,0:T(8,128)(2,1)} custom-call(bf16[512,256]{1,0:T(8,128)(2,1)} %get-tuple-element.410.x_ref), custom_call_target="tpu_custom_call" | custom-call | tf_op jit(solution)/shard_map/pallas_call | solution.py:94
  160.1 21.5 %all-gather.6.cloned.1.call-done.x_ref = bf16[4096,256]{1,0:T(8,128)(2,1)} async-done(((bf16[512,256]{1,0:T(8,128)(2,1)}), bf16[4096,256]{1,0:T(8,128)(2,1)}) %all-gather.6.cloned.1.call-update) | async-done | bytes 2097168 | tf_op jit(solution)/shard_map/all_gather | solution.py:246
  185.0 1.2 scatter_custom_fusion
  213.2 1.2 slice_compare_fusion
  217.8 112.7 %shard_map.159 = bf16[4,4096,256]{2,1,0:T(8,128)(2,1)} custom-call(bf16[4096,256]{1,0:T(8,128)(2,1)} %all-gather.6.cloned.1.call-done.x_ref), custom_call_target="tpu_custom_call" | custom-call | tf_op jit(solution)/shard_map/pallas_call | solution.py:94
  344.5 4.0 %fusion.21 = f32[256,2048]{1,0:T(8,128)S(1)} fusion(bf16[2048,1664]{1,0:T(8,128)(2,1)} %all-gather.4.cloned.1.call-done, f32[256,512]{1,0:T(8,128)S(1)} %copy.108, bf16[256,2048]{0,1:T(8,128)(2,1)} %bitcast.123, bf16[2048,512]{1,0:T(8,128)(2,1)} %bitcast.118), kind=kOutput, calls=%fused_computation.35 | convolution fusion | flops 1074397184 | bytes 7864320 | tf_op jit(solution)/shard_map/dot_general | solution.py:389
  351.6 1.2 fusion.55
  352.8 1.1 constant_dynamic-slice_fusion.2
  354.1 1.6 collective-permute-start.5
  356.8 1.5 fusion.48
  358.3 4.7 %collective-permute-done.5 = bf16[256,512]{1,0:T(8,128)(2,1)S(1)} collective-permute-done((bf16[256,512]{1,0:T(8,128)(2,1)S(1)}, bf16[256,512]{1,0:T(8,128)(2,1)S(1)}, u32[]{:S(2)}, u32[]{:S(2)}) %collective-permute-start.5) | collective-permute-done | bytes 262176 | tf_op jit(solution)/shard_map/ppermute | solution.py:409
  (126 shorter events, 39.7 us)
Async XLA Ops:
  7.2 103.1 %copy-start = (bf16[256,512]{1,0:T(8,128)(2,1)S(1)}, bf16[256,512]{1,0:T(8,128)(2,1)}, u32[]{:S(2)}) copy-start(bf16[256,512]{1,0:T(8,128)(2,1)} %param.16) | copy-start | bytes 786436
  7.2 103.3 %copy-start.1 = (s32[256]{0:T(256)S(1)}, s32[256]{0:T(256)}, u32[]{:S(2)}) copy-start(s32[256]{0:T(256)} %param.26) | copy-start | bytes 3076
  7.2 110.4 %all-gather.4.cloned.1.call-start = ((), (), s32[]{:S(2)}) async-start(), calls=%async_computation | async-start | bytes 7667712 | tf_op jit(solution)/shard_map/all_gather | solution.py:182
  33.2 148.4 %all-gather.6.cloned.1.call-start = ((), (), s32[]{:S(2)}) async-start(), calls=%async_computation.1 | async-start | bytes 2359296 | tf_op jit(solution)/shard_map/all_gather | solution.py:246
  34.3 43.0 %collective-permute-start = (f32[256]{0:T(256)S(1)}, f32[256]{0:T(256)S(1)}, u32[]{:S(2)}, u32[]{:S(2)}) collective-permute-start(f32[256]{0:T(256)S(1)} %fusion.41), channel_id=1, source_target_pairs={{0,1},{1,0},{2,3},{3,2},{4,5},{5,4},{6,7},{7,6},{8,9},{9,8},{10,11... | collective-permute-start | bytes 3080 | tf_op jit(solution)/shard_map/ppermute | solution.py:195
  77.4 32.9 %collective-permute-start.1 = (f32[256]{0:T(256)S(1)}, f32[256]{0:T(256)S(1)}, u32[]{:S(2)}, u32[]{:S(2)}) collective-permute-start(f32[256]{0:T(256)S(1)} %add.741), channel_id=1, source_target_pairs={{0,2},{1,3},{2,0},{3,1},{4,6},{5,7},{6,4},{7,5},{8,10},{9,11},{10,... | collective-permute-start | bytes 3080 | tf_op jit(solution)/shard_map/ppermute | solution.py:198
  110.4 1.6 collective-permute-start.2
  112.2 14.1 %collective-permute-start.3 = (bf16[256,1024]{1,0:T(8,128)(2,1)S(1)}, bf16[256,1024]{1,0:T(8,128)(2,1)S(1)}, u32[]{:S(2)}, u32[]{:S(2)}) collective-permute-start(bf16[256,1024]{1,0:T(8,128)(2,1)S(1)} %maximum_select_fusion.3), channel_id=1, source_target_pairs={{0,2},{1,3},{2,0},{3,1},{4,6},{5,7},{6,4},{7,5},{8,10},{9,11},{10,... | collective-permute-start | bytes 1572872 | tf_op jit(solution)/shard_map/ppermute | solution.py:141
  114.0 16.2 %copy-start.3 = (f32[128]{0:T(128)S(1)}, f32[128]{0:T(128)}, u32[]{:S(2)}) copy-start(f32[128]{0:T(128)} %param.23) | copy-start | bytes 1540
  142.0 193.4 %all-gather.8.cloned.1.call-start = ((), (), s32[]{:S(2)}) async-start(), calls=%async_computation.2 | async-start | bytes 9437184 | tf_op jit(solution)/shard_map/all_gather | solution.py:249
  211.4 4.1 %copy-start.2 = (f32[128]{0:T(128)S(1)}, f32[128]{0:T(128)}, u32[]{:S(2)}) copy-start(f32[128]{0:T(128)} %param.22) | copy-start | bytes 1540
  348.8 5.1 %collective-permute-start.4 = (f32[256,1024]{1,0:T(8,128)S(1)}, f32[256,1024]{1,0:T(8,128)S(1)}, u32[]{:S(2)}, u32[]{:S(2)}) collective-permute-start(f32[256,1024]{1,0:T(8,128)S(1)} %pad_maximum_fusion), channel_id=1, source_target_pairs={{0,1},{1,0},{2,3},{3,2},{4,5},{5,4},{6,7},{7,6},{8,9},{9,8},{10,11... | collective-permute-start | bytes 3145736 | tf_op jit(solution)/shard_map/ppermute | solution.py:406
  354.1 8.8 %collective-permute-start.5 = (bf16[256,512]{1,0:T(8,128)(2,1)S(1)}, bf16[256,512]{1,0:T(8,128)(2,1)S(1)}, u32[]{:S(2)}, u32[]{:S(2)}) collective-permute-start(bf16[256,512]{1,0:T(8,128)(2,1)S(1)} %dynamic-slice_convert_fusion), channel_id=1, source_target_pairs={{0,2},{1,3},{2,0},{3,1},{4,6},{5,7},{6,4},{7,5},{8,10},{9,11},{10,... | collective-permute-start | bytes 786440 | tf_op jit(solution)/shard_map/ppermute | solution.py:409
Sparse Core Ops, SparseCore 0:
  33.3 84.2 all-gather.3
  142.2 39.4 all-gather.5
  183.4 92.1 all-gather.7
